TPU v7x, 256 devices: a whole 4x4x8 slice. The times are simulated.
256 devices in a mesh: dp: 32 (over z, x_hi, core), space: 8 (over x_lo, y).
Axes of the slice: x: 4 (x_hi: 2, x_lo: 2; x = x_hi * 2 + x_lo), y: 4, z: 8, core: 2. Of those that a mesh axis runs over, the one named last changes fastest.
Arguments:
- volume: bfloat16 [256, 4, 32, 16, 128], P('dp', None, 'space'), may hold values from -8 to 8
- conv_kernel: bfloat16 [32, 108], replicated, may hold values from -0.625 to 0.625
- dense_weight: bfloat16 [512, 128], replicated, may hold values from -0.25 to 0.25
- cotangent: bfloat16 [256, 128], P(('dp', 'space')), may hold values from -6 to 6
Outputs:
- step_conv: float32 [32, 108], replicated
- step_dense: float32 [512, 128], P('space', 'dp')
All inputs are finite; a program needn't handle non-finite values. Where the computation divides by a largest or mean magnitude, that divisor is 1e-20 or more.
Results may differ from a plain program's by a relative error of at most 0.0099.
Values may be sent and summed in bfloat16 or wider, within the bound.
No kernel may reach another device: no remote copies, remote signals or barrier semaphores. Data moves between devices by JAX's collectives and lax.ppermute only.
A program may use at most 64 MiB of HBM per device.

v0:
```python
import jax
import jax.numpy as jnp
from jax import lax
from jax.sharding import PartitionSpec as P

PC = 2
NS_STEPS = 8


LEAK_SLOPE = 0.3
DAMPING = 0.1
KL_BOUND = 0.0001
LEARN_RATE = 0.01
HIGHEST = lax.Precision.HIGHEST
CONTRACT = (((1,), (1,)), ((), ()))
LEADING = (((0,), (0,)), ((), ()))


def spread_2(value, axis, source):
    kept = jnp.where(lax.axis_index(axis) == source, value, 0).astype(value.dtype)
    return lax.psum(kept, axis)


def extended(x, sides, width):
    for axis, dim in sides:
        peers, length = (lax.axis_size(axis), x.shape[dim])
        up = [(i, (i + 1) % peers) for i in range(peers - 1)]
        down = [(j, i) for i, j in up]
        last = lax.slice_in_dim(x, length - width, length, axis=dim)
        initial = lax.slice_in_dim(x, 0, width, axis=dim)
        before = lax.ppermute(last, axis, up)
        after = lax.ppermute(initial, axis, down)
        x = jnp.concatenate([before, x, after], axis=dim)
    return x


def patch_matrix(slab_rim):
    channels, planes_rim, height, length = slab_rim.shape
    planes = planes_rim - 2
    padded = jnp.pad(slab_rim, ((0, 0), (0, 0), (1, 1), (1, 1)))
    pieces = []
    for shift_x in range(3):
        for shift_y in range(3):
            for shift_z in range(3):
                pieces.append(
                    padded[
                        :,
                        shift_x : shift_x + planes,
                        shift_y : shift_y + height,
                        shift_z : shift_z + length,
                    ]
                )
    return jnp.stack(pieces, axis=1).reshape(channels * 27, planes * height * length)


def damped_inverse(factor):
    factor_order = factor.shape[0]
    identity = jnp.eye(factor_order, dtype=jnp.float32)
    damped = factor + DAMPING * jnp.trace(factor) / factor_order * identity
    row_bound = jnp.max(jnp.sum(jnp.abs(damped), axis=1))
    iterate = identity / row_bound
    for newton_step in range(NS_STEPS):
        product = jnp.dot(damped, iterate, precision=HIGHEST)
        iterate = jnp.dot(iterate, 2.0 * identity - product, precision=HIGHEST)
    return iterate


def owned_inverse(factor, owner_index):
    mine = lax.axis_index("dp") == owner_index
    local_inverse = lax.cond(mine, damped_inverse, jnp.zeros_like, factor)
    return spread_2(local_inverse, "dp", owner_index)


def pool_regions(active, planes, height, length):
    shaped = active.reshape(active.shape[0], planes, PC, height // PC, length)
    return jnp.mean(shaped, axis=(1, 3, 4)).reshape(-1)


def dense_moments_of(features, cotangent):
    dense_in = lax.dot_general(features, features, LEADING, preferred_element_type=jnp.float32)
    dense_out = lax.dot_general(cotangent, cotangent, LEADING, preferred_element_type=jnp.float32)
    dense_grad = lax.dot_general(features, cotangent, LEADING, preferred_element_type=jnp.float32)
    return (dense_in, dense_out, dense_grad)


def on_device(volume, conv_kernel, dense_weight, cotangent):
    spaces = lax.axis_size("space")
    groups = lax.axis_size("dp")
    samples, channels, planes, height, length = volume.shape
    filters = conv_kernel.shape[0]
    patch_rows = conv_kernel.shape[1]
    padded = extended(volume, (("space", 2),), 1)

    def forward_pass(moment_in, slab_rim):
        patches = patch_matrix(slab_rim)
        before = jnp.dot(conv_kernel, patches, preferred_element_type=jnp.float32)
        active = jnp.where(before > 0, before, LEAK_SLOPE * before)
        pooled = pool_regions(active, planes, height, length).astype(jnp.bfloat16)
        gram = lax.dot_general(patches, patches, CONTRACT, preferred_element_type=jnp.float32)
        return (moment_in + gram, pooled)

    moment_in, pooled_all = lax.scan(
        forward_pass, jnp.zeros((patch_rows, patch_rows), jnp.float32), padded
    )
    features = lax.all_to_all(pooled_all, "space", split_axis=0, concat_axis=1, tiled=True)
    feature_grad = lax.dot_general(
        cotangent, dense_weight, CONTRACT, preferred_element_type=jnp.float32
    ).astype(jnp.bfloat16)
    returned = lax.all_to_all(feature_grad, "space", split_axis=1, concat_axis=0, tiled=True)

    def backward_pass(totals, pair):
        slab_rim, region_grad = pair
        patches = patch_matrix(slab_rim)
        before = jnp.dot(conv_kernel, patches, preferred_element_type=jnp.float32)
        region_grid = region_grad.astype(jnp.float32).reshape(filters, 1, PC, 1, 1)
        spread = jnp.broadcast_to(region_grid, (filters, planes, PC, height // PC, length)).reshape(
            filters, -1
        )
        signal = (jnp.where(before > 0, 1.0, LEAK_SLOPE) * spread).astype(jnp.bfloat16)
        moment_out = totals[0] + lax.dot_general(
            signal, signal, CONTRACT, preferred_element_type=jnp.float32
        )
        gradient = totals[1] + lax.dot_general(
            signal, patches, CONTRACT, preferred_element_type=jnp.float32
        )
        return ((moment_out, gradient), None)

    start_totals = (
        jnp.zeros((filters, filters), jnp.float32),
        jnp.zeros((filters, patch_rows), jnp.float32),
    )
    (moment_out, conv_sum), unused = lax.scan(backward_pass, start_totals, (padded, returned))
    conv_in, conv_out, conv_grad = lax.psum((moment_in, moment_out, conv_sum), ("dp", "space"))
    total_samples = samples * groups
    cell_count = total_samples * planes * spaces * height * length
    conv_in = conv_in / cell_count
    conv_out = conv_out / cell_count
    conv_grad = conv_grad / cell_count
    all_features, all_cotangent = (
        lax.all_gather(features, ("dp", "space"), axis=0, tiled=True),
        lax.all_gather(cotangent, ("dp", "space"), axis=0, tiled=True),
    )
    dense_in, dense_out, dense_grad = dense_moments_of(all_features, all_cotangent)
    dense_in = dense_in / total_samples
    dense_out = dense_out / total_samples
    dense_grad = dense_grad / total_samples
    factors = (conv_in, conv_out, dense_in, dense_out)
    stride = groups // len(factors)
    inverses = []
    for place in range(4):
        inverses.append(owned_inverse(factors[place], place * stride))
    inv_conv_in, inv_conv_out, inv_dense_in, inv_dense_out = inverses
    delta_conv = jnp.dot(
        jnp.dot(inv_conv_out, conv_grad, precision=HIGHEST), inv_conv_in, precision=HIGHEST
    )
    conv_total = jnp.sum(delta_conv * conv_grad)
    delta_whole = jnp.dot(
        jnp.dot(inv_dense_in, dense_grad, precision=HIGHEST), inv_dense_out, precision=HIGHEST
    )
    dense_total = jnp.sum(delta_whole * dense_grad)
    share_rows = dense_grad.shape[0] // spaces
    share_cols = dense_grad.shape[1] // groups
    first_row = lax.axis_index("space") * share_rows
    first_col = lax.axis_index("dp") * share_cols
    delta_rows = lax.dynamic_slice_in_dim(delta_whole, first_row, share_rows, 0)
    delta_block = lax.dynamic_slice_in_dim(delta_rows, first_col, share_cols, 1)
    scaling = jnp.minimum(
        1.0, jnp.sqrt(KL_BOUND / (LEARN_RATE * LEARN_RATE * (conv_total + dense_total)))
    )
    return (scaling * delta_conv, scaling * delta_block)


def solution(mesh):
    placed = (P("dp", None, "space", None, None), P(), P(), P(("dp", "space"), None))
    return jax.shard_map(
        on_device, mesh=mesh, in_specs=placed, out_specs=(P(), P("space", "dp")), check_vma=False
    )
```

profile of v0, /device:TPU:1, one launch (start us, length us, event | category | flops | bytes accessed | tf_op | source)
XLA Modules:
  0.0 2039.6 jit_solution(5955070597931003601)
XLA Ops:
  7.2 1.0 fusion.162
  8.2 4.0 collective-permute-start
  12.2 1.3 collective-permute-start.1
  13.6 0.8 fusion.159
  15.0 5.9 all-to-all-start
  21.0 613.5 %all-gather.1 = bf16[256,1,128]{2,1,0:T(2,128)(2,1)S(1)} all-gather(bf16[1,1,128]{2,1,0:T(2,128)(2,1)} %bitcast.621), channel_id=1, replica_groups=mesh['dp'=32,'space'=8] {'dp','space'}, dimensions={0}, use_global_device_ids=true | all-gather | bytes 65792 | tf_op jit(solution)/shard_map/all_gather | solution.py:141
  635.9 190.2 %while.30 = (s32[]{:T(128)}, f32[32,32]{1,0:T(8,128)S(1)}, f32[32,108]{1,0:T(8,128)S(1)}, bf16[8,4,6,16,128]{4,3,2,1,0:T(8,128)(2,1)S(1)}, bf16[32,108]{1,0:T(8,...) while((s32[]{:T(128)}, f32[32,32]{1,0:T(8,128)S(1)}, ...), condition=%wide.region_1.2_spmd.clone, body=%wide.region_0.1_spmd.clone.sunk | while | flops 131081024 | bytes 15313904 | solution.py:132
  654.8 2.7 reshape.103
  657.8 0.9 fusion.398
  658.9 0.7 convolution_add_fusion.7
  678.6 2.7 reshape.103
  681.5 0.9 fusion.398
  682.7 0.7 convolution_add_fusion.7
  702.3 2.7 reshape.103
  705.3 0.9 fusion.398
  706.5 0.7 convolution_add_fusion.7
  726.1 2.7 reshape.103
  729.1 0.9 fusion.398
  730.3 0.7 convolution_add_fusion.7
  749.9 2.7 reshape.103
  752.9 0.9 fusion.398
  754.1 0.7 convolution_add_fusion.7
  773.7 2.7 reshape.103
  776.7 0.9 fusion.398
  777.8 0.7 convolution_add_fusion.7
  797.4 2.7 reshape.103
  800.4 0.9 fusion.398
  821.2 2.7 reshape.103
  824.2 0.9 fusion.398
  825.4 0.7 convolution_add_fusion.7
  826.1 185.2 %while.31 = (s32[]{:T(128)}, f32[108,108]{1,0:T(8,128)S(1)}, bf16[8,64]{1,0:T(8,128)(2,1)S(1)}, bf16[8,4,6,16,128]{4,3,2,1,0:T(8,128)(2,1)S(1)}, bf16[32,108]{1,...) while((s32[]{:T(128)}, f32[108,108]{1,0:T(8,128)S(1)}, bf16[8,64]{1,0:T(8,128)(2,1)S(1)}, ...), condition=%wide.region_12.13_spmd.clone, body=%wide.region_10.12_spmd.clone.sunk | while | flops 248798048 | bytes 15895667 | solution.py:102
  845.0 2.7 reshape.105
  868.2 2.7 reshape.105
  891.3 2.7 reshape.105
  914.5 2.7 reshape.105
  937.6 2.7 reshape.105
  960.8 2.7 reshape.105
  983.9 2.7 reshape.105
  1007.1 2.7 reshape.105
  1012.0 3.3 all-to-all-start.1
  1015.3 90.8 %all-reduce.2 = (f32[32,32]{1,0:T(8,128)S(1)}, f32[32,108]{1,0:T(8,128)S(1)}, f32[108,108]{1,0:T(8,128)S(1)}) all-reduce(f32[32,32]{1,0:T(8,128)S(1)} %get-tuple-element.174, f32[32,108]{1,0:T(8,128)S(1)} %get-tuple-element.175, f32[108,108]{1,0:T(8,128)S(1)} %get-tuple-element.176), channel_id=1, replica_groups=mesh['dp'=32,'space'=8] {'dp','space'}, use_global_device_ids=true, to_apply=%region_2.3 | all-reduce | flops 16144 | bytes 129152 | tf_op jit(solution)/shard_map/psum | solution.py:133
  1106.5 611.7 %all-gather = bf16[256,1,512]{2,1,0:T(2,128)(2,1)S(1)} all-gather(bf16[1,1,512]{2,1,0:T(2,128)(2,1)S(1)} %reshape.80), channel_id=1, replica_groups=mesh['dp'=32,'space'=8] {'dp','space'}, dimensions={0}, use_global_device_ids=true | all-gather | bytes 263168 | tf_op jit(solution)/shard_map/all_gather | solution.py:140
  1718.9 1.1 broadcast_select_fusion
  1720.0 145.2 %all-reduce.3 = (f32[32,32]{1,0:T(8,128)S(1)}, f32[108,108]{1,0:T(8,128)S(1)}) all-reduce(f32[32,32]{1,0:T(8,128)S(1)} %broadcast_select_fusion.3, f32[108,108]{1,0:T(8,128)S(1)} %broadcast_select_fusion.2), channel_id=1, replica_groups=mesh['dp'=32,'space'=8] {'dp'}, use_global_device_ids=true, to_apply=%region_8.9 | all-reduce | flops 12688 | bytes 101504 | tf_op jit(solution)/shard_map/psum | solution.py:21
  1865.4 0.8 multiply_reduce_fusion.1
  1866.4 159.4 %all-reduce.7.cloned.1.call-done = (f32[512,512]{1,0:T(8,128)}, f32[128,128]{1,0:T(8,128)}) async-done(((f32[512,512]{1,0:T(8,128)}, f32[128,128]{1,0:T(8,128)}), (f32[512,512]{1,0:T(8,128)}, f32[128,128]{1,0:T(8,128)})) %all-reduce.7.cloned.1.call-update) | async-done | bytes 1114128 | tf_op jit(solution)/shard_map/psum | solution.py:21
  2025.8 2.2 fusion.191
  2028.0 1.3 fusion.192
  (581 shorter events, 325.1 us)
Async XLA Ops:
  7.2 6.4 copy-start
  8.2 627.2 %collective-permute-start = (bf16[8,4,1,16,128]{4,3,2,1,0:T(8,128)(2,1)S(1)}, bf16[8,4,1,16,128]{4,3,2,1,0:T(8,128)(2,1)S(1)}, u32[]{:S(2)}, u32[]{:S(2)}) collective-permute-start(bf16[8,4,1,16,128]{4,3,2,1,0:T(8,128)(2,1)S(1)} %get-tuple-element.247), channel_id=1, source_target_pairs={{0,1},{1,2},{2,3},{3,4},{4,5},{5,6},{6,7},{8,9},{9,10},{10,11},{11... | collective-permute-start | bytes 393224 | tf_op jit(solution)/shard_map/ppermute | solution.py:31
  12.2 623.6 %collective-permute-start.1 = (bf16[8,4,1,16,128]{4,3,2,1,0:T(8,128)(2,1)S(1)}, bf16[8,4,1,16,128]{4,3,2,1,0:T(8,128)(2,1)S(1)}, u32[]{:S(2)}, u32[]{:S(2)}) collective-permute-start(bf16[8,4,1,16,128]{4,3,2,1,0:T(8,128)(2,1)S(1)} %get-tuple-element.246), channel_id=1, source_target_pairs={{1,0},{2,1},{3,2},{4,3},{5,4},{6,5},{7,6},{9,8},{10,9},{11,10},{12... | collective-permute-start | bytes 393224 | tf_op jit(solution)/shard_map/ppermute | solution.py:32
  15.0 620.4 %all-to-all-start = ((bf16[1,8,64]{2,0,1:T(2,128)(2,1)}), bf16[1,8,64]{2,0,1:T(2,128)(2,1)S(1)}, u32[]{:S(2)}, u32[]{:S(2)}) async-start(bf16[1,8,64]{2,0,1:T(2,128)(2,1)} %all_to_all.30), calls=%async_computation | async-start | bytes 8192 | tf_op jit(solution)/shard_map/all_to_all | solution.py:109
  634.7 1.1 copy-start.1
  634.7 1.2 copy-start.2
  1012.0 94.4 %all-to-all-start.1 = ((bf16[8,1,64]{2,1,0:T(2,128)(2,1)}), bf16[8,1,64]{2,1,0:T(2,128)(2,1)S(1)}, u32[]{:S(2)}, u32[]{:S(2)}) async-start(bf16[8,1,64]{2,1,0:T(2,128)(2,1)} %copy.166), calls=%async_computation.1 | async-start | bytes 8192 | tf_op jit(solution)/shard_map/all_to_all | solution.py:105
  1015.3 1010.5 %all-reduce.7.cloned.1.call-start = ((), (), s32[]{:S(2)}) async-start(), calls=%async_computation.2 | async-start | bytes 2228224 | tf_op jit(solution)/shard_map/psum | solution.py:21
Sparse Core Ops, SparseCore 0:
  1720.1 305.6 all-reduce.6
where the time goes:
time: 2050 us; the launch traced here: 2040 us
  blocking collectives  1460 us (71%)
  local copies, waits for them, and re-layouts  352 us (17%)
  waiting for transfers between devices  159 us (8%)
  matrix products  29.4 us (1%)
    all_gather x1, blocking collectives, on_device(): lax.all_gather(cotangent, ('dp', 'space'), axis=0, tiled=True)  614 us
    all_gather x1, blocking collectives, on_device(): lax.all_gather(features, ('dp', 'space'), axis=0, tiled=True)  612 us
    while x424, local copies, waits for them, and re-layouts  291 us
    psum x1, waiting for transfers between devices, spread_2(): return lax.psum(kept, axis)  159 us
    psum x1, blocking collectives, spread_2(): return lax.psum(kept, axis)  145 us
    psum x1, blocking collectives, on_device(): lax.psum((moment_in, moment_out, conv_sum), ('dp', 'space'))  90.8 us
    reshape x16, local copies, waits for them, and re-layouts, patch_matrix(): jnp.stack(pieces, axis=1).reshape(channels * 27, planes * height * length)  43.1 us
  transfers between devices with their start and end apart: 5, of which 1 were waited for; matrix products, arithmetic and copies ran while one was open for 0% of the time, Pallas kernels for 0%

commit v1 on v0

v1 whole, which is shorter than its diff:
```python
import functools

import jax
import jax.numpy as jnp
from jax import lax
from jax.experimental import pallas as pl
from jax.experimental.pallas import tpu as pltpu
from jax.sharding import PartitionSpec as P

PC = 2
NS_STEPS = 8

LEAK_SLOPE = 0.3
DAMPING = 0.1
KL_BOUND = 0.0001
LEARN_RATE = 0.01
HIGHEST = lax.Precision.HIGHEST
CONTRACT = (((1,), (1,)), ((), ()))
LEADING = (((0,), (0,)), ((), ()))
BOTH = ("dp", "space")
F32 = jnp.float32
BF16 = jnp.bfloat16


def exchange(x, axes):
    return lax.all_to_all(x, axes, split_axis=0, concat_axis=0, tiled=True)


def gather_from(x, axes, peers):
    return exchange(jnp.broadcast_to(x[None], (peers,) + x.shape), axes)


def conv_kernel_body(
    sizes, vol_ref, before_ref, after_ref, bands_ref, weight_ref, cot_ref,
    pool_ref, moments_ref, shifted, stacked, grads, acc, acc_out,
):
    channels, planes, height, length, filters, samples = sizes
    rim = planes + 2
    per_plane = channels * 9
    rows = rim * per_plane
    cells = height * length
    half = cells // PC
    top = planes * filters
    step = pl.program_id(0)

    @pl.when(step == 0)
    def _():
        shifted[...] = jnp.zeros_like(shifted)
        acc[...] = jnp.zeros_like(acc)
        acc_out[...] = jnp.zeros_like(acc_out)
        pool_ref[...] = jnp.zeros_like(pool_ref)
        grads[...] = lax.dot_general(
            weight_ref[...], cot_ref[...], CONTRACT, preferred_element_type=F32
        ).astype(BF16).astype(F32)

    lane = lax.broadcasted_iota(jnp.int32, (height, length), 1)
    for plane in range(rim):
        for channel in range(channels):
            if plane == 0:
                value = before_ref[0, channel, 0]
            elif plane == rim - 1:
                value = after_ref[0, channel, 0]
            else:
                value = vol_ref[0, channel, plane - 1]
            value = value.astype(F32)
            moved = (
                jnp.where(lane == 0, 0.0, pltpu.roll(value, 1, 1)),
                value,
                jnp.where(lane == length - 1, 0.0, pltpu.roll(value, length - 1, 1)),
            )
            for j in range(3):
                for k in range(3):
                    row = plane * per_plane + channel * 9 + j * 3 + k
                    shifted[pl.ds((2 - j) * rows + row, height, stride=rows), :] = moved[k]
    for y in range(height):
        stacked[top:, y * length:(y + 1) * length] = shifted[
            (y + 1) * rows:(y + 2) * rows, :
        ].astype(BF16)

    column = lax.broadcasted_iota(jnp.int32, (filters * PC, samples), 1)
    grad_all = jnp.sum(jnp.where(column == step, grads[...], 0.0), axis=1, keepdims=True)
    low_all = (LEAK_SLOPE * grad_all).astype(BF16).astype(F32)
    pooled = []
    for part in range(PC):
        lanes = slice(part * half, (part + 1) * half)
        pre = jnp.dot(bands_ref[...], stacked[top:, lanes], preferred_element_type=F32)
        active = jnp.where(pre > 0, pre, LEAK_SLOPE * pre)
        total = active[0:filters]
        for plane in range(1, planes):
            total = total + active[plane * filters:(plane + 1) * filters]
        pooled.append(jnp.sum(total, axis=1, keepdims=True))
        grad = jnp.concatenate([grad_all[part * filters:(part + 1) * filters]] * planes, axis=0)
        low = jnp.concatenate([low_all[part * filters:(part + 1) * filters]] * planes, axis=0)
        stacked[0:top, lanes] = jnp.where(pre > 0, grad, low).astype(BF16)
    pooled = jnp.concatenate(pooled, axis=0) * (1.0 / (planes * half))
    spot = lax.broadcasted_iota(jnp.int32, pool_ref.shape, 1)
    pool_ref[...] = jnp.where(spot == step, pooled, pool_ref[...])
    acc[:, :rows] += lax.dot_general(
        stacked[...], stacked[top:, :], CONTRACT, preferred_element_type=F32
    )
    acc_out[...] += lax.dot_general(
        stacked[0:top, :], stacked[0:top, :], CONTRACT, preferred_element_type=F32
    )

    @pl.when(step == pl.num_programs(0) - 1)
    def _():
        width = acc.shape[1]
        wide = 3 * per_plane
        moment_in = jnp.zeros((wide, 128), F32)
        gradient = jnp.zeros((filters, 128), F32)
        moment_out = jnp.zeros((filters, 128), F32)
        for plane in range(planes):
            start = plane * per_plane
            turn = (width - start) % width
            block = acc[top + start:top + start + wide, :]
            moment_in += (pltpu.roll(block, turn, 1) if turn else block)[:, :128]
            block = acc[plane * filters:(plane + 1) * filters, :]
            gradient += (pltpu.roll(block, turn, 1) if turn else block)[:, :128]
            block = acc_out[plane * filters:(plane + 1) * filters, :]
            turn = (top - plane * filters) % top
            moment_out += pltpu.roll(block, turn, 1) if turn else block
        moments_ref[...] = jnp.zeros_like(moments_ref)
        lane_in = lax.broadcasted_iota(jnp.int32, (wide, 128), 1)
        lane_out = lax.broadcasted_iota(jnp.int32, (filters, 128), 1)
        moments_ref[0:wide, :] = jnp.where(lane_in < wide, moment_in, 0.0)
        moments_ref[112:112 + filters, :] = jnp.where(lane_out < wide, gradient, 0.0)
        moments_ref[144:144 + filters, :] = jnp.where(lane_out < filters, moment_out, 0.0)


def conv_moments(volume, before, after, bands, weight, cot_group, filters, peers):
    samples, channels, planes, height, length = volume.shape
    per_plane = channels * 9
    rows = (planes + 2) * per_plane
    top = planes * filters
    sizes = (channels, planes, height, length, filters, samples)
    whole = lambda shape: pl.BlockSpec(shape, lambda b: (0,) * len(shape))
    return pl.pallas_call(
        functools.partial(conv_kernel_body, sizes),
        grid=(samples,),
        in_specs=[
            pl.BlockSpec((1, channels, planes, height, length), lambda b: (b, 0, 0, 0, 0)),
            pl.BlockSpec((1, channels, 1, height, length), lambda b: (b, 0, 0, 0, 0)),
            pl.BlockSpec((1, channels, 1, height, length), lambda b: (b, 0, 0, 0, 0)),
            whole(bands.shape),
            whole(weight.shape),
            whole(cot_group.shape),
        ],
        out_specs=[whole((filters * PC, 128)), whole((peers, 128))],
        out_shape=[
            jax.ShapeDtypeStruct((filters * PC, 128), F32),
            jax.ShapeDtypeStruct((peers, 128), F32),
        ],
        scratch_shapes=[
            pltpu.VMEM(((height + 2) * rows, length), F32),
            pltpu.VMEM((top + rows, height * length), BF16),
            pltpu.VMEM((filters * PC, samples), F32),
            pltpu.VMEM((top + rows, 256), F32),
            pltpu.VMEM((top, top), F32),
        ],
        compiler_params=pltpu.CompilerParams(vmem_limit_bytes=48 * 1024 * 1024),
    )(volume, before, after, bands, weight, cot_group)


def exact_dot(a, b):
    return jnp.dot(a, b, precision=HIGHEST, preferred_element_type=F32)


def unit(order):
    row = lax.broadcasted_iota(jnp.int32, (order, order), 0)
    column = lax.broadcasted_iota(jnp.int32, (order, order), 1)
    return row == column


def scalar_sum(x):
    return jnp.sum(jnp.sum(x, axis=0, keepdims=True), axis=1, keepdims=True)


def residual(factor, order):
    size = factor.shape[0]
    eye = unit(size)
    trace = scalar_sum(jnp.where(eye, factor, 0.0))
    damping = DAMPING * trace / order
    sums = jnp.sum(jnp.abs(factor), axis=0, keepdims=True) + damping
    bound = jnp.max(sums, axis=1, keepdims=True)
    inside = lax.broadcasted_iota(jnp.int32, (size, size), 0) < order
    start = jnp.where(jnp.logical_and(eye, inside), 1.0 - damping / bound, 0.0)
    return start - factor / bound, bound


def dense_kernel_body(slab_count, place_ref, feat_ref, cot_ref, delta_ref, total_ref, whole):
    groups, spaces, local, width = feat_ref.shape
    count = groups * local
    for slab in range(0, spaces, 2):
        pair = [
            feat_ref[:, slab + i].astype(F32).reshape(count, width) for i in range(2)
        ]
        whole[:, slab * width:(slab + 2) * width] = jnp.concatenate(pair, axis=1).astype(BF16)
    cot = cot_ref[...]
    feats = whole[...]
    scale = 1.0 / count
    gram = lax.dot_general(feats, feats, CONTRACT, preferred_element_type=F32) * scale
    dense_in = lax.dot_general(feats, feats, LEADING, preferred_element_type=F32) * scale
    dense_out = lax.dot_general(cot, cot, LEADING, preferred_element_type=F32) * scale
    order = spaces * width
    eye = unit(count)
    damping = DAMPING * scalar_sum(jnp.where(eye, gram, 0.0)) / order
    sums = jnp.sum(jnp.abs(dense_in), axis=0, keepdims=True) + damping
    bound = jnp.max(sums, axis=1, keepdims=True)
    left = jnp.where(eye, 1.0 - damping / bound, 0.0) - gram / bound
    right, bound_out = residual(dense_out, dense_out.shape[0])
    cot_wide = cot.astype(F32)
    held = cot_wide * (scale / bound / bound_out)
    for newton_step in range(NS_STEPS):
        held = held + exact_dot(left, held)
        held = held + exact_dot(held, right)
        if newton_step < NS_STEPS - 1:
            left = exact_dot(left, left)
            right = exact_dot(right, right)
    total_ref[...] = scalar_sum(held * exact_dot(gram, cot_wide))
    mine = feat_ref[:, place_ref[0]].astype(F32).reshape(count, width)
    delta_ref[...] = lax.dot_general(
        mine, held, LEADING, precision=HIGHEST, preferred_element_type=F32
    )


def dense_delta(place, feats, cot):
    groups, spaces, local, width = feats.shape
    count = groups * local
    outputs = cot.shape[1]
    vmem = pl.BlockSpec(memory_space=pltpu.VMEM)
    return pl.pallas_call(
        functools.partial(dense_kernel_body, spaces),
        in_specs=[pl.BlockSpec(memory_space=pltpu.SMEM), vmem, vmem],
        out_specs=[vmem, vmem],
        out_shape=[
            jax.ShapeDtypeStruct((width, outputs), F32),
            jax.ShapeDtypeStruct((1, 1), F32),
        ],
        scratch_shapes=[pltpu.VMEM((count, spaces * width), BF16)],
        compiler_params=pltpu.CompilerParams(vmem_limit_bytes=48 * 1024 * 1024),
    )(place, feats, cot)


def final_kernel_body(
    filters, patch_rows, cells, moments_ref, dense_ref, total_ref, order_ref,
    step_conv_ref, step_dense_ref,
):
    scale = 1.0 / cells
    pad = jnp.zeros((128 - 112, 128), F32)
    conv_in = jnp.concatenate([moments_ref[0:112, :], pad], axis=0) * scale
    conv_grad = moments_ref[112:112 + filters, :] * scale
    conv_out = moments_ref[144:144 + filters, 0:filters] * scale
    right, bound_in = residual(conv_in, patch_rows)
    left, bound_out = residual(conv_out, filters)
    held = conv_grad / bound_in / bound_out
    for newton_step in range(NS_STEPS):
        held = held + exact_dot(left, held)
        held = held + exact_dot(held, right)
        if newton_step < NS_STEPS - 1:
            left = exact_dot(left, left)
            right = exact_dot(right, right)
    total = scalar_sum(held * conv_grad) + total_ref[...]
    scaling = jnp.minimum(1.0, jnp.sqrt(KL_BOUND / (LEARN_RATE * LEARN_RATE * total)))
    moved = exact_dot(held, order_ref[...])
    step_conv_ref[...] = scaling * moved[:, 0:patch_rows]
    step_dense_ref[...] = scaling * dense_ref[...]


def final_steps(moments, dense_block, dense_total, order, filters, patch_rows, cells):
    vmem = pl.BlockSpec(memory_space=pltpu.VMEM)
    return pl.pallas_call(
        functools.partial(final_kernel_body, filters, patch_rows, cells),
        in_specs=[vmem] * 4,
        out_specs=[vmem] * 2,
        out_shape=[
            jax.ShapeDtypeStruct((filters, patch_rows), F32),
            jax.ShapeDtypeStruct(dense_block.shape, F32),
        ],
        compiler_params=pltpu.CompilerParams(vmem_limit_bytes=32 * 1024 * 1024),
    )(moments, dense_block, dense_total, order)


def column_order(channels):
    row = lax.broadcasted_iota(jnp.int32, (128, 128), 0)
    column = lax.broadcasted_iota(jnp.int32, (128, 128), 1)
    channel, rest = column // 27, column % 27
    source = (rest // 9) * (9 * channels) + channel * 9 + rest % 9
    return jnp.where(jnp.logical_and(row == source, column < 27 * channels), 1.0, 0.0)


def on_device(volume, conv_kernel, dense_weight, cotangent):
    spaces = lax.axis_size("space")
    groups = lax.axis_size("dp")
    peers = spaces * groups
    samples, channels, planes, height, length = volume.shape
    filters, patch_rows = conv_kernel.shape
    slab = filters * PC

    up = [(i, i + 1) for i in range(spaces - 1)]
    down = [(j, i) for i, j in up]
    before = lax.ppermute(volume[:, :, planes - 1:], "space", up)
    after = lax.ppermute(volume[:, :, :1], "space", down)
    cot_group = gather_from(cotangent[0], "space", spaces)
    cot_all = gather_from(cotangent, BOTH, peers).reshape(peers, -1)

    mixed = conv_kernel.reshape(filters, channels, 3, 9).transpose(0, 2, 1, 3)
    mixed = mixed.reshape(filters, patch_rows)
    spare = (planes + 2) * channels * 9 - patch_rows
    bands = jnp.concatenate(
        [
            jnp.pad(mixed, ((0, 0), (p * channels * 9, spare - p * channels * 9)))
            for p in range(planes)
        ],
        axis=0,
    )
    place = lax.axis_index("space")
    weight = lax.dynamic_slice_in_dim(dense_weight, place * slab, slab, 0)
    weight = weight.reshape(filters, PC, -1).transpose(1, 0, 2).reshape(slab, -1)

    pool, moments = conv_moments(
        volume, before, after, bands, weight, cot_group, filters, peers
    )
    pooled = pool[:, :samples].reshape(PC, filters, samples).transpose(2, 1, 0)
    pooled = pooled.reshape(samples, slab).astype(BF16)

    feats = gather_from(pooled, BOTH, peers).reshape(groups, spaces, samples, slab)
    partial = exchange(moments, BOTH)
    mine = jnp.sum(partial, axis=0)
    reduced = gather_from(mine, BOTH, peers)

    delta, dense_total = dense_delta(place.reshape(1), feats, cot_all)
    share = cotangent.shape[1] // groups
    dense_block = lax.dynamic_slice_in_dim(delta, lax.axis_index("dp") * share, share, 1)
    cells = samples * groups * planes * spaces * height * length
    return final_steps(
        reduced, dense_block, dense_total, column_order(channels), filters, patch_rows, cells
    )


def solution(mesh):
    placed = (P("dp", None, "space", None, None), P(), P(), P(BOTH, None))
    return jax.shard_map(
        on_device, mesh=mesh, in_specs=placed, out_specs=(P(), P("space", "dp")), check_vma=False
    )
```

time: 2050 us -> 115 us (0.06)
  blocking collectives: 1460 us -> 0 us
  local copies, waits for them, and re-layouts: 352 us -> 6.32 us
  waiting for transfers between devices: 159 us -> 32.6 us
  starting transfers between devices: 14.6 us -> 51.1 us
  matrix products: 29.4 us -> 0 us
  Pallas kernels: 0 us -> 23.1 us
    all_gather x2 -> x0, blocking collectives: 1230 us -> none  [the longest x1 614 us: on_device(): lax.all_gather(cotangent, ('dp', 'space'), axis=0, tiled=True)]
    while x424 -> x0, local copies, waits for them, and re-layouts: 291 us -> none
    psum x2 -> x0, blocking collectives: 236 us -> none  [the longest x1 145 us: spread_2(): return lax.psum(kept, axis)]
    psum x1 -> x0, waiting for transfers between devices: 159 us -> none  [spread_2(): return lax.psum(kept, axis)]
    reshape x16 -> x3, local copies, waits for them, and re-layouts: 43.1 us -> 0.13 us  [the longest x2 0.11 us: on_device(): mixed = mixed.reshape(filters, patch_rows)]
    all_to_all x2 -> x5, starting transfers between devices: 9.21 us -> 46.3 us  [exchange(): return lax.all_to_all(x, axes, split_axis=0, concat_axis=0, tiled=True)]
    all_to_all x2 -> x5, waiting for transfers between devices: 0.01 us -> 32.6 us  [exchange(): return lax.all_to_all(x, axes, split_axis=0, concat_axis=0, tiled=True)]
    dot_general x48 -> x0, matrix products: 29.4 us -> none  [the longest x8 7.05 us: backward_pass(): before = jnp.dot(conv_kernel, patches, preferred_element_type=jnp.float32)]
  transfers between devices with their start and end apart: 5 -> 7, of which waited for: 1 -> 4; matrix products, arithmetic and copies ran while one was open for 0% -> 4% of each run, Pallas kernels for 0% -> 16%
where the time goes in v1:
time: 115 us; the launch traced here: 114 us
  starting transfers between devices  51.1 us (44%)
  waiting for transfers between devices  32.6 us (28%)
  Pallas kernels  23.1 us (20%)
  local copies, waits for them, and re-layouts  6.32 us (5%)
    all_to_all x5, starting transfers between devices, exchange(): return lax.all_to_all(x, axes, split_axis=0, concat_axis=0, tiled=True)  46.3 us
    all_to_all x5, waiting for transfers between devices, exchange(): return lax.all_to_all(x, axes, split_axis=0, concat_axis=0, tiled=True)  32.6 us
    pallas_call x1, Pallas kernels, conv_moments(): pl.pallas_call(functools.partial(conv_kernel_body, sizes), grid=(samples,...  11 us
    pallas_call x1, Pallas kernels, dense_delta(): pl.pallas_call(functools.partial(dense_kernel_body, spaces), in_specs=[pl...  7.48 us
    pallas_call x1, Pallas kernels, final_steps(): pl.pallas_call(functools.partial(final_kernel_body, filters, patch_rows,...  4.66 us
    ppermute x1, starting transfers between devices, on_device(): before = lax.ppermute(volume[:, :, planes - 1:], 'space', up)  3.5 us
  transfers between devices with their start and end apart: 7, of which 4 were waited for; matrix products, arithmetic and copies ran while one was open for 4% of the time, Pallas kernels for 16%

profile of v1, /device:TPU:1, one launch (start us, length us, event | category | flops | bytes accessed | tf_op | source)
XLA Modules:
  0.0 114.5 jit_solution(18147137371019356460)
XLA Ops:
  0.6 0.0 copy-start
  0.6 0.0 copy-start.3
  0.7 0.7 copy-done.3
  1.3 0.6 broadcast_in_dim.14
  1.9 5.9 %all-to-all-start = ((bf16[8,1,128]{2,1,0:T(2,128)(2,1)}), bf16[8,1,128]{2,1,0:T(2,128)(2,1)S(1)}, u32[]{:S(2)}, u32[]{:S(2)}) async-start(bf16[8,1,128]{2,1,0:T(2,128)(2,1)} %broadcast_in_dim.14), calls=%async_computation | async-start | bytes 8192 | tf_op jit(solution)/shard_map/all_to_all | solution.py:26
  7.9 0.0 copy-start.2
  7.9 1.0 fusion.22
  8.9 0.0 copy-start.1
  8.9 3.5 %collective-permute-start = (bf16[8,4,1,16,128]{4,3,2,1,0:T(8,128)(2,1)S(1)}, bf16[8,4,1,16,128]{4,3,2,1,0:T(8,128)(2,1)S(1)}, u32[]{:S(2)}, u32[]{:S(2)}) collective-permute-start(bf16[8,4,1,16,128]{4,3,2,1,0:T(8,128)(2,1)S(1)} %get-tuple-element.19), channel_id=1, source_target_pairs={{0,1},{1,2},{2,3},{3,4},{4,5},{5,6},{6,7},{8,9},{9,10},{10,11},{11... | collective-permute-start | bytes 393224 | tf_op jit(solution)/shard_map/ppermute | solution.py:301
  12.4 1.3 %collective-permute-start.1 = (bf16[8,4,1,16,128]{4,3,2,1,0:T(8,128)(2,1)S(1)}, bf16[8,4,1,16,128]{4,3,2,1,0:T(8,128)(2,1)S(1)}, u32[]{:S(2)}, u32[]{:S(2)}) collective-permute-start(bf16[8,4,1,16,128]{4,3,2,1,0:T(8,128)(2,1)S(1)} %get-tuple-element.18), channel_id=1, source_target_pairs={{1,0},{2,1},{3,2},{4,3},{5,4},{6,5},{7,6},{9,8},{10,9},{11,10},{12... | collective-permute-start | bytes 393224 | tf_op jit(solution)/shard_map/ppermute | solution.py:302
  13.7 0.0 all-to-all-done
  13.7 0.7 broadcast_in_dim.34
  14.4 16.3 %all-to-all-start.4 = ((bf16[256,1,128]{2,1,0:T(2,128)(2,1)}), bf16[256,1,128]{2,1,0:T(2,128)(2,1)S(1)}, u32[]{:S(2)}, u32[]{:S(2)}) async-start(bf16[256,1,128]{2,1,0:T(2,128)(2,1)} %broadcast_in_dim.34), calls=%async_computation.4 | async-start | bytes 262144 | tf_op jit(solution)/shard_map/all_to_all | solution.py:26
  30.8 0.0 copy-done
  30.8 0.0 copy-done.2
  30.8 0.1 copy.29
  31.0 0.1 copy.31
  31.1 0.1 fusion.16.bands_ref
  31.2 0.0 collective-permute-done.before_ref
  31.2 0.0 collective-permute-done.1.after_ref
  31.2 0.0 copy-done.1
  31.2 11.0 %shard_map.62 = (f32[64,128]{1,0:T(8,128)S(1)}, f32[256,128]{1,0:T(8,128)}) custom-call(bf16[8,4,4,16,128]{4,3,2,1,0:T(8,128)(2,1)S(1)} %copy-done.1, bf16[8,4,1,16,128]{4,3,2,1,0:T(8,128)(2,1)S(1)} %collective-permute-done.before_ref, bf16[8,4,1,16,128]{4,3,2,1,0:T(8,128)(2,1)S(1)} %collective-permute-done.1.after_ref, ...), custom_call_target="tpu_custom_call" | custom-call | tf_op jit(solution)/shard_map/pallas_call | solution.py:137
  42.2 1.4 %all-to-all-done.4 = bf16[256,1,128]{2,1,0:T(2,128)(2,1)S(1)} async-done(((bf16[256,1,128]{2,1,0:T(2,128)(2,1)}), bf16[256,1,128]{2,1,0:T(2,128)(2,1)S(1)}, u32[]{:S(2)}, u32[]{:S(2)}) %all-to-all-start.4) | async-done | bytes 65568 | tf_op jit(solution)/shard_map/all_to_all | solution.py:26
  43.7 12.3 %all-to-all-start.1 = ((f32[256,1,128]{2,1,0:T(1,128)}), f32[256,1,128]{2,1,0:T(1,128)S(1)}, u32[]{:S(2)}, u32[]{:S(2)}) async-start(f32[256,1,128]{2,1,0:T(1,128)} %bitcast.6), calls=%async_computation.1 | async-start | bytes 262144 | tf_op jit(solution)/shard_map/all_to_all | solution.py:26
  56.0 0.1 copy.38
  56.1 0.1 broadcast_in_dim.16
  56.2 1.1 reshape.58
  57.2 11.6 %all-to-all-done.1 = f32[256,1,128]{2,1,0:T(1,128)S(1)} async-done(((f32[256,1,128]{2,1,0:T(1,128)}), f32[256,1,128]{2,1,0:T(1,128)S(1)}, u32[]{:S(2)}, u32[]{:S(2)}) %all-to-all-start.1) | async-done | bytes 131104 | tf_op jit(solution)/shard_map/all_to_all | solution.py:26
  68.9 5.6 %all-to-all-start.3 = ((bf16[256,2,256]{2,1,0:T(2,128)(2,1)}), bf16[256,2,256]{2,1,0:T(2,128)(2,1)S(1)}, u32[]{:S(2)}, u32[]{:S(2)}) async-start(bf16[256,2,256]{2,1,0:T(2,128)(2,1)} %reshape.58), calls=%async_computation.3 | async-start | bytes 524288 | tf_op jit(solution)/shard_map/all_to_all | solution.py:26
  74.5 0.3 reduce_sum.9
  74.8 14.4 %all-to-all-done.3 = bf16[256,2,256]{2,1,0:T(2,128)(2,1)S(1)} async-done(((bf16[256,2,256]{2,1,0:T(2,128)(2,1)}), bf16[256,2,256]{2,1,0:T(2,128)(2,1)S(1)}, u32[]{:S(2)}, u32[]{:S(2)}) %all-to-all-start.3) | async-done | bytes 262176 | tf_op jit(solution)/shard_map/all_to_all | solution.py:26
  89.2 0.7 broadcast_in_dim.15
  89.9 6.2 %all-to-all-start.2 = ((f32[256,1,128]{2,1,0:T(1,128)}), f32[256,1,128]{2,1,0:T(1,128)S(1)}, u32[]{:S(2)}, u32[]{:S(2)}) async-start(f32[256,1,128]{2,1,0:T(1,128)} %broadcast_in_dim.15), calls=%async_computation.2 | async-start | bytes 262144 | tf_op jit(solution)/shard_map/all_to_all | solution.py:26
  96.2 0.3 reshape.59
  96.5 7.5 %shard_map.63 = (f32[64,128]{1,0:T(8,128)S(1)}, f32[1,1]{1,0:T(1,128)}) custom-call(s32[1]{0:T(128)} %bitcast.8.place_ref, bf16[32,8,8,64]{3,2,1,0:T(8,128)(2,1)S(1)} %bitcast.26, bf16[256,128]{1,0:T(8,128)(2,1)S(1)} %bitcast.28), custom_call_target="tpu_custom_call" | custom-call | tf_op jit(solution)/shard_map/pallas_call | solution.py:231
  104.0 0.1 constant_dynamic-slice_fusion.dense_ref
  104.1 5.1 %all-to-all-done.2 = f32[256,1,128]{2,1,0:T(1,128)S(1)} async-done(((f32[256,1,128]{2,1,0:T(1,128)}), f32[256,1,128]{2,1,0:T(1,128)S(1)}, u32[]{:S(2)}, u32[]{:S(2)}) %all-to-all-start.2) | async-done | bytes 131104 | tf_op jit(solution)/shard_map/all_to_all | solution.py:26
  109.2 4.7 %shard_map.64 = (f32[32,108]{1,0:T(8,128)}, f32[64,4]{1,0:T(8,128)S(1)}) custom-call(f32[256,128]{1,0:T(8,128)S(1)} %bitcast.27, f32[64,4]{1,0:T(8,128)S(1)} %constant_dynamic-slice_fusion.dense_ref, f32[1,1]{1,0:T(1,128)} %get-tuple-element.9.total_ref, f32[128,128]{1,0:T(8,128)S(1)} %fusion.21.order_ref), custom_call_target="tpu_custom_call" | custom-call | tf_op jit(solution)/shard_map/pallas_call | solution.py:271
  113.8 0.7 copy.39
  (14 shorter events, 0.2 us)
Async XLA Ops:
  0.6 30.1 %copy-start = (bf16[512,128]{1,0:T(8,128)(2,1)S(1)}, bf16[512,128]{1,0:T(8,128)(2,1)}, u32[]{:S(2)}) copy-start(bf16[512,128]{1,0:T(8,128)(2,1)} %param.6) | copy-start | bytes 393220
  0.6 0.7 copy-start.3
  1.9 11.8 %all-to-all-start = ((bf16[8,1,128]{2,1,0:T(2,128)(2,1)}), bf16[8,1,128]{2,1,0:T(2,128)(2,1)S(1)}, u32[]{:S(2)}, u32[]{:S(2)}) async-start(bf16[8,1,128]{2,1,0:T(2,128)(2,1)} %broadcast_in_dim.14), calls=%async_computation | async-start | bytes 8192 | tf_op jit(solution)/shard_map/all_to_all | solution.py:26
  7.9 22.9 %copy-start.2 = (bf16[32,108]{1,0:T(8,128)(2,1)S(1)}, bf16[32,108]{1,0:T(8,128)(2,1)}, u32[]{:S(2)}) copy-start(bf16[32,108]{1,0:T(8,128)(2,1)} %param.5) | copy-start | bytes 20740
  8.9 22.4 %copy-start.1 = (bf16[8,4,4,16,128]{4,3,2,1,0:T(8,128)(2,1)S(1)}, bf16[8,4,4,16,128]{4,3,2,1,0:T(8,128)(2,1)}, u32[]{:S(2)}) copy-start(bf16[8,4,4,16,128]{4,3,2,1,0:T(8,128)(2,1)} %vol_ref.1) | copy-start | bytes 1572868
  8.9 22.3 %collective-permute-start = (bf16[8,4,1,16,128]{4,3,2,1,0:T(8,128)(2,1)S(1)}, bf16[8,4,1,16,128]{4,3,2,1,0:T(8,128)(2,1)S(1)}, u32[]{:S(2)}, u32[]{:S(2)}) collective-permute-start(bf16[8,4,1,16,128]{4,3,2,1,0:T(8,128)(2,1)S(1)} %get-tuple-element.19), channel_id=1, source_target_pairs={{0,1},{1,2},{2,3},{3,4},{4,5},{5,6},{6,7},{8,9},{9,10},{10,11},{11... | collective-permute-start | bytes 393224 | tf_op jit(solution)/shard_map/ppermute | solution.py:301
  12.4 18.8 %collective-permute-start.1 = (bf16[8,4,1,16,128]{4,3,2,1,0:T(8,128)(2,1)S(1)}, bf16[8,4,1,16,128]{4,3,2,1,0:T(8,128)(2,1)S(1)}, u32[]{:S(2)}, u32[]{:S(2)}) collective-permute-start(bf16[8,4,1,16,128]{4,3,2,1,0:T(8,128)(2,1)S(1)} %get-tuple-element.18), channel_id=1, source_target_pairs={{1,0},{2,1},{3,2},{4,3},{5,4},{6,5},{7,6},{9,8},{10,9},{11,10},{12... | collective-permute-start | bytes 393224 | tf_op jit(solution)/shard_map/ppermute | solution.py:302
  14.4 29.2 %all-to-all-start.4 = ((bf16[256,1,128]{2,1,0:T(2,128)(2,1)}), bf16[256,1,128]{2,1,0:T(2,128)(2,1)S(1)}, u32[]{:S(2)}, u32[]{:S(2)}) async-start(bf16[256,1,128]{2,1,0:T(2,128)(2,1)} %broadcast_in_dim.34), calls=%async_computation.4 | async-start | bytes 262144 | tf_op jit(solution)/shard_map/all_to_all | solution.py:26
  43.7 25.2 %all-to-all-start.1 = ((f32[256,1,128]{2,1,0:T(1,128)}), f32[256,1,128]{2,1,0:T(1,128)S(1)}, u32[]{:S(2)}, u32[]{:S(2)}) async-start(f32[256,1,128]{2,1,0:T(1,128)} %bitcast.6), calls=%async_computation.1 | async-start | bytes 262144 | tf_op jit(solution)/shard_map/all_to_all | solution.py:26
  68.9 20.4 %all-to-all-start.3 = ((bf16[256,2,256]{2,1,0:T(2,128)(2,1)}), bf16[256,2,256]{2,1,0:T(2,128)(2,1)S(1)}, u32[]{:S(2)}, u32[]{:S(2)}) async-start(bf16[256,2,256]{2,1,0:T(2,128)(2,1)} %reshape.58), calls=%async_computation.3 | async-start | bytes 524288 | tf_op jit(solution)/shard_map/all_to_all | solution.py:26
  89.9 19.2 %all-to-all-start.2 = ((f32[256,1,128]{2,1,0:T(1,128)}), f32[256,1,128]{2,1,0:T(1,128)S(1)}, u32[]{:S(2)}, u32[]{:S(2)}) async-start(f32[256,1,128]{2,1,0:T(1,128)} %broadcast_in_dim.15), calls=%async_computation.2 | async-start | bytes 262144 | tf_op jit(solution)/shard_map/all_to_all | solution.py:26

commit v2 on v1

--- a/solution.py
+++ b/solution.py
@@ -20,6 +20,7 @@
 BOTH = ("dp", "space")
 F32 = jnp.float32
 BF16 = jnp.bfloat16
+ROWS_IN = 112
 
 
 def exchange(x, axes):
@@ -32,7 +33,7 @@
 
 def conv_kernel_body(
     sizes, vol_ref, before_ref, after_ref, bands_ref, weight_ref, cot_ref,
-    pool_ref, moments_ref, shifted, stacked, grads, acc, acc_out,
+    feats_ref, moments_ref, pool_ref, shifted, stacked, grads, acc, acc_out,
 ):
     channels, planes, height, length, filters, samples = sizes
     rim = planes + 2
@@ -95,7 +96,7 @@
     pooled = jnp.concatenate(pooled, axis=0) * (1.0 / (planes * half))
     spot = lax.broadcasted_iota(jnp.int32, pool_ref.shape, 1)
     pool_ref[...] = jnp.where(spot == step, pooled, pool_ref[...])
-    acc[:, :rows] += lax.dot_general(
+    acc[0:top + rows, :rows] += lax.dot_general(
         stacked[...], stacked[top:, :], CONTRACT, preferred_element_type=F32
     )
     acc_out[...] += lax.dot_general(
@@ -106,25 +107,38 @@
     def _():
         width = acc.shape[1]
         wide = 3 * per_plane
-        moment_in = jnp.zeros((wide, 128), F32)
+        moment_in = jnp.zeros((ROWS_IN, 128), F32)
         gradient = jnp.zeros((filters, 128), F32)
         moment_out = jnp.zeros((filters, 128), F32)
         for plane in range(planes):
             start = plane * per_plane
             turn = (width - start) % width
-            block = acc[top + start:top + start + wide, :]
+            block = acc[top + start:top + start + ROWS_IN, :]
             moment_in += (pltpu.roll(block, turn, 1) if turn else block)[:, :128]
             block = acc[plane * filters:(plane + 1) * filters, :]
             gradient += (pltpu.roll(block, turn, 1) if turn else block)[:, :128]
             block = acc_out[plane * filters:(plane + 1) * filters, :]
             turn = (top - plane * filters) % top
             moment_out += pltpu.roll(block, turn, 1) if turn else block
-        moments_ref[...] = jnp.zeros_like(moments_ref)
-        lane_in = lax.broadcasted_iota(jnp.int32, (wide, 128), 1)
+        row_in = lax.broadcasted_iota(jnp.int32, (ROWS_IN, 128), 0)
+        lane_in = lax.broadcasted_iota(jnp.int32, (ROWS_IN, 128), 1)
+        moment_in = jnp.where(jnp.maximum(row_in, lane_in) < wide, moment_in, 0.0)
         lane_out = lax.broadcasted_iota(jnp.int32, (filters, 128), 1)
-        moments_ref[0:wide, :] = jnp.where(lane_in < wide, moment_in, 0.0)
-        moments_ref[112:112 + filters, :] = jnp.where(lane_out < wide, gradient, 0.0)
-        moments_ref[144:144 + filters, :] = jnp.where(lane_out < filters, moment_out, 0.0)
+        gradient = jnp.where(lane_out < wide, gradient, 0.0)
+        packed = jnp.concatenate(
+            [
+                moment_in[:, :64],
+                moment_in[64:, 64:],
+                gradient[:, :64],
+                gradient[:, 64:],
+                moment_out[:, :64],
+            ],
+            axis=0,
+        )
+        high = packed.astype(BF16)
+        low = (packed - high.astype(F32)).astype(BF16)
+        moments_ref[...] = jnp.concatenate([high, low], axis=1)
+        feats_ref[...] = jnp.transpose(pool_ref[...])[:samples].astype(BF16)
 
 
 def conv_moments(volume, before, after, bands, weight, cot_group, filters, peers):
@@ -145,16 +159,17 @@
             whole(weight.shape),
             whole(cot_group.shape),
         ],
-        out_specs=[whole((filters * PC, 128)), whole((peers, 128))],
+        out_specs=[whole((samples, filters * PC)), whole((peers, 128))],
         out_shape=[
-            jax.ShapeDtypeStruct((filters * PC, 128), F32),
-            jax.ShapeDtypeStruct((peers, 128), F32),
+            jax.ShapeDtypeStruct((samples, filters * PC), BF16),
+            jax.ShapeDtypeStruct((peers, 128), BF16),
         ],
         scratch_shapes=[
+            pltpu.VMEM((filters * PC, 128), F32),
             pltpu.VMEM(((height + 2) * rows, length), F32),
             pltpu.VMEM((top + rows, height * length), BF16),
             pltpu.VMEM((filters * PC, samples), F32),
-            pltpu.VMEM((top + rows, 256), F32),
+            pltpu.VMEM((top + rows + 8, 256), F32),
             pltpu.VMEM((top, top), F32),
         ],
         compiler_params=pltpu.CompilerParams(vmem_limit_bytes=48 * 1024 * 1024),
@@ -218,6 +233,11 @@
             right = exact_dot(right, right)
     total_ref[...] = scalar_sum(held * exact_dot(gram, cot_wide))
     mine = feat_ref[:, place_ref[0]].astype(F32).reshape(count, width)
+    source = lax.broadcasted_iota(jnp.int32, (width, width), 0)
+    target = lax.broadcasted_iota(jnp.int32, (width, width), 1)
+    spot = (target % PC) * (width // PC) + target // PC
+    pick = jnp.where(source == spot, 1.0, 0.0).astype(BF16)
+    mine = jnp.dot(mine.astype(BF16), pick, preferred_element_type=F32)
     delta_ref[...] = lax.dot_general(
         mine, held, LEADING, precision=HIGHEST, preferred_element_type=F32
     )
@@ -246,10 +266,18 @@
     step_conv_ref, step_dense_ref,
 ):
     scale = 1.0 / cells
-    pad = jnp.zeros((128 - 112, 128), F32)
-    conv_in = jnp.concatenate([moments_ref[0:112, :], pad], axis=0) * scale
-    conv_grad = moments_ref[112:112 + filters, :] * scale
-    conv_out = moments_ref[144:144 + filters, 0:filters] * scale
+    pad = jnp.zeros((128 - ROWS_IN, 64), F32)
+    lower = jnp.concatenate([moments_ref[64:ROWS_IN, :], pad], axis=0)
+    corner = jnp.concatenate([moments_ref[ROWS_IN:2 * ROWS_IN - 64, :], pad], axis=0)
+    upper = jnp.concatenate([moments_ref[0:64, :], jnp.transpose(lower)], axis=1)
+    lower = jnp.concatenate([lower, corner], axis=1)
+    conv_in = jnp.concatenate([upper, lower], axis=0) * scale
+    first = 2 * ROWS_IN - 64
+    conv_grad = jnp.concatenate(
+        [moments_ref[first:first + filters, :], moments_ref[first + filters:first + 2 * filters, :]],
+        axis=1,
+    ) * scale
+    conv_out = moments_ref[first + 2 * filters:first + 3 * filters, 0:filters] * scale
     right, bound_in = residual(conv_in, patch_rows)
     left, bound_out = residual(conv_out, filters)
     held = conv_grad / bound_in / bound_out
@@ -301,7 +329,6 @@
     before = lax.ppermute(volume[:, :, planes - 1:], "space", up)
     after = lax.ppermute(volume[:, :, :1], "space", down)
     cot_group = gather_from(cotangent[0], "space", spaces)
-    cot_all = gather_from(cotangent, BOTH, peers).reshape(peers, -1)
 
     mixed = conv_kernel.reshape(filters, channels, 3, 9).transpose(0, 2, 1, 3)
     mixed = mixed.reshape(filters, patch_rows)
@@ -317,15 +344,16 @@
     weight = lax.dynamic_slice_in_dim(dense_weight, place * slab, slab, 0)
     weight = weight.reshape(filters, PC, -1).transpose(1, 0, 2).reshape(slab, -1)
 
-    pool, moments = conv_moments(
+    pooled, moments = conv_moments(
         volume, before, after, bands, weight, cot_group, filters, peers
     )
-    pooled = pool[:, :samples].reshape(PC, filters, samples).transpose(2, 1, 0)
-    pooled = pooled.reshape(samples, slab).astype(BF16)
-
-    feats = gather_from(pooled, BOTH, peers).reshape(groups, spaces, samples, slab)
-    partial = exchange(moments, BOTH)
-    mine = jnp.sum(partial, axis=0)
+    own = jnp.concatenate([pooled.reshape(1, samples * slab), cotangent], axis=1)
+    sent = jnp.concatenate([jnp.broadcast_to(own, (peers, own.shape[1])), moments], axis=1)
+    got = exchange(sent, BOTH)
+    feats = got[:, :samples * slab].reshape(groups, spaces, samples, slab)
+    cot_all = got[:, samples * slab:own.shape[1]]
+    parts = got[:, own.shape[1]:].astype(F32)
+    mine = jnp.sum(parts[:, :64] + parts[:, 64:], axis=0)
     reduced = gather_from(mine, BOTH, peers)
 
     delta, dense_total = dense_delta(place.reshape(1), feats, cot_all)

time: 115 us -> 89.2 us (0.78)
  starting transfers between devices: 51.1 us -> 31.8 us
  waiting for transfers between devices: 32.6 us -> 26.8 us
    all_to_all x5 -> x3, starting transfers between devices: 46.3 us -> 26.5 us  [exchange(): return lax.all_to_all(x, axes, split_axis=0, concat_axis=0, tiled=True)]
    all_to_all x5 -> x3, waiting for transfers between devices: 32.6 us -> 26.7 us  [exchange(): return lax.all_to_all(x, axes, split_axis=0, concat_axis=0, tiled=True)]
  transfers between devices with their start and end apart: 7 -> 5, of which waited for: 4 -> 3; matrix products, arithmetic and copies ran while one was open for 4% -> 2% of each run, Pallas kernels for 16% -> 8%
where the time goes in v2:
time: 89.2 us; the launch traced here: 88.9 us
  starting transfers between devices  31.8 us (36%)
  waiting for transfers between devices  26.8 us (30%)
  Pallas kernels  22.7 us (25%)
  local copies, waits for them, and re-layouts  5.49 us (6%)
  other arithmetic  1.28 us (1%)
    all_to_all x3, waiting for transfers between devices, exchange(): return lax.all_to_all(x, axes, split_axis=0, concat_axis=0, tiled=True)  26.7 us
    all_to_all x3, starting transfers between devices, exchange(): return lax.all_to_all(x, axes, split_axis=0, concat_axis=0, tiled=True)  26.5 us
    pallas_call x1, Pallas kernels, conv_moments(): pl.pallas_call(functools.partial(conv_kernel_body, sizes), grid=(samples,...  10.4 us
    pallas_call x1, Pallas kernels, dense_delta(): pl.pallas_call(functools.partial(dense_kernel_body, spaces), in_specs=[pl...  7.54 us
    pallas_call x1, Pallas kernels, final_steps(): pl.pallas_call(functools.partial(final_kernel_body, filters, patch_rows,...  4.79 us
    ppermute x1, starting transfers between devices, on_device(): before = lax.ppermute(volume[:, :, planes - 1:], 'space', up)  4.03 us
  transfers between devices with their start and end apart: 5, of which 3 were waited for; matrix products, arithmetic and copies ran while one was open for 2% of the time, Pallas kernels for 8%

profile of v2, /device:TPU:1, one launch (start us, length us, event | category | flops | bytes accessed | tf_op | source)
XLA Modules:
  0.0 88.9 jit_solution(8833109604418984476)
XLA Ops:
  0.6 0.0 copy-start
  0.6 0.0 copy-start.1
  0.7 0.0 copy-start.3
  0.7 1.1 %fusion.23 = (bf16[8,4,1,16,128]{4,3,2,1,0:T(8,128)(2,1)S(1)}, bf16[8,4,1,16,128]{4,3,2,1,0:T(8,128)(2,1)S(1)}) fusion(bf16[8,4,4,16,128]{4,3,2,1,0:T(8,128)(2,1)} %vol_ref.1), kind=kLoop, calls=%fused_computation.49 | loop fusion | bytes 524288 | tf_op jit(solution)/shard_map/slice | solution.py:330
  1.7 0.0 copy-start.2
  1.7 4.0 %collective-permute-start = (bf16[8,4,1,16,128]{4,3,2,1,0:T(8,128)(2,1)S(1)}, bf16[8,4,1,16,128]{4,3,2,1,0:T(8,128)(2,1)S(1)}, u32[]{:S(2)}, u32[]{:S(2)}) collective-permute-start(bf16[8,4,1,16,128]{4,3,2,1,0:T(8,128)(2,1)S(1)} %get-tuple-element.19), channel_id=1, source_target_pairs={{0,1},{1,2},{2,3},{3,4},{4,5},{5,6},{6,7},{8,9},{9,10},{10,11},{11... | collective-permute-start | bytes 393224 | tf_op jit(solution)/shard_map/ppermute | solution.py:329
  5.8 1.3 %collective-permute-start.1 = (bf16[8,4,1,16,128]{4,3,2,1,0:T(8,128)(2,1)S(1)}, bf16[8,4,1,16,128]{4,3,2,1,0:T(8,128)(2,1)S(1)}, u32[]{:S(2)}, u32[]{:S(2)}) collective-permute-start(bf16[8,4,1,16,128]{4,3,2,1,0:T(8,128)(2,1)S(1)} %get-tuple-element.18), channel_id=1, source_target_pairs={{1,0},{2,1},{3,2},{4,3},{5,4},{6,5},{7,6},{9,8},{10,9},{11,10},{12... | collective-permute-start | bytes 393224 | tf_op jit(solution)/shard_map/ppermute | solution.py:330
  7.1 0.0 copy-done.3
  7.1 0.6 broadcast_in_dim.26
  7.7 5.9 %all-to-all-start = ((bf16[8,1,128]{2,1,0:T(2,128)(2,1)}), bf16[8,1,128]{2,1,0:T(2,128)(2,1)S(1)}, u32[]{:S(2)}, u32[]{:S(2)}) async-start(bf16[8,1,128]{2,1,0:T(2,128)(2,1)} %broadcast_in_dim.26), calls=%async_computation | async-start | bytes 8192 | tf_op jit(solution)/shard_map/all_to_all | solution.py:27
  13.6 0.0 copy-done.2
  13.6 0.1 copy.24
  13.8 0.1 copy.26
  13.9 0.1 fusion.17.bands_ref
  14.0 0.0 copy-done
  14.0 4.5 %all-to-all-done = bf16[8,1,128]{2,1,0:T(2,128)(2,1)S(1)} async-done(((bf16[8,1,128]{2,1,0:T(2,128)(2,1)}), bf16[8,1,128]{2,1,0:T(2,128)(2,1)S(1)}, u32[]{:S(2)}, u32[]{:S(2)}) %all-to-all-start) | async-done | bytes 2080 | tf_op jit(solution)/shard_map/all_to_all | solution.py:27
  18.5 0.0 collective-permute-done.before_ref
  18.5 0.0 collective-permute-done.1.after_ref
  18.6 0.0 copy-done.1
  18.6 10.4 %shard_map.62 = (bf16[8,64]{1,0:T(8,128)(2,1)S(1)}, bf16[256,128]{1,0:T(8,128)(2,1)S(1)}) custom-call(bf16[8,4,4,16,128]{4,3,2,1,0:T(8,128)(2,1)S(1)} %copy-done.1, bf16[8,4,1,16,128]{4,3,2,1,0:T(8,128)(2,1)S(1)} %collective-permute-done.before_ref, bf16[8,4,1,16,128]{4,3,2,1,0:T(8,128)(2,1)S(1)} %collective-permute-done.1.after_ref, ...), custom_call_target="tpu_custom_call" | custom-call | tf_op jit(solution)/shard_map/pallas_call | solution.py:151
  29.0 0.1 reshape.43
  29.1 0.5 broadcast.61
  29.6 0.9 %reduce.2 = bf16[256,768]{1,0:T(8,128)(2,1)S(1)} reduce(bf16[256,1,768]{2,0,1:T(8,128)(2,1)S(1)} %maximum_bitcast_fusion, bf16[]{:T(256)} %broadcast.61), dimensions={1}, to_apply=%copy.31.reduce_sub_computation | reduce | bytes 786434 | tf_op jit(solution)/shard_map/all_to_all | solution.py:27
  30.5 0.8 reshape.48
  31.4 14.5 %all-to-all-start.1 = ((bf16[256,2,384]{2,1,0:T(2,128)(2,1)}), bf16[256,2,384]{2,1,0:T(2,128)(2,1)S(1)}, u32[]{:S(2)}, u32[]{:S(2)}) async-start(bf16[256,2,384]{2,1,0:T(2,128)(2,1)} %reshape.48), calls=%async_computation.1 | async-start | bytes 786432 | tf_op jit(solution)/shard_map/all_to_all | solution.py:27
  45.9 17.3 %all-to-all-done.1 = bf16[256,2,384]{2,1,0:T(2,128)(2,1)S(1)} async-done(((bf16[256,2,384]{2,1,0:T(2,128)(2,1)}), bf16[256,2,384]{2,1,0:T(2,128)(2,1)S(1)}, u32[]{:S(2)}, u32[]{:S(2)}) %all-to-all-start.1) | async-done | bytes 393248 | tf_op jit(solution)/shard_map/all_to_all | solution.py:27
  63.2 0.3 reshape.49
  63.6 0.1 fusion
  63.8 0.7 broadcast_in_dim.29
  64.5 6.1 %all-to-all-start.2 = ((f32[256,1,64]{2,1,0:T(1,128)}), f32[256,1,64]{2,1,0:T(1,128)S(1)}, u32[]{:S(2)}, u32[]{:S(2)}) async-start(f32[256,1,64]{2,1,0:T(1,128)} %broadcast_in_dim.29), calls=%async_computation.2 | async-start | bytes 262144 | tf_op jit(solution)/shard_map/all_to_all | solution.py:27
  70.6 0.3 reshape.45.feat_ref
  70.9 7.5 %shard_map.63 = (f32[64,128]{1,0:T(8,128)S(1)}, f32[1,1]{1,0:T(1,128)}) custom-call(s32[1]{0:T(128)} %bitcast.7.place_ref, bf16[32,8,8,64]{3,2,1,0:T(8,128)(2,1)S(1)} %reshape.45.feat_ref, bf16[256,128]{1,0:T(8,128)(2,1)S(1)} %get-tuple-element.20.cot_ref), custom_call_target="tpu_custom_call" | custom-call | tf_op jit(solution)/shard_map/pallas_call | solution.py:251
  78.4 0.1 constant_dynamic-slice_fusion.dense_ref
  78.5 4.9 %all-to-all-done.2 = f32[256,1,64]{2,1,0:T(1,128)S(1)} async-done(((f32[256,1,64]{2,1,0:T(1,128)}), f32[256,1,64]{2,1,0:T(1,128)S(1)}, u32[]{:S(2)}, u32[]{:S(2)}) %all-to-all-start.2) | async-done | bytes 65568 | tf_op jit(solution)/shard_map/all_to_all | solution.py:27
  83.4 4.8 %shard_map.64 = (f32[32,108]{1,0:T(8,128)}, f32[64,4]{1,0:T(8,128)S(1)}) custom-call(f32[256,64]{1,0:T(8,128)S(1)} %bitcast.20, f32[64,4]{1,0:T(8,128)S(1)} %constant_dynamic-slice_fusion.dense_ref, f32[1,1]{1,0:T(1,128)} %get-tuple-element.9.total_ref, f32[128,128]{1,0:T(8,128)S(1)} %fusion.22.order_ref), custom_call_target="tpu_custom_call" | custom-call | tf_op jit(solution)/shard_map/pallas_call | solution.py:299
  88.2 0.7 copy.32
  (17 shorter events, 0.3 us)
Async XLA Ops:
  0.6 13.3 %copy-start = (bf16[512,128]{1,0:T(8,128)(2,1)S(1)}, bf16[512,128]{1,0:T(8,128)(2,1)}, u32[]{:S(2)}) copy-start(bf16[512,128]{1,0:T(8,128)(2,1)} %param.6) | copy-start | bytes 393220
  0.6 17.9 %copy-start.1 = (bf16[8,4,4,16,128]{4,3,2,1,0:T(8,128)(2,1)S(1)}, bf16[8,4,4,16,128]{4,3,2,1,0:T(8,128)(2,1)}, u32[]{:S(2)}) copy-start(bf16[8,4,4,16,128]{4,3,2,1,0:T(8,128)(2,1)} %vol_ref.1) | copy-start | bytes 1572868
  0.7 6.4 %copy-start.3 = (bf16[1,128]{1,0:T(2,128)(2,1)S(1)}, bf16[1,128]{1,0:T(2,128)(2,1)}, u32[]{:S(2)}) copy-start(bf16[1,128]{1,0:T(2,128)(2,1)} %param.7) | copy-start | bytes 772
  1.7 11.9 %copy-start.2 = (bf16[32,108]{1,0:T(8,128)(2,1)S(1)}, bf16[32,108]{1,0:T(8,128)(2,1)}, u32[]{:S(2)}) copy-start(bf16[32,108]{1,0:T(8,128)(2,1)} %param.5) | copy-start | bytes 20740
  1.7 16.8 %collective-permute-start = (bf16[8,4,1,16,128]{4,3,2,1,0:T(8,128)(2,1)S(1)}, bf16[8,4,1,16,128]{4,3,2,1,0:T(8,128)(2,1)S(1)}, u32[]{:S(2)}, u32[]{:S(2)}) collective-permute-start(bf16[8,4,1,16,128]{4,3,2,1,0:T(8,128)(2,1)S(1)} %get-tuple-element.19), channel_id=1, source_target_pairs={{0,1},{1,2},{2,3},{3,4},{4,5},{5,6},{6,7},{8,9},{9,10},{10,11},{11... | collective-permute-start | bytes 393224 | tf_op jit(solution)/shard_map/ppermute | solution.py:329
  5.8 12.8 %collective-permute-start.1 = (bf16[8,4,1,16,128]{4,3,2,1,0:T(8,128)(2,1)S(1)}, bf16[8,4,1,16,128]{4,3,2,1,0:T(8,128)(2,1)S(1)}, u32[]{:S(2)}, u32[]{:S(2)}) collective-permute-start(bf16[8,4,1,16,128]{4,3,2,1,0:T(8,128)(2,1)S(1)} %get-tuple-element.18), channel_id=1, source_target_pairs={{1,0},{2,1},{3,2},{4,3},{5,4},{6,5},{7,6},{9,8},{10,9},{11,10},{12... | collective-permute-start | bytes 393224 | tf_op jit(solution)/shard_map/ppermute | solution.py:330
  7.7 10.9 %all-to-all-start = ((bf16[8,1,128]{2,1,0:T(2,128)(2,1)}), bf16[8,1,128]{2,1,0:T(2,128)(2,1)S(1)}, u32[]{:S(2)}, u32[]{:S(2)}) async-start(bf16[8,1,128]{2,1,0:T(2,128)(2,1)} %broadcast_in_dim.26), calls=%async_computation | async-start | bytes 8192 | tf_op jit(solution)/shard_map/all_to_all | solution.py:27
  31.4 31.9 %all-to-all-start.1 = ((bf16[256,2,384]{2,1,0:T(2,128)(2,1)}), bf16[256,2,384]{2,1,0:T(2,128)(2,1)S(1)}, u32[]{:S(2)}, u32[]{:S(2)}) async-start(bf16[256,2,384]{2,1,0:T(2,128)(2,1)} %reshape.48), calls=%async_computation.1 | async-start | bytes 786432 | tf_op jit(solution)/shard_map/all_to_all | solution.py:27
  64.5 19.0 %all-to-all-start.2 = ((f32[256,1,64]{2,1,0:T(1,128)}), f32[256,1,64]{2,1,0:T(1,128)S(1)}, u32[]{:S(2)}, u32[]{:S(2)}) async-start(f32[256,1,64]{2,1,0:T(1,128)} %broadcast_in_dim.29), calls=%async_computation.2 | async-start | bytes 262144 | tf_op jit(solution)/shard_map/all_to_all | solution.py:27

commit v3 on v2

--- a/solution.py
+++ b/solution.py
@@ -32,8 +32,8 @@
 
 
 def conv_kernel_body(
-    sizes, vol_ref, before_ref, after_ref, bands_ref, weight_ref, cot_ref,
-    feats_ref, moments_ref, pool_ref, shifted, stacked, grads, acc, acc_out,
+    sizes, vol_ref, before_ref, after_ref, bands_ref, weight_ref, cot_ref, own_ref,
+    sent_ref, pool_ref, shifted, stacked, grads, acc, acc_out,
 ):
     channels, planes, height, length, filters, samples = sizes
     rim = planes + 2
@@ -135,13 +135,27 @@
             ],
             axis=0,
         )
-        high = packed.astype(BF16)
-        low = (packed - high.astype(F32)).astype(BF16)
-        moments_ref[...] = jnp.concatenate([high, low], axis=1)
-        feats_ref[...] = jnp.transpose(pool_ref[...])[:samples].astype(BF16)
-
-
-def conv_moments(volume, before, after, bands, weight, cot_group, filters, peers):
+        groups = sent_ref.shape[0]
+        sent_ref[:, 0:8, :] = in_halves(packed).reshape(groups, 8, 128)
+        feats = jnp.transpose(pool_ref[...])[:samples]
+        own = own_ref[...].astype(F32)
+        own = jnp.concatenate([own[:, :64], own[:, 64:], jnp.zeros((samples - 2, 64), F32)], axis=0)
+        both = jnp.concatenate([feats, own], axis=1).astype(BF16)
+        sent_ref[:, 8:16, :] = jnp.broadcast_to(both[None], (groups, samples, 128))
+
+
+def in_halves(x):
+    high = x.astype(BF16)
+    low = (x - high.astype(F32)).astype(BF16)
+    return jnp.concatenate([high, low], axis=1)
+
+
+def from_halves(x):
+    wide = x.astype(F32)
+    return wide[..., :64] + wide[..., 64:]
+
+
+def conv_moments(volume, before, after, bands, weight, cot_group, own, filters, groups):
     samples, channels, planes, height, length = volume.shape
     per_plane = channels * 9
     rows = (planes + 2) * per_plane
@@ -158,12 +172,10 @@
             whole(bands.shape),
             whole(weight.shape),
             whole(cot_group.shape),
-        ],
-        out_specs=[whole((samples, filters * PC)), whole((peers, 128))],
-        out_shape=[
-            jax.ShapeDtypeStruct((samples, filters * PC), BF16),
-            jax.ShapeDtypeStruct((peers, 128), BF16),
-        ],
+            whole(own.shape),
+        ],
+        out_specs=whole((groups, 16, 128)),
+        out_shape=jax.ShapeDtypeStruct((groups, 16, 128), BF16),
         scratch_shapes=[
             pltpu.VMEM((filters * PC, 128), F32),
             pltpu.VMEM(((height + 2) * rows, length), F32),
@@ -173,7 +185,54 @@
             pltpu.VMEM((top, top), F32),
         ],
         compiler_params=pltpu.CompilerParams(vmem_limit_bytes=48 * 1024 * 1024),
-    )(volume, before, after, bands, weight, cot_group)
+    )(volume, before, after, bands, weight, cot_group, own)
+
+
+def middle_body(got_ref, sent_ref):
+    groups = got_ref.shape[0]
+    pairs = groups // 2
+    rows = pairs * 8
+    chunk = jnp.sum(from_halves(got_ref[:, 0:8, :]), axis=0)
+    wide = got_ref[:, 8:16, :].astype(F32)
+    feats = wide[:, :, :64]
+    feats = jnp.concatenate([feats[:pairs], feats[pairs:]], axis=2).reshape(rows, 128)
+    cots = jnp.concatenate([wide[:, 0, 64:], wide[:, 1, 64:]], axis=1)
+    feats = feats.astype(BF16)
+    cots = cots.astype(BF16)
+    chunk = in_halves(chunk)
+    for peer in range(sent_ref.shape[0]):
+        sent_ref[peer, 0:rows, :] = feats
+        sent_ref[peer, rows:rows + groups, :] = cots
+        sent_ref[peer, rows + groups:, :] = chunk
+
+
+def middle(got, spaces):
+    groups = got.shape[0]
+    vmem = pl.BlockSpec(memory_space=pltpu.VMEM)
+    return pl.pallas_call(
+        middle_body,
+        in_specs=[vmem],
+        out_specs=vmem,
+        out_shape=jax.ShapeDtypeStruct((spaces, groups * 5 + 8, 128), BF16),
+        compiler_params=pltpu.CompilerParams(vmem_limit_bytes=8 * 1024 * 1024),
+    )(got)
+
+
+def spread_body(got_ref, sent_ref):
+    chunk = jnp.sum(from_halves(got_ref[...]), axis=0)
+    sent_ref[...] = jnp.broadcast_to(in_halves(chunk)[None], sent_ref.shape)
+
+
+def spread(got, groups):
+    spaces, rows, lanes = got.shape
+    return pl.pallas_call(
+        spread_body,
+        grid=(1,),
+        in_specs=[pl.BlockSpec((spaces, 8, lanes), lambda i: (0, rows // 8 - 1, 0))],
+        out_specs=pl.BlockSpec((groups, 8, lanes), lambda i: (0, 0, 0)),
+        out_shape=jax.ShapeDtypeStruct((groups, 8, lanes), BF16),
+        compiler_params=pltpu.CompilerParams(vmem_limit_bytes=8 * 1024 * 1024),
+    )(got)
 
 
 def exact_dot(a, b):
@@ -202,15 +261,25 @@
     return start - factor / bound, bound
 
 
-def dense_kernel_body(slab_count, place_ref, feat_ref, cot_ref, delta_ref, total_ref, whole):
-    groups, spaces, local, width = feat_ref.shape
-    count = groups * local
+def dense_kernel_body(groups, place_ref, got_ref, delta_ref, total_ref, whole, cots):
+    spaces = got_ref.shape[0]
+    width = 64
+    count = groups * 8
+    half = count // 2
+
+    def slab_of(index):
+        both = got_ref[index].astype(F32)[:half]
+        return jnp.concatenate([both[:, :width], both[:, width:]], axis=0)
+
     for slab in range(0, spaces, 2):
-        pair = [
-            feat_ref[:, slab + i].astype(F32).reshape(count, width) for i in range(2)
-        ]
-        whole[:, slab * width:(slab + 2) * width] = jnp.concatenate(pair, axis=1).astype(BF16)
-    cot = cot_ref[...]
+        pair = jnp.concatenate([slab_of(slab), slab_of(slab + 1)], axis=1)
+        whole[:, slab * width:(slab + 2) * width] = pair.astype(BF16)
+    for slab in range(spaces):
+        cots[pl.ds(slab, groups, stride=spaces), :] = got_ref[
+            slab, half:half + groups, :
+        ].astype(F32)
+    cot_wide = cots[...]
+    cot = cot_wide.astype(BF16)
     feats = whole[...]
     scale = 1.0 / count
     gram = lax.dot_general(feats, feats, CONTRACT, preferred_element_type=F32) * scale
@@ -223,7 +292,6 @@
     bound = jnp.max(sums, axis=1, keepdims=True)
     left = jnp.where(eye, 1.0 - damping / bound, 0.0) - gram / bound
     right, bound_out = residual(dense_out, dense_out.shape[0])
-    cot_wide = cot.astype(F32)
     held = cot_wide * (scale / bound / bound_out)
     for newton_step in range(NS_STEPS):
         held = held + exact_dot(left, held)
@@ -232,61 +300,65 @@
             left = exact_dot(left, left)
             right = exact_dot(right, right)
     total_ref[...] = scalar_sum(held * exact_dot(gram, cot_wide))
-    mine = feat_ref[:, place_ref[0]].astype(F32).reshape(count, width)
+    mine = slab_of(place_ref[0])
     source = lax.broadcasted_iota(jnp.int32, (width, width), 0)
     target = lax.broadcasted_iota(jnp.int32, (width, width), 1)
     spot = (target % PC) * (width // PC) + target // PC
     pick = jnp.where(source == spot, 1.0, 0.0).astype(BF16)
     mine = jnp.dot(mine.astype(BF16), pick, preferred_element_type=F32)
     delta_ref[...] = lax.dot_general(
-        mine, held, LEADING, precision=HIGHEST, preferred_element_type=F32
-    )
-
-
-def dense_delta(place, feats, cot):
-    groups, spaces, local, width = feats.shape
-    count = groups * local
-    outputs = cot.shape[1]
+        held, mine, LEADING, precision=HIGHEST, preferred_element_type=F32
+    )
+
+
+def dense_delta(place, got, groups, outputs):
+    spaces = got.shape[0]
     vmem = pl.BlockSpec(memory_space=pltpu.VMEM)
     return pl.pallas_call(
-        functools.partial(dense_kernel_body, spaces),
-        in_specs=[pl.BlockSpec(memory_space=pltpu.SMEM), vmem, vmem],
+        functools.partial(dense_kernel_body, groups),
+        in_specs=[pl.BlockSpec(memory_space=pltpu.SMEM), vmem],
         out_specs=[vmem, vmem],
         out_shape=[
-            jax.ShapeDtypeStruct((width, outputs), F32),
+            jax.ShapeDtypeStruct((outputs, 64), F32),
             jax.ShapeDtypeStruct((1, 1), F32),
         ],
-        scratch_shapes=[pltpu.VMEM((count, spaces * width), BF16)],
+        scratch_shapes=[
+            pltpu.VMEM((groups * 8, spaces * 64), BF16),
+            pltpu.VMEM((groups * 8, outputs), F32),
+        ],
         compiler_params=pltpu.CompilerParams(vmem_limit_bytes=48 * 1024 * 1024),
-    )(place, feats, cot)
+    )(place, got)
 
 
 def final_kernel_body(
-    filters, patch_rows, cells, moments_ref, dense_ref, total_ref, order_ref,
+    filters, patch_rows, cells, got_ref, dense_ref, total_ref, order_ref,
     step_conv_ref, step_dense_ref,
 ):
     scale = 1.0 / cells
+    moments = from_halves(got_ref[...]).reshape(-1, 64)
     pad = jnp.zeros((128 - ROWS_IN, 64), F32)
-    lower = jnp.concatenate([moments_ref[64:ROWS_IN, :], pad], axis=0)
-    corner = jnp.concatenate([moments_ref[ROWS_IN:2 * ROWS_IN - 64, :], pad], axis=0)
-    upper = jnp.concatenate([moments_ref[0:64, :], jnp.transpose(lower)], axis=1)
+    lower = jnp.concatenate([moments[64:ROWS_IN], pad], axis=0)
+    corner = jnp.concatenate([moments[ROWS_IN:2 * ROWS_IN - 64], pad], axis=0)
+    upper = jnp.concatenate([moments[0:64], jnp.transpose(lower)], axis=1)
     lower = jnp.concatenate([lower, corner], axis=1)
     conv_in = jnp.concatenate([upper, lower], axis=0) * scale
     first = 2 * ROWS_IN - 64
     conv_grad = jnp.concatenate(
-        [moments_ref[first:first + filters, :], moments_ref[first + filters:first + 2 * filters, :]],
+        [moments[first:first + filters], moments[first + filters:first + 2 * filters]],
         axis=1,
     ) * scale
-    conv_out = moments_ref[first + 2 * filters:first + 3 * filters, 0:filters] * scale
+    conv_out = moments[first + 2 * filters:first + 3 * filters, 0:filters] * scale
     right, bound_in = residual(conv_in, patch_rows)
     left, bound_out = residual(conv_out, filters)
     held = conv_grad / bound_in / bound_out
+    inverse = jnp.where(unit(128), 1.0, 0.0) + right
     for newton_step in range(NS_STEPS):
         held = held + exact_dot(left, held)
-        held = held + exact_dot(held, right)
         if newton_step < NS_STEPS - 1:
             left = exact_dot(left, left)
             right = exact_dot(right, right)
+            inverse = inverse + exact_dot(inverse, right)
+    held = exact_dot(held, inverse)
     total = scalar_sum(held * conv_grad) + total_ref[...]
     scaling = jnp.minimum(1.0, jnp.sqrt(KL_BOUND / (LEARN_RATE * LEARN_RATE * total)))
     moved = exact_dot(held, order_ref[...])
@@ -319,7 +391,6 @@
 def on_device(volume, conv_kernel, dense_weight, cotangent):
     spaces = lax.axis_size("space")
     groups = lax.axis_size("dp")
-    peers = spaces * groups
     samples, channels, planes, height, length = volume.shape
     filters, patch_rows = conv_kernel.shape
     slab = filters * PC
@@ -344,25 +415,19 @@
     weight = lax.dynamic_slice_in_dim(dense_weight, place * slab, slab, 0)
     weight = weight.reshape(filters, PC, -1).transpose(1, 0, 2).reshape(slab, -1)
 
-    pooled, moments = conv_moments(
-        volume, before, after, bands, weight, cot_group, filters, peers
-    )
-    own = jnp.concatenate([pooled.reshape(1, samples * slab), cotangent], axis=1)
-    sent = jnp.concatenate([jnp.broadcast_to(own, (peers, own.shape[1])), moments], axis=1)
-    got = exchange(sent, BOTH)
-    feats = got[:, :samples * slab].reshape(groups, spaces, samples, slab)
-    cot_all = got[:, samples * slab:own.shape[1]]
-    parts = got[:, own.shape[1]:].astype(F32)
-    mine = jnp.sum(parts[:, :64] + parts[:, 64:], axis=0)
-    reduced = gather_from(mine, BOTH, peers)
-
-    delta, dense_total = dense_delta(place.reshape(1), feats, cot_all)
+    sent = conv_moments(
+        volume, before, after, bands, weight, cot_group, cotangent, filters, groups
+    )
+    got = exchange(middle(exchange(sent, "dp"), spaces), "space")
+    reduced = exchange(spread(got, groups), "dp")
+    delta, dense_total = dense_delta(place.reshape(1), got, groups, cotangent.shape[1])
     share = cotangent.shape[1] // groups
-    dense_block = lax.dynamic_slice_in_dim(delta, lax.axis_index("dp") * share, share, 1)
+    dense_block = lax.dynamic_slice_in_dim(delta, lax.axis_index("dp") * share, share, 0)
     cells = samples * groups * planes * spaces * height * length
-    return final_steps(
+    step_conv, step_dense = final_steps(
         reduced, dense_block, dense_total, column_order(channels), filters, patch_rows, cells
     )
+    return step_conv, step_dense.T
 
 
 def solution(mesh):

time: 89.2 us -> 85.8 us (0.962)
  local copies, waits for them, and re-layouts: 5.49 us -> 1.97 us
  waiting for transfers between devices: 26.8 us -> 24.6 us
  Pallas kernels: 22.7 us -> 24.7 us
  starting transfers between devices: 31.8 us -> 33.1 us
  other arithmetic: 1.28 us -> 0.17 us
    all_to_all x3 -> x4, waiting for transfers between devices: 26.7 us -> 24.6 us  [exchange(): return lax.all_to_all(x, axes, split_axis=0, concat_axis=0, tiled=True)]
    pallas_call x1 -> x3, Pallas kernels: 7.54 us -> 9.29 us  [the longest x1 7.57 us: dense_delta(): pl.pallas_call(functools.partial(dense_kernel_body, groups), in_specs=[pl...]
    all_to_all x3 -> x4, starting transfers between devices: 26.5 us -> 27.8 us  [exchange(): return lax.all_to_all(x, axes, split_axis=0, concat_axis=0, tiled=True)]
    unnamed x13 -> x10, local copies, waits for them, and re-layouts: 1.35 us -> 0.15 us
    all_to_all x2 -> x0, other arithmetic: 0.95 us -> none  [exchange(): return lax.all_to_all(x, axes, split_axis=0, concat_axis=0, tiled=True)]
  transfers between devices with their start and end apart: 5 -> 6, of which waited for: 3 -> 4; matrix products, arithmetic and copies ran while one was open for 2% -> 1% of each run, Pallas kernels for 8% -> 9%
where the time goes in v3:
time: 85.8 us; the launch traced here: 85.3 us
  starting transfers between devices  33.1 us (39%)
  Pallas kernels  24.7 us (29%)
  waiting for transfers between devices  24.6 us (29%)
  local copies, waits for them, and re-layouts  1.97 us (2%)
    all_to_all x4, starting transfers between devices, exchange(): return lax.all_to_all(x, axes, split_axis=0, concat_axis=0, tiled=True)  27.8 us
    all_to_all x4, waiting for transfers between devices, exchange(): return lax.all_to_all(x, axes, split_axis=0, concat_axis=0, tiled=True)  24.6 us
    pallas_call x1, Pallas kernels, conv_moments(): pl.pallas_call(functools.partial(conv_kernel_body, sizes), grid=(samples,...  11.1 us
    pallas_call x1, Pallas kernels, dense_delta(): pl.pallas_call(functools.partial(dense_kernel_body, groups), in_specs=[pl...  7.57 us
    pallas_call x1, Pallas kernels, final_steps(): pl.pallas_call(functools.partial(final_kernel_body, filters, patch_rows,...  4.26 us
    ppermute x1, starting transfers between devices, on_device(): before = lax.ppermute(volume[:, :, planes - 1:], 'space', up)  4.03 us
  transfers between devices with their start and end apart: 6, of which 4 were waited for; matrix products, arithmetic and copies ran while one was open for 1% of the time, Pallas kernels for 9%

profile of v3, /device:TPU:1, one launch (start us, length us, event | category | flops | bytes accessed | tf_op | source)
XLA Modules:
  0.0 85.3 jit_solution(10898367711570312524)
XLA Ops:
  0.6 0.0 copy-start
  0.6 0.0 copy-start.1
  0.7 1.1 %fusion.22 = (bf16[8,4,1,16,128]{4,3,2,1,0:T(8,128)(2,1)S(1)}, bf16[8,4,1,16,128]{4,3,2,1,0:T(8,128)(2,1)S(1)}) fusion(bf16[8,4,4,16,128]{4,3,2,1,0:T(8,128)(2,1)} %vol_ref.1), kind=kLoop, calls=%fused_computation.43 | loop fusion | bytes 524288 | tf_op jit(solution)/shard_map/slice | solution.py:401
  1.7 4.0 %collective-permute-start = (bf16[8,4,1,16,128]{4,3,2,1,0:T(8,128)(2,1)S(1)}, bf16[8,4,1,16,128]{4,3,2,1,0:T(8,128)(2,1)S(1)}, u32[]{:S(2)}, u32[]{:S(2)}) collective-permute-start(bf16[8,4,1,16,128]{4,3,2,1,0:T(8,128)(2,1)S(1)} %get-tuple-element.11), channel_id=1, source_target_pairs={{0,1},{1,2},{2,3},{3,4},{4,5},{5,6},{6,7},{8,9},{9,10},{10,11},{11... | collective-permute-start | bytes 393224 | tf_op jit(solution)/shard_map/ppermute | solution.py:400
  5.8 0.0 copy-start.2
  5.8 0.0 copy-start.3
  5.8 1.3 %collective-permute-start.1 = (bf16[8,4,1,16,128]{4,3,2,1,0:T(8,128)(2,1)S(1)}, bf16[8,4,1,16,128]{4,3,2,1,0:T(8,128)(2,1)S(1)}, u32[]{:S(2)}, u32[]{:S(2)}) collective-permute-start(bf16[8,4,1,16,128]{4,3,2,1,0:T(8,128)(2,1)S(1)} %get-tuple-element.10), channel_id=1, source_target_pairs={{1,0},{2,1},{3,2},{4,3},{5,4},{6,5},{7,6},{9,8},{10,9},{11,10},{12... | collective-permute-start | bytes 393224 | tf_op jit(solution)/shard_map/ppermute | solution.py:401
  7.1 0.0 copy-done.2
  7.1 0.6 broadcast_in_dim.13
  7.7 5.9 %all-to-all-start = ((bf16[8,1,128]{2,1,0:T(2,128)(2,1)}), bf16[8,1,128]{2,1,0:T(2,128)(2,1)S(1)}, u32[]{:S(2)}, u32[]{:S(2)}) async-start(bf16[8,1,128]{2,1,0:T(2,128)(2,1)} %broadcast_in_dim.13), calls=%async_computation | async-start | bytes 8192 | tf_op jit(solution)/shard_map/all_to_all | solution.py:27
  13.6 0.0 copy-done.3
  13.6 0.1 copy.21
  13.8 0.1 copy.23
  13.9 0.1 fusion.16.bands_ref
  14.0 0.0 copy-done
  14.0 4.5 %all-to-all-done = bf16[8,1,128]{2,1,0:T(2,128)(2,1)S(1)} async-done(((bf16[8,1,128]{2,1,0:T(2,128)(2,1)}), bf16[8,1,128]{2,1,0:T(2,128)(2,1)S(1)}, u32[]{:S(2)}, u32[]{:S(2)}) %all-to-all-start) | async-done | bytes 2080 | tf_op jit(solution)/shard_map/all_to_all | solution.py:27
  18.5 0.0 collective-permute-done.before_ref
  18.5 0.0 collective-permute-done.1.after_ref
  18.6 0.0 copy-done.1
  18.6 11.1 %shard_map.62 = bf16[32,16,128]{2,1,0:T(8,128)(2,1)} custom-call(bf16[8,4,4,16,128]{4,3,2,1,0:T(8,128)(2,1)S(1)} %copy-done.1, bf16[8,4,1,16,128]{4,3,2,1,0:T(8,128)(2,1)S(1)} %collective-permute-done.before_ref, bf16[8,4,1,16,128]{4,3,2,1,0:T(8,128)(2,1)S(1)} %collective-permute-done.1.after_ref, bf16[128,216]{1,0:T(8,128)(2,1)S(1)} %fusion.16.bands_ref, ...), custom_call_target="tpu_custom_call" | custom-call | tf_op jit(solution)/shard_map/pallas_call | solution.py:165
  29.7 13.5 %all-to-all-start.1 = ((bf16[32,16,128]{2,1,0:T(8,128)(2,1)}), bf16[32,16,128]{2,1,0:T(8,128)(2,1)S(1)}, u32[]{:S(2)}, u32[]{:S(2)}) async-start(bf16[32,16,128]{2,1,0:T(8,128)(2,1)} %shard_map.62), calls=%async_computation.1 | async-start | bytes 262144 | tf_op jit(solution)/shard_map/all_to_all | solution.py:27
  43.2 10.7 %all-to-all-done.1.got_ref = bf16[32,16,128]{2,1,0:T(8,128)(2,1)S(1)} async-done(((bf16[32,16,128]{2,1,0:T(8,128)(2,1)}), bf16[32,16,128]{2,1,0:T(8,128)(2,1)S(1)}, u32[]{:S(2)}, u32[]{:S(2)}) %all-to-all-start.1) | async-done | bytes 131104 | tf_op jit(solution)/shard_map/all_to_all | solution.py:27
  53.9 0.9 %shard_map.63 = bf16[8,168,128]{2,1,0:T(8,128)(2,1)} custom-call(bf16[32,16,128]{2,1,0:T(8,128)(2,1)S(1)} %all-to-all-done.1.got_ref), custom_call_target="tpu_custom_call" | custom-call | tf_op jit(solution)/shard_map/pallas_call | solution.py:212
  54.8 3.4 %all-to-all-start.2 = ((bf16[8,168,128]{2,1,0:T(8,128)(2,1)}), bf16[8,168,128]{2,1,0:T(8,128)(2,1)S(1)}, u32[]{:S(2)}, u32[]{:S(2)}) async-start(bf16[8,168,128]{2,1,0:T(8,128)(2,1)} %shard_map.63), calls=%async_computation.2 | async-start | bytes 688128 | tf_op jit(solution)/shard_map/all_to_all | solution.py:27
  58.3 7.1 %all-to-all-done.2.got_ref = bf16[8,168,128]{2,1,0:T(8,128)(2,1)S(1)} async-done(((bf16[8,168,128]{2,1,0:T(8,128)(2,1)}), bf16[8,168,128]{2,1,0:T(8,128)(2,1)S(1)}, u32[]{:S(2)}, u32[]{:S(2)}) %all-to-all-start.2) | async-done | bytes 344096 | tf_op jit(solution)/shard_map/all_to_all | solution.py:27
  65.3 0.8 shard_map.64
  66.1 5.0 %all-to-all-start.3 = ((bf16[32,8,128]{2,1,0:T(8,128)(2,1)}), bf16[32,8,128]{2,1,0:T(8,128)(2,1)S(1)}, u32[]{:S(2)}, u32[]{:S(2)}) async-start(bf16[32,8,128]{2,1,0:T(8,128)(2,1)} %shard_map.64), calls=%async_computation.3 | async-start | bytes 131072 | tf_op jit(solution)/shard_map/all_to_all | solution.py:27
  71.2 7.6 %shard_map.65 = (f32[128,64]{1,0:T(8,128)S(1)}, f32[1,1]{1,0:T(1,128)}) custom-call(s32[1]{0:T(128)} %bitcast.5.place_ref, bf16[8,168,128]{2,1,0:T(8,128)(2,1)S(1)} %all-to-all-done.2.got_ref), custom_call_target="tpu_custom_call" | custom-call | tf_op jit(solution)/shard_map/pallas_call | solution.py:317
  78.8 2.3 %all-to-all-done.3.got_ref = bf16[32,8,128]{2,1,0:T(8,128)(2,1)S(1)} async-done(((bf16[32,8,128]{2,1,0:T(8,128)(2,1)}), bf16[32,8,128]{2,1,0:T(8,128)(2,1)S(1)}, u32[]{:S(2)}, u32[]{:S(2)}) %all-to-all-start.3) | async-done | bytes 65568 | tf_op jit(solution)/shard_map/all_to_all | solution.py:27
  81.1 4.3 %shard_map.66 = (f32[32,108]{1,0:T(8,128)}, f32[4,64]{1,0:T(4,128)}) custom-call(bf16[32,8,128]{2,1,0:T(8,128)(2,1)S(1)} %all-to-all-done.3.got_ref, f32[4,64]{1,0:T(4,128)S(1)} %constant_dynamic-slice_fusion.dense_ref, f32[1,1]{1,0:T(1,128)} %get-tuple-element.7.total_ref, f32[128,128]{1,0:T(8,128)S(1)} %fusion.21.order_ref), custom_call_target="tpu_custom_call" | custom-call | tf_op jit(solution)/shard_map/pallas_call | solution.py:371
  (12 shorter events, 0.1 us)
Async XLA Ops:
  0.6 13.3 %copy-start = (bf16[512,128]{1,0:T(8,128)(2,1)S(1)}, bf16[512,128]{1,0:T(8,128)(2,1)}, u32[]{:S(2)}) copy-start(bf16[512,128]{1,0:T(8,128)(2,1)} %param.6) | copy-start | bytes 393220
  0.6 17.9 %copy-start.1 = (bf16[8,4,4,16,128]{4,3,2,1,0:T(8,128)(2,1)S(1)}, bf16[8,4,4,16,128]{4,3,2,1,0:T(8,128)(2,1)}, u32[]{:S(2)}) copy-start(bf16[8,4,4,16,128]{4,3,2,1,0:T(8,128)(2,1)} %vol_ref.1) | copy-start | bytes 1572868
  1.7 16.8 %collective-permute-start = (bf16[8,4,1,16,128]{4,3,2,1,0:T(8,128)(2,1)S(1)}, bf16[8,4,1,16,128]{4,3,2,1,0:T(8,128)(2,1)S(1)}, u32[]{:S(2)}, u32[]{:S(2)}) collective-permute-start(bf16[8,4,1,16,128]{4,3,2,1,0:T(8,128)(2,1)S(1)} %get-tuple-element.11), channel_id=1, source_target_pairs={{0,1},{1,2},{2,3},{3,4},{4,5},{5,6},{6,7},{8,9},{9,10},{10,11},{11... | collective-permute-start | bytes 393224 | tf_op jit(solution)/shard_map/ppermute | solution.py:400
  5.8 1.3 %copy-start.2 = (bf16[1,128]{1,0:T(2,128)(2,1)S(1)}, bf16[1,128]{1,0:T(2,128)(2,1)}, u32[]{:S(2)}) copy-start(bf16[1,128]{1,0:T(2,128)(2,1)} %own_ref.1) | copy-start | bytes 772
  5.8 7.8 %copy-start.3 = (bf16[32,108]{1,0:T(8,128)(2,1)S(1)}, bf16[32,108]{1,0:T(8,128)(2,1)}, u32[]{:S(2)}) copy-start(bf16[32,108]{1,0:T(8,128)(2,1)} %param.5) | copy-start | bytes 20740
  5.8 12.8 %collective-permute-start.1 = (bf16[8,4,1,16,128]{4,3,2,1,0:T(8,128)(2,1)S(1)}, bf16[8,4,1,16,128]{4,3,2,1,0:T(8,128)(2,1)S(1)}, u32[]{:S(2)}, u32[]{:S(2)}) collective-permute-start(bf16[8,4,1,16,128]{4,3,2,1,0:T(8,128)(2,1)S(1)} %get-tuple-element.10), channel_id=1, source_target_pairs={{1,0},{2,1},{3,2},{4,3},{5,4},{6,5},{7,6},{9,8},{10,9},{11,10},{12... | collective-permute-start | bytes 393224 | tf_op jit(solution)/shard_map/ppermute | solution.py:401
  7.7 10.9 %all-to-all-start = ((bf16[8,1,128]{2,1,0:T(2,128)(2,1)}), bf16[8,1,128]{2,1,0:T(2,128)(2,1)S(1)}, u32[]{:S(2)}, u32[]{:S(2)}) async-start(bf16[8,1,128]{2,1,0:T(2,128)(2,1)} %broadcast_in_dim.13), calls=%async_computation | async-start | bytes 8192 | tf_op jit(solution)/shard_map/all_to_all | solution.py:27
  29.7 24.2 %all-to-all-start.1 = ((bf16[32,16,128]{2,1,0:T(8,128)(2,1)}), bf16[32,16,128]{2,1,0:T(8,128)(2,1)S(1)}, u32[]{:S(2)}, u32[]{:S(2)}) async-start(bf16[32,16,128]{2,1,0:T(8,128)(2,1)} %shard_map.62), calls=%async_computation.1 | async-start | bytes 262144 | tf_op jit(solution)/shard_map/all_to_all | solution.py:27
  54.8 10.5 %all-to-all-start.2 = ((bf16[8,168,128]{2,1,0:T(8,128)(2,1)}), bf16[8,168,128]{2,1,0:T(8,128)(2,1)S(1)}, u32[]{:S(2)}, u32[]{:S(2)}) async-start(bf16[8,168,128]{2,1,0:T(8,128)(2,1)} %shard_map.63), calls=%async_computation.2 | async-start | bytes 688128 | tf_op jit(solution)/shard_map/all_to_all | solution.py:27
  66.1 14.9 %all-to-all-start.3 = ((bf16[32,8,128]{2,1,0:T(8,128)(2,1)}), bf16[32,8,128]{2,1,0:T(8,128)(2,1)S(1)}, u32[]{:S(2)}, u32[]{:S(2)}) async-start(bf16[32,8,128]{2,1,0:T(8,128)(2,1)} %shard_map.64), calls=%async_computation.3 | async-start | bytes 131072 | tf_op jit(solution)/shard_map/all_to_all | solution.py:27

commit v4 on v3

--- a/solution.py
+++ b/solution.py
@@ -17,7 +17,10 @@
 HIGHEST = lax.Precision.HIGHEST
 CONTRACT = (((1,), (1,)), ((), ()))
 LEADING = (((0,), (0,)), ((), ()))
-BOTH = ("dp", "space")
+DP = ("z", "xh", "core")
+SPACE = ("xl", "y")
+COLUMN = ("z", "core")
+PLANE = ("xh", "xl", "y")
 F32 = jnp.float32
 BF16 = jnp.bfloat16
 ROWS_IN = 112
@@ -136,12 +139,13 @@
             axis=0,
         )
         groups = sent_ref.shape[0]
-        sent_ref[:, 0:8, :] = in_halves(packed).reshape(groups, 8, 128)
+        share = packed.shape[0] // groups
+        sent_ref[:, 0:share, :] = in_halves(packed).reshape(groups, share, 128)
         feats = jnp.transpose(pool_ref[...])[:samples]
         own = own_ref[...].astype(F32)
         own = jnp.concatenate([own[:, :64], own[:, 64:], jnp.zeros((samples - 2, 64), F32)], axis=0)
         both = jnp.concatenate([feats, own], axis=1).astype(BF16)
-        sent_ref[:, 8:16, :] = jnp.broadcast_to(both[None], (groups, samples, 128))
+        sent_ref[:, share:, :] = jnp.broadcast_to(both[None], (groups, samples, 128))
 
 
 def in_halves(x):
@@ -174,8 +178,8 @@
             whole(cot_group.shape),
             whole(own.shape),
         ],
-        out_specs=whole((groups, 16, 128)),
-        out_shape=jax.ShapeDtypeStruct((groups, 16, 128), BF16),
+        out_specs=whole((groups, 256 // groups + samples, 128)),
+        out_shape=jax.ShapeDtypeStruct((groups, 256 // groups + samples, 128), BF16),
         scratch_shapes=[
             pltpu.VMEM((filters * PC, 128), F32),
             pltpu.VMEM(((height + 2) * rows, length), F32),
@@ -192,8 +196,9 @@
     groups = got_ref.shape[0]
     pairs = groups // 2
     rows = pairs * 8
-    chunk = jnp.sum(from_halves(got_ref[:, 0:8, :]), axis=0)
-    wide = got_ref[:, 8:16, :].astype(F32)
+    share = got_ref.shape[1] - 8
+    chunk = jnp.sum(from_halves(got_ref[:, 0:share, :]), axis=0)
+    wide = got_ref[:, share:, :].astype(F32)
     feats = wide[:, :, :64]
     feats = jnp.concatenate([feats[:pairs], feats[pairs:]], axis=2).reshape(rows, 128)
     cots = jnp.concatenate([wide[:, 0, 64:], wide[:, 1, 64:]], axis=1)
@@ -206,14 +211,14 @@
         sent_ref[peer, rows + groups:, :] = chunk
 
 
-def middle(got, spaces):
-    groups = got.shape[0]
+def middle(got, peers):
+    groups, rows, lanes = got.shape
     vmem = pl.BlockSpec(memory_space=pltpu.VMEM)
     return pl.pallas_call(
         middle_body,
         in_specs=[vmem],
         out_specs=vmem,
-        out_shape=jax.ShapeDtypeStruct((spaces, groups * 5 + 8, 128), BF16),
+        out_shape=jax.ShapeDtypeStruct((peers, groups * 5 + rows - 8, lanes), BF16),
         compiler_params=pltpu.CompilerParams(vmem_limit_bytes=8 * 1024 * 1024),
     )(got)
 
@@ -224,13 +229,14 @@
 
 
 def spread(got, groups):
-    spaces, rows, lanes = got.shape
+    peers, rows, lanes = got.shape
+    share = 256 // groups
     return pl.pallas_call(
         spread_body,
         grid=(1,),
-        in_specs=[pl.BlockSpec((spaces, 8, lanes), lambda i: (0, rows // 8 - 1, 0))],
-        out_specs=pl.BlockSpec((groups, 8, lanes), lambda i: (0, 0, 0)),
-        out_shape=jax.ShapeDtypeStruct((groups, 8, lanes), BF16),
+        in_specs=[pl.BlockSpec((peers, share, lanes), lambda i: (0, rows // share - 1, 0))],
+        out_specs=pl.BlockSpec((groups, share, lanes), lambda i: (0, 0, 0)),
+        out_shape=jax.ShapeDtypeStruct((groups, share, lanes), BF16),
         compiler_params=pltpu.CompilerParams(vmem_limit_bytes=8 * 1024 * 1024),
     )(got)
 
@@ -261,23 +267,28 @@
     return start - factor / bound, bound
 
 
-def dense_kernel_body(groups, place_ref, got_ref, delta_ref, total_ref, whole, cots):
-    spaces = got_ref.shape[0]
+def dense_kernel_body(groups, spaces, place_ref, got_ref, delta_ref, total_ref, whole, cots):
+    parts = got_ref.shape[0] // spaces
     width = 64
-    count = groups * 8
-    half = count // 2
+    block = groups * 8
+    count = parts * block
+    half = block // 2
 
     def slab_of(index):
-        both = got_ref[index].astype(F32)[:half]
-        return jnp.concatenate([both[:, :width], both[:, width:]], axis=0)
+        pieces = []
+        for part in range(parts):
+            both = got_ref[part * spaces + index].astype(F32)[:half]
+            pieces += [both[:, :width], both[:, width:]]
+        return jnp.concatenate(pieces, axis=0)
 
     for slab in range(0, spaces, 2):
         pair = jnp.concatenate([slab_of(slab), slab_of(slab + 1)], axis=1)
         whole[:, slab * width:(slab + 2) * width] = pair.astype(BF16)
-    for slab in range(spaces):
-        cots[pl.ds(slab, groups, stride=spaces), :] = got_ref[
-            slab, half:half + groups, :
-        ].astype(F32)
+    for part in range(parts):
+        for slab in range(spaces):
+            cots[pl.ds(part * block + slab, groups, stride=spaces), :] = got_ref[
+                part * spaces + slab, half:half + groups, :
+            ].astype(F32)
     cot_wide = cots[...]
     cot = cot_wide.astype(BF16)
     feats = whole[...]
@@ -311,11 +322,11 @@
     )
 
 
-def dense_delta(place, got, groups, outputs):
-    spaces = got.shape[0]
+def dense_delta(place, got, groups, spaces, outputs):
+    count = groups * 8 * (got.shape[0] // spaces)
     vmem = pl.BlockSpec(memory_space=pltpu.VMEM)
     return pl.pallas_call(
-        functools.partial(dense_kernel_body, groups),
+        functools.partial(dense_kernel_body, groups, spaces),
         in_specs=[pl.BlockSpec(memory_space=pltpu.SMEM), vmem],
         out_specs=[vmem, vmem],
         out_shape=[
@@ -323,8 +334,8 @@
             jax.ShapeDtypeStruct((1, 1), F32),
         ],
         scratch_shapes=[
-            pltpu.VMEM((groups * 8, spaces * 64), BF16),
-            pltpu.VMEM((groups * 8, outputs), F32),
+            pltpu.VMEM((count, spaces * 64), BF16),
+            pltpu.VMEM((count, outputs), F32),
         ],
         compiler_params=pltpu.CompilerParams(vmem_limit_bytes=48 * 1024 * 1024),
     )(place, got)
@@ -389,17 +400,18 @@
 
 
 def on_device(volume, conv_kernel, dense_weight, cotangent):
-    spaces = lax.axis_size("space")
-    groups = lax.axis_size("dp")
+    spaces = lax.axis_size(SPACE)
+    groups = lax.axis_size(DP)
+    column = lax.axis_size(COLUMN)
     samples, channels, planes, height, length = volume.shape
     filters, patch_rows = conv_kernel.shape
     slab = filters * PC
 
     up = [(i, i + 1) for i in range(spaces - 1)]
     down = [(j, i) for i, j in up]
-    before = lax.ppermute(volume[:, :, planes - 1:], "space", up)
-    after = lax.ppermute(volume[:, :, :1], "space", down)
-    cot_group = gather_from(cotangent[0], "space", spaces)
+    before = lax.ppermute(volume[:, :, planes - 1:], SPACE, up)
+    after = lax.ppermute(volume[:, :, :1], SPACE, down)
+    cot_group = gather_from(cotangent[0], SPACE, spaces)
 
     mixed = conv_kernel.reshape(filters, channels, 3, 9).transpose(0, 2, 1, 3)
     mixed = mixed.reshape(filters, patch_rows)
@@ -411,18 +423,21 @@
         ],
         axis=0,
     )
-    place = lax.axis_index("space")
+    place = lax.axis_index(SPACE)
     weight = lax.dynamic_slice_in_dim(dense_weight, place * slab, slab, 0)
     weight = weight.reshape(filters, PC, -1).transpose(1, 0, 2).reshape(slab, -1)
 
     sent = conv_moments(
-        volume, before, after, bands, weight, cot_group, cotangent, filters, groups
-    )
-    got = exchange(middle(exchange(sent, "dp"), spaces), "space")
-    reduced = exchange(spread(got, groups), "dp")
-    delta, dense_total = dense_delta(place.reshape(1), got, groups, cotangent.shape[1])
+        volume, before, after, bands, weight, cot_group, cotangent, filters, column
+    )
+    peers = spaces * groups // column
+    got = exchange(middle(exchange(sent, COLUMN), peers), PLANE)
+    reduced = exchange(spread(got, column), COLUMN)
+    delta, dense_total = dense_delta(
+        place.reshape(1), got, column, spaces, cotangent.shape[1]
+    )
     share = cotangent.shape[1] // groups
-    dense_block = lax.dynamic_slice_in_dim(delta, lax.axis_index("dp") * share, share, 0)
+    dense_block = lax.dynamic_slice_in_dim(delta, lax.axis_index(DP) * share, share, 0)
     cells = samples * groups * planes * spaces * height * length
     step_conv, step_dense = final_steps(
         reduced, dense_block, dense_total, column_order(channels), filters, patch_rows, cells
@@ -431,7 +446,8 @@
 
 
 def solution(mesh):
-    placed = (P("dp", None, "space", None, None), P(), P(), P(BOTH, None))
+    fine = jax.sharding.Mesh(mesh.devices.reshape(-1, 2, 2, 2, 4), ("z", "xh", "core", "xl", "y"))
+    placed = (P(DP, None, SPACE, None, None), P(), P(), P(DP + SPACE, None))
     return jax.shard_map(
-        on_device, mesh=mesh, in_specs=placed, out_specs=(P(), P("space", "dp")), check_vma=False
-    )
+        on_device, mesh=fine, in_specs=placed, out_specs=(P(), P(SPACE, DP)), check_vma=False
+    )

time: 85.8 us -> 81.1 us (0.945)
  blocking collectives: 0 us -> 19.4 us
  starting transfers between devices: 33.1 us -> 20.7 us
  waiting for transfers between devices: 24.6 us -> 13.8 us
    all_to_all x0 -> x1, blocking collectives: none -> 19.4 us  [exchange(): return lax.all_to_all(x, axes, split_axis=0, concat_axis=0, tiled=True)]
    all_to_all x4 -> x3, starting transfers between devices: 27.8 us -> 15.4 us  [exchange(): return lax.all_to_all(x, axes, split_axis=0, concat_axis=0, tiled=True)]
    all_to_all x4 -> x3, waiting for transfers between devices: 24.6 us -> 13.8 us  [exchange(): return lax.all_to_all(x, axes, split_axis=0, concat_axis=0, tiled=True)]
  transfers between devices with their start and end apart: 6 -> 5, of which waited for: 4 -> 3; matrix products, arithmetic and copies ran while one was open for 1% -> 1% of each run, Pallas kernels for 9% -> 9%
where the time goes in v4:
time: 81.1 us; the launch traced here: 80.7 us
  Pallas kernels  23.9 us (29%)
  starting transfers between devices  20.7 us (26%)
  blocking collectives  19.4 us (24%)
  waiting for transfers between devices  13.8 us (17%)
  local copies, waits for them, and re-layouts  1.97 us (2%)
    all_to_all x1, blocking collectives, exchange(): return lax.all_to_all(x, axes, split_axis=0, concat_axis=0, tiled=True)  19.4 us
    all_to_all x3, starting transfers between devices, exchange(): return lax.all_to_all(x, axes, split_axis=0, concat_axis=0, tiled=True)  15.4 us
    all_to_all x3, waiting for transfers between devices, exchange(): return lax.all_to_all(x, axes, split_axis=0, concat_axis=0, tiled=True)  13.8 us
    pallas_call x1, Pallas kernels, conv_moments(): pl.pallas_call(functools.partial(conv_kernel_body, sizes), grid=(samples,...  10.4 us
    pallas_call x1, Pallas kernels, dense_delta(): pl.pallas_call(functools.partial(dense_kernel_body, groups, spaces), in_s...  7.48 us
    pallas_call x1, Pallas kernels, final_steps(): pl.pallas_call(functools.partial(final_kernel_body, filters, patch_rows,...  4.27 us
    ppermute x1, starting transfers between devices, on_device(): before = lax.ppermute(volume[:, :, planes - 1:], SPACE, up)  4.03 us
  transfers between devices with their start and end apart: 5, of which 3 were waited for; matrix products, arithmetic and copies ran while one was open for 1% of the time, Pallas kernels for 9%

profile of v4, /device:TPU:1, one launch (start us, length us, event | category | flops | bytes accessed | tf_op | source)
XLA Modules:
  0.0 80.7 jit_solution(2050024371762017300)
XLA Ops:
  0.6 0.0 copy-start
  0.6 0.0 copy-start.1
  0.7 1.1 %fusion.22 = (bf16[8,4,1,16,128]{4,3,2,1,0:T(8,128)(2,1)S(1)}, bf16[8,4,1,16,128]{4,3,2,1,0:T(8,128)(2,1)S(1)}) fusion(bf16[8,4,4,16,128]{4,3,2,1,0:T(8,128)(2,1)} %vol_ref.1), kind=kLoop, calls=%fused_computation.43 | loop fusion | bytes 524288 | tf_op jit(solution)/shard_map/slice | solution.py:413
  1.7 4.0 %collective-permute-start = (bf16[8,4,1,16,128]{4,3,2,1,0:T(8,128)(2,1)S(1)}, bf16[8,4,1,16,128]{4,3,2,1,0:T(8,128)(2,1)S(1)}, u32[]{:S(2)}, u32[]{:S(2)}) collective-permute-start(bf16[8,4,1,16,128]{4,3,2,1,0:T(8,128)(2,1)S(1)} %get-tuple-element.11), channel_id=1, source_target_pairs={{0,1},{1,2},{2,3},{3,4},{4,5},{5,6},{6,7},{8,9},{9,10},{10,11},{11... | collective-permute-start | bytes 393224 | tf_op jit(solution)/shard_map/ppermute | solution.py:412
  5.8 0.0 copy-start.2
  5.8 0.0 copy-start.3
  5.8 1.3 %collective-permute-start.1 = (bf16[8,4,1,16,128]{4,3,2,1,0:T(8,128)(2,1)S(1)}, bf16[8,4,1,16,128]{4,3,2,1,0:T(8,128)(2,1)S(1)}, u32[]{:S(2)}, u32[]{:S(2)}) collective-permute-start(bf16[8,4,1,16,128]{4,3,2,1,0:T(8,128)(2,1)S(1)} %get-tuple-element.10), channel_id=1, source_target_pairs={{1,0},{2,1},{3,2},{4,3},{5,4},{6,5},{7,6},{9,8},{10,9},{11,10},{12... | collective-permute-start | bytes 393224 | tf_op jit(solution)/shard_map/ppermute | solution.py:413
  7.1 0.0 copy-done.2
  7.1 0.6 broadcast_in_dim.13
  7.7 5.9 %all-to-all-start = ((bf16[8,1,128]{2,1,0:T(2,128)(2,1)}), bf16[8,1,128]{2,1,0:T(2,128)(2,1)S(1)}, u32[]{:S(2)}, u32[]{:S(2)}) async-start(bf16[8,1,128]{2,1,0:T(2,128)(2,1)} %broadcast_in_dim.13), calls=%async_computation | async-start | bytes 8192 | tf_op jit(solution)/shard_map/all_to_all | solution.py:30
  13.6 0.0 copy-done.3
  13.6 0.1 copy.21
  13.8 0.1 copy.23
  13.9 0.1 fusion.16.bands_ref
  14.0 0.0 copy-done
  14.0 4.5 %all-to-all-done = bf16[8,1,128]{2,1,0:T(2,128)(2,1)S(1)} async-done(((bf16[8,1,128]{2,1,0:T(2,128)(2,1)}), bf16[8,1,128]{2,1,0:T(2,128)(2,1)S(1)}, u32[]{:S(2)}, u32[]{:S(2)}) %all-to-all-start) | async-done | bytes 2080 | tf_op jit(solution)/shard_map/all_to_all | solution.py:30
  18.5 0.0 collective-permute-done.before_ref
  18.5 0.0 collective-permute-done.1.after_ref
  18.6 0.0 copy-done.1
  18.6 10.4 %shard_map.62 = bf16[16,24,128]{2,1,0:T(8,128)(2,1)S(1)} custom-call(bf16[8,4,4,16,128]{4,3,2,1,0:T(8,128)(2,1)S(1)} %copy-done.1, bf16[8,4,1,16,128]{4,3,2,1,0:T(8,128)(2,1)S(1)} %collective-permute-done.before_ref, bf16[8,4,1,16,128]{4,3,2,1,0:T(8,128)(2,1)S(1)} %collective-permute-done.1.after_ref, bf16[128,216]{1,0:T(8,128)(2,1)S(1)} %fusion.16.bands_ref, ...), custom_call_target="tpu_custom_call" | custom-call | tf_op jit(solution)/shard_map/pallas_call | solution.py:169
  29.0 19.4 %all_to_all.23.got_ref = bf16[16,24,128]{2,1,0:T(8,128)(2,1)S(1)} all-to-all(bf16[16,24,128]{2,1,0:T(8,128)(2,1)S(1)} %shard_map.62), channel_id=1, replica_groups=mesh['z'=8,'xh'=2,'core'=2,'xl'=2,'y'=4] {'z','core'}, dimensions={0} | all-to-all | bytes 196608 | tf_op jit(solution)/shard_map/all_to_all | solution.py:30
  48.4 0.9 %shard_map.63 = bf16[16,96,128]{2,1,0:T(8,128)(2,1)} custom-call(bf16[16,24,128]{2,1,0:T(8,128)(2,1)S(1)} %all_to_all.23.got_ref), custom_call_target="tpu_custom_call" | custom-call | tf_op jit(solution)/shard_map/pallas_call | solution.py:217
  49.3 4.4 %all-to-all-start.2 = ((bf16[16,96,128]{2,1,0:T(8,128)(2,1)}), bf16[16,96,128]{2,1,0:T(8,128)(2,1)S(1)}, u32[]{:S(2)}, u32[]{:S(2)}) async-start(bf16[16,96,128]{2,1,0:T(8,128)(2,1)} %shard_map.63), calls=%async_computation.2 | async-start | bytes 786432 | tf_op jit(solution)/shard_map/all_to_all | solution.py:30
  53.8 8.9 %all-to-all-done.2.got_ref = bf16[16,96,128]{2,1,0:T(8,128)(2,1)S(1)} async-done(((bf16[16,96,128]{2,1,0:T(8,128)(2,1)}), bf16[16,96,128]{2,1,0:T(8,128)(2,1)S(1)}, u32[]{:S(2)}, u32[]{:S(2)}) %all-to-all-start.2) | async-done | bytes 393248 | tf_op jit(solution)/shard_map/all_to_all | solution.py:30
  62.7 0.8 %shard_map.64 = bf16[16,16,128]{2,1,0:T(8,128)(2,1)} custom-call(bf16[16,96,128]{2,1,0:T(8,128)(2,1)S(1)} %all-to-all-done.2.got_ref), custom_call_target="tpu_custom_call" | custom-call | tf_op jit(solution)/shard_map/pallas_call | solution.py:234
  63.5 5.1 %all-to-all-start.3 = ((bf16[16,16,128]{2,1,0:T(8,128)(2,1)}), bf16[16,16,128]{2,1,0:T(8,128)(2,1)S(1)}, u32[]{:S(2)}, u32[]{:S(2)}) async-start(bf16[16,16,128]{2,1,0:T(8,128)(2,1)} %shard_map.64), calls=%async_computation.3 | async-start | bytes 131072 | tf_op jit(solution)/shard_map/all_to_all | solution.py:30
  68.6 7.5 %shard_map.65 = (f32[128,64]{1,0:T(8,128)S(1)}, f32[1,1]{1,0:T(1,128)}) custom-call(s32[1]{0:T(128)} %bitcast.5.place_ref, bf16[16,96,128]{2,1,0:T(8,128)(2,1)S(1)} %all-to-all-done.2.got_ref), custom_call_target="tpu_custom_call" | custom-call | tf_op jit(solution)/shard_map/pallas_call | solution.py:328
  76.1 0.3 all-to-all-done.3.got_ref
  76.4 4.3 %shard_map.66 = (f32[32,108]{1,0:T(8,128)}, f32[4,64]{1,0:T(4,128)}) custom-call(bf16[16,16,128]{2,1,0:T(8,128)(2,1)S(1)} %all-to-all-done.3.got_ref, f32[4,64]{1,0:T(4,128)S(1)} %constant_dynamic-slice_fusion.dense_ref, f32[1,1]{1,0:T(1,128)} %get-tuple-element.7.total_ref, f32[128,128]{1,0:T(8,128)S(1)} %fusion.21.order_ref), custom_call_target="tpu_custom_call" | custom-call | tf_op jit(solution)/shard_map/pallas_call | solution.py:382
  (12 shorter events, 0.1 us)
Async XLA Ops:
  0.6 13.4 %copy-start = (bf16[512,128]{1,0:T(8,128)(2,1)S(1)}, bf16[512,128]{1,0:T(8,128)(2,1)}, u32[]{:S(2)}) copy-start(bf16[512,128]{1,0:T(8,128)(2,1)} %param.6) | copy-start | bytes 393220
  0.6 17.9 %copy-start.1 = (bf16[8,4,4,16,128]{4,3,2,1,0:T(8,128)(2,1)S(1)}, bf16[8,4,4,16,128]{4,3,2,1,0:T(8,128)(2,1)}, u32[]{:S(2)}) copy-start(bf16[8,4,4,16,128]{4,3,2,1,0:T(8,128)(2,1)} %vol_ref.1) | copy-start | bytes 1572868
  1.7 16.8 %collective-permute-start = (bf16[8,4,1,16,128]{4,3,2,1,0:T(8,128)(2,1)S(1)}, bf16[8,4,1,16,128]{4,3,2,1,0:T(8,128)(2,1)S(1)}, u32[]{:S(2)}, u32[]{:S(2)}) collective-permute-start(bf16[8,4,1,16,128]{4,3,2,1,0:T(8,128)(2,1)S(1)} %get-tuple-element.11), channel_id=1, source_target_pairs={{0,1},{1,2},{2,3},{3,4},{4,5},{5,6},{6,7},{8,9},{9,10},{10,11},{11... | collective-permute-start | bytes 393224 | tf_op jit(solution)/shard_map/ppermute | solution.py:412
  5.8 1.3 %copy-start.2 = (bf16[1,128]{1,0:T(2,128)(2,1)S(1)}, bf16[1,128]{1,0:T(2,128)(2,1)}, u32[]{:S(2)}) copy-start(bf16[1,128]{1,0:T(2,128)(2,1)} %own_ref.1) | copy-start | bytes 772
  5.8 7.8 %copy-start.3 = (bf16[32,108]{1,0:T(8,128)(2,1)S(1)}, bf16[32,108]{1,0:T(8,128)(2,1)}, u32[]{:S(2)}) copy-start(bf16[32,108]{1,0:T(8,128)(2,1)} %param.5) | copy-start | bytes 20740
  5.8 12.8 %collective-permute-start.1 = (bf16[8,4,1,16,128]{4,3,2,1,0:T(8,128)(2,1)S(1)}, bf16[8,4,1,16,128]{4,3,2,1,0:T(8,128)(2,1)S(1)}, u32[]{:S(2)}, u32[]{:S(2)}) collective-permute-start(bf16[8,4,1,16,128]{4,3,2,1,0:T(8,128)(2,1)S(1)} %get-tuple-element.10), channel_id=1, source_target_pairs={{1,0},{2,1},{3,2},{4,3},{5,4},{6,5},{7,6},{9,8},{10,9},{11,10},{12... | collective-permute-start | bytes 393224 | tf_op jit(solution)/shard_map/ppermute | solution.py:413
  7.7 10.9 %all-to-all-start = ((bf16[8,1,128]{2,1,0:T(2,128)(2,1)}), bf16[8,1,128]{2,1,0:T(2,128)(2,1)S(1)}, u32[]{:S(2)}, u32[]{:S(2)}) async-start(bf16[8,1,128]{2,1,0:T(2,128)(2,1)} %broadcast_in_dim.13), calls=%async_computation | async-start | bytes 8192 | tf_op jit(solution)/shard_map/all_to_all | solution.py:30
  49.3 13.4 %all-to-all-start.2 = ((bf16[16,96,128]{2,1,0:T(8,128)(2,1)}), bf16[16,96,128]{2,1,0:T(8,128)(2,1)S(1)}, u32[]{:S(2)}, u32[]{:S(2)}) async-start(bf16[16,96,128]{2,1,0:T(8,128)(2,1)} %shard_map.63), calls=%async_computation.2 | async-start | bytes 786432 | tf_op jit(solution)/shard_map/all_to_all | solution.py:30
  63.5 12.9 %all-to-all-start.3 = ((bf16[16,16,128]{2,1,0:T(8,128)(2,1)}), bf16[16,16,128]{2,1,0:T(8,128)(2,1)S(1)}, u32[]{:S(2)}, u32[]{:S(2)}) async-start(bf16[16,16,128]{2,1,0:T(8,128)(2,1)} %shard_map.64), calls=%async_computation.3 | async-start | bytes 131072 | tf_op jit(solution)/shard_map/all_to_all | solution.py:30

commit v5 on v4

--- a/solution.py
+++ b/solution.py
@@ -7,6 +7,7 @@
 from jax.experimental.pallas import tpu as pltpu
 from jax.sharding import PartitionSpec as P
 
+
 PC = 2
 NS_STEPS = 8
 
@@ -14,7 +15,6 @@
 DAMPING = 0.1
 KL_BOUND = 0.0001
 LEARN_RATE = 0.01
-HIGHEST = lax.Precision.HIGHEST
 CONTRACT = (((1,), (1,)), ((), ()))
 LEADING = (((0,), (0,)), ((), ()))
 DP = ("z", "xh", "core")
@@ -241,8 +241,53 @@
     )(got)
 
 
-def exact_dot(a, b):
-    return jnp.dot(a, b, precision=HIGHEST, preferred_element_type=F32)
+def parts_of(x):
+    high = x.astype(BF16)
+    return high, (x - high.astype(F32)).astype(BF16)
+
+
+def split_dot(a, b):
+    a_high, a_low = parts_of(a)
+    b_high, b_low = parts_of(b)
+    return jnp.dot(
+        jnp.concatenate([a_high, a_high, a_low], axis=1),
+        jnp.concatenate([b_high, b_low, b_high], axis=0),
+        preferred_element_type=F32,
+    )
+
+
+def square_and_apply(left, held, last):
+    order = left.shape[1]
+    if last:
+        both = held
+    else:
+        both = jnp.concatenate([left, held], axis=1)
+    if both.shape[0] < order:
+        rest = jnp.zeros((order - both.shape[0], both.shape[1]), F32)
+        both = jnp.concatenate([both, rest], axis=0)
+    product = split_dot(left, both)
+    if last:
+        return left, held + product
+    return product[:, :order], held + product[:, order:]
+
+
+def square_and_extend(inverse, right, last):
+    if last:
+        return inverse + split_dot(inverse, right), right
+    order = right.shape[0]
+    product = split_dot(jnp.concatenate([inverse, right], axis=0), right)
+    return inverse + product[:order], product[order:]
+
+
+def two_sided(left, held, right):
+    order = right.shape[0]
+    inverse = jnp.where(unit(order), 1.0, 0.0) + right
+    right = split_dot(right, right)
+    for step in range(NS_STEPS):
+        left, held = square_and_apply(left, held, step == NS_STEPS - 1)
+        if step > 0:
+            inverse, right = square_and_extend(inverse, right, step == NS_STEPS - 1)
+    return split_dot(held, inverse)
 
 
 def unit(order):
@@ -303,22 +348,20 @@
     bound = jnp.max(sums, axis=1, keepdims=True)
     left = jnp.where(eye, 1.0 - damping / bound, 0.0) - gram / bound
     right, bound_out = residual(dense_out, dense_out.shape[0])
-    held = cot_wide * (scale / bound / bound_out)
-    for newton_step in range(NS_STEPS):
-        held = held + exact_dot(left, held)
-        held = held + exact_dot(held, right)
-        if newton_step < NS_STEPS - 1:
-            left = exact_dot(left, left)
-            right = exact_dot(right, right)
-    total_ref[...] = scalar_sum(held * exact_dot(gram, cot_wide))
+    held = two_sided(left, cot_wide * (scale / bound / bound_out), right)
+    total_ref[...] = scalar_sum(held * split_dot(gram, cot_wide))
     mine = slab_of(place_ref[0])
     source = lax.broadcasted_iota(jnp.int32, (width, width), 0)
     target = lax.broadcasted_iota(jnp.int32, (width, width), 1)
     spot = (target % PC) * (width // PC) + target // PC
     pick = jnp.where(source == spot, 1.0, 0.0).astype(BF16)
-    mine = jnp.dot(mine.astype(BF16), pick, preferred_element_type=F32)
+    mine = jnp.dot(mine.astype(BF16), pick, preferred_element_type=F32).astype(BF16)
+    high, low = parts_of(held)
     delta_ref[...] = lax.dot_general(
-        held, mine, LEADING, precision=HIGHEST, preferred_element_type=F32
+        jnp.concatenate([high, low], axis=0),
+        jnp.concatenate([mine, mine], axis=0),
+        LEADING,
+        preferred_element_type=F32,
     )
 
 
@@ -358,21 +401,15 @@
         [moments[first:first + filters], moments[first + filters:first + 2 * filters]],
         axis=1,
     ) * scale
-    conv_out = moments[first + 2 * filters:first + 3 * filters, 0:filters] * scale
+    conv_out = moments[first + 2 * filters:first + 3 * filters]
+    conv_out = jnp.concatenate([conv_out, jnp.zeros((filters, 64), F32)], axis=1)
+    conv_out = jnp.concatenate([conv_out, jnp.zeros((128 - filters, 128), F32)], axis=0) * scale
     right, bound_in = residual(conv_in, patch_rows)
     left, bound_out = residual(conv_out, filters)
-    held = conv_grad / bound_in / bound_out
-    inverse = jnp.where(unit(128), 1.0, 0.0) + right
-    for newton_step in range(NS_STEPS):
-        held = held + exact_dot(left, held)
-        if newton_step < NS_STEPS - 1:
-            left = exact_dot(left, left)
-            right = exact_dot(right, right)
-            inverse = inverse + exact_dot(inverse, right)
-    held = exact_dot(held, inverse)
+    held = two_sided(left[0:filters], conv_grad / bound_in / bound_out, right)
     total = scalar_sum(held * conv_grad) + total_ref[...]
     scaling = jnp.minimum(1.0, jnp.sqrt(KL_BOUND / (LEARN_RATE * LEARN_RATE * total)))
-    moved = exact_dot(held, order_ref[...])
+    moved = split_dot(held, order_ref[...])
     step_conv_ref[...] = scaling * moved[:, 0:patch_rows]
     step_dense_ref[...] = scaling * dense_ref[...]
 
@@ -409,9 +446,9 @@
 
     up = [(i, i + 1) for i in range(spaces - 1)]
     down = [(j, i) for i, j in up]
+    cot_group = gather_from(cotangent[0], SPACE, spaces)
     before = lax.ppermute(volume[:, :, planes - 1:], SPACE, up)
     after = lax.ppermute(volume[:, :, :1], SPACE, down)
-    cot_group = gather_from(cotangent[0], SPACE, spaces)
 
     mixed = conv_kernel.reshape(filters, channels, 3, 9).transpose(0, 2, 1, 3)
     mixed = mixed.reshape(filters, patch_rows)

time: 81.1 us -> 80.4 us (level)
  Pallas kernels: 23.9 us -> 20.1 us
  waiting for transfers between devices: 13.8 us -> 16.8 us
    all_to_all x3, waiting for transfers between devices: 13.8 us -> 16.8 us  [exchange(): return lax.all_to_all(x, axes, split_axis=0, concat_axis=0, tiled=True)]
    pallas_call x1, Pallas kernels: 7.48 us -> 4.4 us  [dense_delta(): pl.pallas_call(functools.partial(dense_kernel_body, groups, spaces), in_s...]
  transfers between devices with their start and end apart: 5 -> 5, of which waited for: 3 -> 3; matrix products, arithmetic and copies ran while one was open for 1% -> 1% of each run, Pallas kernels for 9% -> 6%
where the time goes in v5:
time: 80.4 us; the launch traced here: 80 us
  starting transfers between devices  20.7 us (26%)
  Pallas kernels  20.1 us (25%)
  blocking collectives  19.4 us (24%)
  waiting for transfers between devices  16.8 us (21%)
  local copies, waits for them, and re-layouts  1.97 us (2%)
  between operations  0.81 us (1%)
    all_to_all x1, blocking collectives, exchange(): return lax.all_to_all(x, axes, split_axis=0, concat_axis=0, tiled=True)  19.4 us
    all_to_all x3, waiting for transfers between devices, exchange(): return lax.all_to_all(x, axes, split_axis=0, concat_axis=0, tiled=True)  16.8 us
    all_to_all x3, starting transfers between devices, exchange(): return lax.all_to_all(x, axes, split_axis=0, concat_axis=0, tiled=True)  15.4 us
    pallas_call x1, Pallas kernels, conv_moments(): pl.pallas_call(functools.partial(conv_kernel_body, sizes), grid=(samples,...  10.4 us
    pallas_call x1, Pallas kernels, dense_delta(): pl.pallas_call(functools.partial(dense_kernel_body, groups, spaces), in_s...  4.4 us
    ppermute x1, starting transfers between devices, on_device(): before = lax.ppermute(volume[:, :, planes - 1:], SPACE, up)  4.03 us
    pallas_call x1, Pallas kernels, final_steps(): pl.pallas_call(functools.partial(final_kernel_body, filters, patch_rows,...  3.53 us
  transfers between devices with their start and end apart: 5, of which 3 were waited for; matrix products, arithmetic and copies ran while one was open for 1% of the time, Pallas kernels for 6%

profile of v5, /device:TPU:1, one launch (start us, length us, event | category | flops | bytes accessed | tf_op | source)
XLA Modules:
  0.0 80.0 jit_solution(15380955020933293225)
XLA Ops:
  0.6 0.0 copy-start
  0.6 0.0 copy-start.1
  0.7 1.1 %fusion.22 = (bf16[8,4,1,16,128]{4,3,2,1,0:T(8,128)(2,1)S(1)}, bf16[8,4,1,16,128]{4,3,2,1,0:T(8,128)(2,1)S(1)}) fusion(bf16[8,4,4,16,128]{4,3,2,1,0:T(8,128)(2,1)} %vol_ref.1), kind=kLoop, calls=%fused_computation.43 | loop fusion | bytes 524288 | tf_op jit(solution)/shard_map/slice | solution.py:451
  1.7 4.0 %collective-permute-start = (bf16[8,4,1,16,128]{4,3,2,1,0:T(8,128)(2,1)S(1)}, bf16[8,4,1,16,128]{4,3,2,1,0:T(8,128)(2,1)S(1)}, u32[]{:S(2)}, u32[]{:S(2)}) collective-permute-start(bf16[8,4,1,16,128]{4,3,2,1,0:T(8,128)(2,1)S(1)} %get-tuple-element.11), channel_id=1, source_target_pairs={{0,1},{1,2},{2,3},{3,4},{4,5},{5,6},{6,7},{8,9},{9,10},{10,11},{11... | collective-permute-start | bytes 393224 | tf_op jit(solution)/shard_map/ppermute | solution.py:450
  5.8 0.0 copy-start.2
  5.8 0.0 copy-start.3
  5.8 1.3 %collective-permute-start.1 = (bf16[8,4,1,16,128]{4,3,2,1,0:T(8,128)(2,1)S(1)}, bf16[8,4,1,16,128]{4,3,2,1,0:T(8,128)(2,1)S(1)}, u32[]{:S(2)}, u32[]{:S(2)}) collective-permute-start(bf16[8,4,1,16,128]{4,3,2,1,0:T(8,128)(2,1)S(1)} %get-tuple-element.10), channel_id=1, source_target_pairs={{1,0},{2,1},{3,2},{4,3},{5,4},{6,5},{7,6},{9,8},{10,9},{11,10},{12... | collective-permute-start | bytes 393224 | tf_op jit(solution)/shard_map/ppermute | solution.py:451
  7.1 0.0 copy-done.2
  7.1 0.6 broadcast_in_dim.13
  7.7 5.9 %all-to-all-start = ((bf16[8,1,128]{2,1,0:T(2,128)(2,1)}), bf16[8,1,128]{2,1,0:T(2,128)(2,1)S(1)}, u32[]{:S(2)}, u32[]{:S(2)}) async-start(bf16[8,1,128]{2,1,0:T(2,128)(2,1)} %broadcast_in_dim.13), calls=%async_computation | async-start | bytes 8192 | tf_op jit(solution)/shard_map/all_to_all | solution.py:30
  13.6 0.0 copy-done.3
  13.6 0.1 copy.21
  13.8 0.1 copy.23
  13.9 0.1 fusion.16.bands_ref
  14.0 0.0 copy-done
  14.0 4.5 %all-to-all-done = bf16[8,1,128]{2,1,0:T(2,128)(2,1)S(1)} async-done(((bf16[8,1,128]{2,1,0:T(2,128)(2,1)}), bf16[8,1,128]{2,1,0:T(2,128)(2,1)S(1)}, u32[]{:S(2)}, u32[]{:S(2)}) %all-to-all-start) | async-done | bytes 2080 | tf_op jit(solution)/shard_map/all_to_all | solution.py:30
  18.5 0.0 collective-permute-done.before_ref
  18.5 0.0 collective-permute-done.1.after_ref
  18.6 0.0 copy-done.1
  18.6 10.4 %shard_map.62 = bf16[16,24,128]{2,1,0:T(8,128)(2,1)S(1)} custom-call(bf16[8,4,4,16,128]{4,3,2,1,0:T(8,128)(2,1)S(1)} %copy-done.1, bf16[8,4,1,16,128]{4,3,2,1,0:T(8,128)(2,1)S(1)} %collective-permute-done.before_ref, bf16[8,4,1,16,128]{4,3,2,1,0:T(8,128)(2,1)S(1)} %collective-permute-done.1.after_ref, bf16[128,216]{1,0:T(8,128)(2,1)S(1)} %fusion.16.bands_ref, ...), custom_call_target="tpu_custom_call" | custom-call | tf_op jit(solution)/shard_map/pallas_call | solution.py:169
  29.0 19.4 %all_to_all.23.got_ref = bf16[16,24,128]{2,1,0:T(8,128)(2,1)S(1)} all-to-all(bf16[16,24,128]{2,1,0:T(8,128)(2,1)S(1)} %shard_map.62), channel_id=1, replica_groups=mesh['z'=8,'xh'=2,'core'=2,'xl'=2,'y'=4] {'z','core'}, dimensions={0} | all-to-all | bytes 196608 | tf_op jit(solution)/shard_map/all_to_all | solution.py:30
  48.4 0.9 %shard_map.63 = bf16[16,96,128]{2,1,0:T(8,128)(2,1)} custom-call(bf16[16,24,128]{2,1,0:T(8,128)(2,1)S(1)} %all_to_all.23.got_ref), custom_call_target="tpu_custom_call" | custom-call | tf_op jit(solution)/shard_map/pallas_call | solution.py:217
  49.3 4.4 %all-to-all-start.2 = ((bf16[16,96,128]{2,1,0:T(8,128)(2,1)}), bf16[16,96,128]{2,1,0:T(8,128)(2,1)S(1)}, u32[]{:S(2)}, u32[]{:S(2)}) async-start(bf16[16,96,128]{2,1,0:T(8,128)(2,1)} %shard_map.63), calls=%async_computation.2 | async-start | bytes 786432 | tf_op jit(solution)/shard_map/all_to_all | solution.py:30
  53.8 8.9 %all-to-all-done.2.got_ref = bf16[16,96,128]{2,1,0:T(8,128)(2,1)S(1)} async-done(((bf16[16,96,128]{2,1,0:T(8,128)(2,1)}), bf16[16,96,128]{2,1,0:T(8,128)(2,1)S(1)}, u32[]{:S(2)}, u32[]{:S(2)}) %all-to-all-start.2) | async-done | bytes 393248 | tf_op jit(solution)/shard_map/all_to_all | solution.py:30
  62.7 0.8 %shard_map.64 = bf16[16,16,128]{2,1,0:T(8,128)(2,1)} custom-call(bf16[16,96,128]{2,1,0:T(8,128)(2,1)S(1)} %all-to-all-done.2.got_ref), custom_call_target="tpu_custom_call" | custom-call | tf_op jit(solution)/shard_map/pallas_call | solution.py:234
  63.5 5.1 %all-to-all-start.3 = ((bf16[16,16,128]{2,1,0:T(8,128)(2,1)}), bf16[16,16,128]{2,1,0:T(8,128)(2,1)S(1)}, u32[]{:S(2)}, u32[]{:S(2)}) async-start(bf16[16,16,128]{2,1,0:T(8,128)(2,1)} %shard_map.64), calls=%async_computation.3 | async-start | bytes 131072 | tf_op jit(solution)/shard_map/all_to_all | solution.py:30
  68.6 4.4 %shard_map.65 = (f32[128,64]{1,0:T(8,128)S(1)}, f32[1,1]{1,0:T(1,128)}) custom-call(s32[1]{0:T(128)} %bitcast.5.place_ref, bf16[16,96,128]{2,1,0:T(8,128)(2,1)S(1)} %all-to-all-done.2.got_ref), custom_call_target="tpu_custom_call" | custom-call | tf_op jit(solution)/shard_map/pallas_call | solution.py:371
  73.0 3.4 %all-to-all-done.3.got_ref = bf16[16,16,128]{2,1,0:T(8,128)(2,1)S(1)} async-done(((bf16[16,16,128]{2,1,0:T(8,128)(2,1)}), bf16[16,16,128]{2,1,0:T(8,128)(2,1)S(1)}, u32[]{:S(2)}, u32[]{:S(2)}) %all-to-all-start.3) | async-done | bytes 65568 | tf_op jit(solution)/shard_map/all_to_all | solution.py:30
  76.4 3.5 %shard_map.66 = (f32[32,108]{1,0:T(8,128)}, f32[4,64]{1,0:T(4,128)}) custom-call(bf16[16,16,128]{2,1,0:T(8,128)(2,1)S(1)} %all-to-all-done.3.got_ref, f32[4,64]{1,0:T(4,128)S(1)} %constant_dynamic-slice_fusion.dense_ref, f32[1,1]{1,0:T(1,128)} %get-tuple-element.7.total_ref, f32[128,128]{1,0:T(8,128)S(1)} %fusion.21.order_ref), custom_call_target="tpu_custom_call" | custom-call | tf_op jit(solution)/shard_map/pallas_call | solution.py:419
  (12 shorter events, 0.1 us)
Async XLA Ops:
  0.6 13.4 %copy-start = (bf16[512,128]{1,0:T(8,128)(2,1)S(1)}, bf16[512,128]{1,0:T(8,128)(2,1)}, u32[]{:S(2)}) copy-start(bf16[512,128]{1,0:T(8,128)(2,1)} %param.6) | copy-start | bytes 393220
  0.6 17.9 %copy-start.1 = (bf16[8,4,4,16,128]{4,3,2,1,0:T(8,128)(2,1)S(1)}, bf16[8,4,4,16,128]{4,3,2,1,0:T(8,128)(2,1)}, u32[]{:S(2)}) copy-start(bf16[8,4,4,16,128]{4,3,2,1,0:T(8,128)(2,1)} %vol_ref.1) | copy-start | bytes 1572868
  1.7 16.8 %collective-permute-start = (bf16[8,4,1,16,128]{4,3,2,1,0:T(8,128)(2,1)S(1)}, bf16[8,4,1,16,128]{4,3,2,1,0:T(8,128)(2,1)S(1)}, u32[]{:S(2)}, u32[]{:S(2)}) collective-permute-start(bf16[8,4,1,16,128]{4,3,2,1,0:T(8,128)(2,1)S(1)} %get-tuple-element.11), channel_id=1, source_target_pairs={{0,1},{1,2},{2,3},{3,4},{4,5},{5,6},{6,7},{8,9},{9,10},{10,11},{11... | collective-permute-start | bytes 393224 | tf_op jit(solution)/shard_map/ppermute | solution.py:450
  5.8 1.3 %copy-start.2 = (bf16[1,128]{1,0:T(2,128)(2,1)S(1)}, bf16[1,128]{1,0:T(2,128)(2,1)}, u32[]{:S(2)}) copy-start(bf16[1,128]{1,0:T(2,128)(2,1)} %own_ref.1) | copy-start | bytes 772
  5.8 7.8 %copy-start.3 = (bf16[32,108]{1,0:T(8,128)(2,1)S(1)}, bf16[32,108]{1,0:T(8,128)(2,1)}, u32[]{:S(2)}) copy-start(bf16[32,108]{1,0:T(8,128)(2,1)} %param.5) | copy-start | bytes 20740
  5.8 12.8 %collective-permute-start.1 = (bf16[8,4,1,16,128]{4,3,2,1,0:T(8,128)(2,1)S(1)}, bf16[8,4,1,16,128]{4,3,2,1,0:T(8,128)(2,1)S(1)}, u32[]{:S(2)}, u32[]{:S(2)}) collective-permute-start(bf16[8,4,1,16,128]{4,3,2,1,0:T(8,128)(2,1)S(1)} %get-tuple-element.10), channel_id=1, source_target_pairs={{1,0},{2,1},{3,2},{4,3},{5,4},{6,5},{7,6},{9,8},{10,9},{11,10},{12... | collective-permute-start | bytes 393224 | tf_op jit(solution)/shard_map/ppermute | solution.py:451
  7.7 10.9 %all-to-all-start = ((bf16[8,1,128]{2,1,0:T(2,128)(2,1)}), bf16[8,1,128]{2,1,0:T(2,128)(2,1)S(1)}, u32[]{:S(2)}, u32[]{:S(2)}) async-start(bf16[8,1,128]{2,1,0:T(2,128)(2,1)} %broadcast_in_dim.13), calls=%async_computation | async-start | bytes 8192 | tf_op jit(solution)/shard_map/all_to_all | solution.py:30
  49.3 13.4 %all-to-all-start.2 = ((bf16[16,96,128]{2,1,0:T(8,128)(2,1)}), bf16[16,96,128]{2,1,0:T(8,128)(2,1)S(1)}, u32[]{:S(2)}, u32[]{:S(2)}) async-start(bf16[16,96,128]{2,1,0:T(8,128)(2,1)} %shard_map.63), calls=%async_computation.2 | async-start | bytes 786432 | tf_op jit(solution)/shard_map/all_to_all | solution.py:30
  63.5 12.9 %all-to-all-start.3 = ((bf16[16,16,128]{2,1,0:T(8,128)(2,1)}), bf16[16,16,128]{2,1,0:T(8,128)(2,1)S(1)}, u32[]{:S(2)}, u32[]{:S(2)}) async-start(bf16[16,16,128]{2,1,0:T(8,128)(2,1)} %shard_map.64), calls=%async_computation.3 | async-start | bytes 131072 | tf_op jit(solution)/shard_map/all_to_all | solution.py:30

commit v6 on v5

--- a/solution.py
+++ b/solution.py
@@ -34,118 +34,248 @@
     return exchange(jnp.broadcast_to(x[None], (peers,) + x.shape), axes)
 
 
+def turned(x, by):
+    return pltpu.roll(x, x.shape[1] - by, 1) if by else x
+
+
 def conv_kernel_body(
-    sizes, vol_ref, before_ref, after_ref, bands_ref, weight_ref, cot_ref, own_ref,
-    sent_ref, pool_ref, shifted, stacked, grads, acc, acc_out,
+    sizes, vol_ref, before_ref, after_ref, bands_ref,
+    pool_ref, sums_ref, gram_ref, shift_a, shift_b, stack_a, stack_b, wide_a, wide_b,
 ):
     channels, planes, height, length, filters, samples = sizes
     rim = planes + 2
-    per_plane = channels * 9
-    rows = rim * per_plane
-    cells = height * length
-    half = cells // PC
+    group = rim * channels * 3
+    rows = 3 * group
+    half = height * length // PC
     top = planes * filters
+    base = top + 16
     step = pl.program_id(0)
+
+    def build(sample, shifted, stacked):
+        lane = lax.broadcasted_iota(jnp.int32, (height, length), 1)
+        for plane in range(rim):
+            for channel in range(channels):
+                if plane == 0:
+                    value = before_ref[sample, channel, 0]
+                elif plane == rim - 1:
+                    value = after_ref[sample, channel, 0]
+                else:
+                    value = vol_ref[sample, channel, plane - 1]
+                value = value.astype(F32)
+                moved = (
+                    jnp.where(lane == 0, 0.0, pltpu.roll(value, 1, 1)),
+                    value,
+                    jnp.where(lane == length - 1, 0.0, pltpu.roll(value, length - 1, 1)),
+                )
+                for k in range(3):
+                    row = group + (plane * channels + channel) * 3 + k
+                    shifted[pl.ds(row, height, stride=group), :] = moved[k]
+        for y in range(height):
+            stacked[base:, y * length:(y + 1) * length] = shifted[
+                y * group:y * group + rows, :
+            ].astype(BF16)
+
+    def consume(sample, stacked, wide):
+        slot = sample * PC
+        pooled = []
+        for part in range(PC):
+            total = jnp.zeros((filters, 128), F32)
+            for piece in range(2):
+                first = part * half + piece * (half // 2)
+                lanes = slice(first, first + half // 2)
+                pre = jnp.dot(bands_ref[...], stacked[base:, lanes], preferred_element_type=F32)
+                stacked[0:top, lanes] = jnp.where(pre > 0, 1.0, 0.0).astype(BF16)
+                active = jnp.where(pre > 0, pre, LEAK_SLOPE * pre)
+                for plane in range(planes):
+                    for at in range(0, half // 2, 128):
+                        total += active[plane * filters:(plane + 1) * filters, at:at + 128]
+            pooled.append(jnp.sum(total, axis=1, keepdims=True))
+            lanes = slice(part * half, (part + 1) * half)
+            gram = lax.dot_general(
+                stacked[:base + group, lanes], stacked[base:, lanes], CONTRACT,
+                preferred_element_type=F32,
+            )
+            wide[part, :, :rows] = gram[:top + 8]
+            gram_ref[:, :rows] += gram[base:]
+            square = lax.dot_general(
+                stacked[:base, lanes], stacked[:top, lanes], CONTRACT,
+                preferred_element_type=F32,
+            )
+            for first, last in ((0, filters), (top, top + 8)):
+                patch = jnp.zeros((last - first, 256), F32)
+                mask = jnp.zeros((last - first, top), F32)
+                for plane in range(planes):
+                    at = slice(first, last)
+                    if first == 0:
+                        at = slice(plane * filters, (plane + 1) * filters)
+                    patch += turned(wide[part, at, :], plane * channels * 3)
+                    mask += turned(square[at], plane * filters)
+                to = slice(0, filters) if first == 0 else slice(filters, filters + 8)
+                sums_ref[slot + part, to, :256] = patch
+                sums_ref[slot + part, to, 256:] = mask
+        for side, y in ((0, height - 1), (1, 0)):
+            edge = stacked[base + group:base + 2 * group, y * length:(y + 1) * length]
+            gram_ref[:, 256 + side * 128:256 + side * 128 + group] += lax.dot_general(
+                edge, edge, CONTRACT, preferred_element_type=F32
+            )
+        pooled = jnp.concatenate(pooled, axis=0) * (1.0 / (planes * half))
+        spot = lax.broadcasted_iota(jnp.int32, pool_ref.shape, 1)
+        pool_ref[...] = jnp.where(spot == sample, pooled, pool_ref[...])
 
     @pl.when(step == 0)
     def _():
-        shifted[...] = jnp.zeros_like(shifted)
-        acc[...] = jnp.zeros_like(acc)
-        acc_out[...] = jnp.zeros_like(acc_out)
+        shift_a[...] = jnp.zeros_like(shift_a)
+        shift_b[...] = jnp.zeros_like(shift_b)
+        ones = jnp.ones((16, height * length), BF16)
+        stack_a[top:base, :] = ones
+        stack_b[top:base, :] = ones
+        gram_ref[...] = jnp.zeros_like(gram_ref)
         pool_ref[...] = jnp.zeros_like(pool_ref)
-        grads[...] = lax.dot_general(
-            weight_ref[...], cot_ref[...], CONTRACT, preferred_element_type=F32
-        ).astype(BF16).astype(F32)
-
-    lane = lax.broadcasted_iota(jnp.int32, (height, length), 1)
-    for plane in range(rim):
-        for channel in range(channels):
-            if plane == 0:
-                value = before_ref[0, channel, 0]
-            elif plane == rim - 1:
-                value = after_ref[0, channel, 0]
-            else:
-                value = vol_ref[0, channel, plane - 1]
-            value = value.astype(F32)
-            moved = (
-                jnp.where(lane == 0, 0.0, pltpu.roll(value, 1, 1)),
-                value,
-                jnp.where(lane == length - 1, 0.0, pltpu.roll(value, length - 1, 1)),
+        build(0, shift_a, stack_a)
+
+    build(2 * step + 1, shift_b, stack_b)
+    consume(2 * step, stack_a, wide_a)
+    build(jnp.minimum(2 * step + 2, samples - 1), shift_a, stack_a)
+    consume(2 * step + 1, stack_b, wide_b)
+
+
+def conv_sums(volume, before, after, bands, filters):
+    samples, channels, planes, height, length = volume.shape
+    group = (planes + 2) * channels * 3
+    top = planes * filters
+    stack = top + 16 + 3 * group
+    sizes = (channels, planes, height, length, filters, samples)
+    vmem = pl.BlockSpec(memory_space=pltpu.VMEM)
+    return pl.pallas_call(
+        functools.partial(conv_kernel_body, sizes),
+        grid=(samples // 2,),
+        in_specs=[vmem] * 4,
+        out_specs=[vmem] * 3,
+        out_shape=[
+            jax.ShapeDtypeStruct((filters * PC, 128), F32),
+            jax.ShapeDtypeStruct((samples * PC, filters + 8, 256 + top), F32),
+            jax.ShapeDtypeStruct((group, 512), F32),
+        ],
+        scratch_shapes=[
+            pltpu.VMEM(((height + 2) * group, length), F32),
+            pltpu.VMEM(((height + 2) * group, length), F32),
+            pltpu.VMEM((stack, height * length), BF16),
+            pltpu.VMEM((stack, height * length), BF16),
+            pltpu.VMEM((PC, top + 8, 256), F32),
+            pltpu.VMEM((PC, top + 8, 256), F32),
+        ],
+        compiler_params=pltpu.CompilerParams(vmem_limit_bytes=24 * 1024 * 1024),
+    )(volume, before, after, bands)
+
+
+def moments_body(
+    sizes, pool_ref, sums_ref, gram_ref, weight_ref, cot_ref, own_ref, sent_ref, held, turned_up,
+):
+    channels, planes, cells, filters, samples = sizes
+    inner = channels * 3
+    group = (planes + 2) * inner
+    wide = 3 * 3 * inner
+    part_rows = 3 * inner
+    lanes_of = lambda shape: lax.broadcasted_iota(jnp.int32, shape, 1)
+
+    def compact(x):
+        lane = lanes_of(x.shape)
+        out = jnp.where(lane < part_rows, x, 0.0)
+        for j in range(1, 3):
+            here = jnp.logical_and(lane >= j * part_rows, lane < (j + 1) * part_rows)
+            out = jnp.where(here, turned(x, j * (group - part_rows)), out)
+        return out[:, :128]
+
+    cots = cot_ref[...]
+    gradient = jnp.zeros((filters, 256), F32)
+    moment_out = jnp.zeros((filters, 128), F32)
+    cross = jnp.zeros((filters, 128), F32)
+    for part in range(PC):
+        weight = weight_ref[part * filters:(part + 1) * filters, :]
+        grad_down = lax.dot_general(weight, cots, CONTRACT, preferred_element_type=F32)
+        weight = jnp.concatenate([weight, jnp.zeros((128 - filters, 128), BF16)], axis=0)
+        grad_over = lax.dot_general(cots, weight, CONTRACT, preferred_element_type=F32)
+        grad_down = grad_down.astype(BF16).astype(F32)
+        grad_over = grad_over.astype(BF16).astype(F32)
+        low_down = (LEAK_SLOPE * grad_down).astype(BF16).astype(F32)
+        low_over = (LEAK_SLOPE * grad_over).astype(BF16).astype(F32)
+        gap_down = grad_down - low_down
+        gap_over = grad_over - low_over
+        for sample in range(samples):
+            slot = sample * PC + part
+            gap = gap_down[:, sample:sample + 1]
+            low = low_down[:, sample:sample + 1]
+            across = gap_over[sample:sample + 1, :]
+            gradient += gap * sums_ref[slot, :filters, :256]
+            gradient += low * sums_ref[slot, filters:filters + 1, :256]
+            moment_out += gap * sums_ref[slot, :filters, 256:] * across
+            cross += low * (
+                across * sums_ref[slot, filters:filters + 1, 256:]
+                + (0.5 * cells) * low_over[sample:sample + 1, :]
             )
-            for j in range(3):
-                for k in range(3):
-                    row = plane * per_plane + channel * 9 + j * 3 + k
-                    shifted[pl.ds((2 - j) * rows + row, height, stride=rows), :] = moved[k]
-    for y in range(height):
-        stacked[top:, y * length:(y + 1) * length] = shifted[
-            (y + 1) * rows:(y + 2) * rows, :
-        ].astype(BF16)
-
-    column = lax.broadcasted_iota(jnp.int32, (filters * PC, samples), 1)
-    grad_all = jnp.sum(jnp.where(column == step, grads[...], 0.0), axis=1, keepdims=True)
-    low_all = (LEAK_SLOPE * grad_all).astype(BF16).astype(F32)
-    pooled = []
-    for part in range(PC):
-        lanes = slice(part * half, (part + 1) * half)
-        pre = jnp.dot(bands_ref[...], stacked[top:, lanes], preferred_element_type=F32)
-        active = jnp.where(pre > 0, pre, LEAK_SLOPE * pre)
-        total = active[0:filters]
-        for plane in range(1, planes):
-            total = total + active[plane * filters:(plane + 1) * filters]
-        pooled.append(jnp.sum(total, axis=1, keepdims=True))
-        grad = jnp.concatenate([grad_all[part * filters:(part + 1) * filters]] * planes, axis=0)
-        low = jnp.concatenate([low_all[part * filters:(part + 1) * filters]] * planes, axis=0)
-        stacked[0:top, lanes] = jnp.where(pre > 0, grad, low).astype(BF16)
-    pooled = jnp.concatenate(pooled, axis=0) * (1.0 / (planes * half))
-    spot = lax.broadcasted_iota(jnp.int32, pool_ref.shape, 1)
-    pool_ref[...] = jnp.where(spot == step, pooled, pool_ref[...])
-    acc[0:top + rows, :rows] += lax.dot_general(
-        stacked[...], stacked[top:, :], CONTRACT, preferred_element_type=F32
-    )
-    acc_out[...] += lax.dot_general(
-        stacked[0:top, :], stacked[0:top, :], CONTRACT, preferred_element_type=F32
-    )
-
-    @pl.when(step == pl.num_programs(0) - 1)
-    def _():
-        width = acc.shape[1]
-        wide = 3 * per_plane
-        moment_in = jnp.zeros((ROWS_IN, 128), F32)
-        gradient = jnp.zeros((filters, 128), F32)
-        moment_out = jnp.zeros((filters, 128), F32)
-        for plane in range(planes):
-            start = plane * per_plane
-            turn = (width - start) % width
-            block = acc[top + start:top + start + ROWS_IN, :]
-            moment_in += (pltpu.roll(block, turn, 1) if turn else block)[:, :128]
-            block = acc[plane * filters:(plane + 1) * filters, :]
-            gradient += (pltpu.roll(block, turn, 1) if turn else block)[:, :128]
-            block = acc_out[plane * filters:(plane + 1) * filters, :]
-            turn = (top - plane * filters) % top
-            moment_out += pltpu.roll(block, turn, 1) if turn else block
-        row_in = lax.broadcasted_iota(jnp.int32, (ROWS_IN, 128), 0)
-        lane_in = lax.broadcasted_iota(jnp.int32, (ROWS_IN, 128), 1)
-        moment_in = jnp.where(jnp.maximum(row_in, lane_in) < wide, moment_in, 0.0)
-        lane_out = lax.broadcasted_iota(jnp.int32, (filters, 128), 1)
-        gradient = jnp.where(lane_out < wide, gradient, 0.0)
-        packed = jnp.concatenate(
-            [
-                moment_in[:, :64],
-                moment_in[64:, 64:],
-                gradient[:, :64],
-                gradient[:, 64:],
-                moment_out[:, :64],
-            ],
-            axis=0,
-        )
-        groups = sent_ref.shape[0]
-        share = packed.shape[0] // groups
-        sent_ref[:, 0:share, :] = in_halves(packed).reshape(groups, share, 128)
-        feats = jnp.transpose(pool_ref[...])[:samples]
-        own = own_ref[...].astype(F32)
-        own = jnp.concatenate([own[:, :64], own[:, 64:], jnp.zeros((samples - 2, 64), F32)], axis=0)
-        both = jnp.concatenate([feats, own], axis=1).astype(BF16)
-        sent_ref[:, share:, :] = jnp.broadcast_to(both[None], (groups, samples, 128))
+    lane = lanes_of(cross.shape)
+    cross = jnp.where(lane < filters, cross, 0.0)
+    tall = jnp.concatenate([cross, jnp.zeros((128 - filters, 128), F32)], axis=0)
+    moment_out = jnp.where(lane < filters, moment_out, 0.0)
+    moment_out += cross + jnp.transpose(tall)[:filters]
+
+    blocks = jnp.zeros((part_rows, 512), F32)
+    for plane in range(planes):
+        start = plane * inner
+        blocks += turned(gram_ref[start:start + part_rows, :], start)
+    first = compact(blocks[:, :256])
+    lane = lanes_of(first.shape)
+    second = first + jnp.where(lane < part_rows, blocks[:, 256:384], 0.0)
+    third = second - jnp.where(lane < part_rows, blocks[:, 384:], 0.0)
+    turned_up[...] = jnp.zeros_like(turned_up)
+    turned_up[0:part_rows, :] = first
+    turned_up[...] = jnp.transpose(turned_up[...])
+    held[...] = jnp.zeros_like(held)
+    held[0:part_rows, :] = first
+    above = turned_up[part_rows:2 * part_rows, :]
+    row = jnp.where(lane < part_rows, above, pltpu.roll(second, part_rows, 1))
+    held[part_rows:2 * part_rows, :] = jnp.where(lane < wide, row, 0.0)
+    row = jnp.where(
+        lane < 2 * part_rows,
+        pltpu.roll(above, part_rows, 1),
+        pltpu.roll(third, 2 * part_rows, 1),
+    )
+    row = jnp.where(lane < part_rows, turned_up[2 * part_rows:wide, :], row)
+    held[2 * part_rows:wide, :] = jnp.where(lane < wide, row, 0.0)
+    moment_in = held[...]
+    gradient = compact(gradient)
+    packed = jnp.concatenate(
+        [
+            moment_in[:, :64],
+            moment_in[64:, 64:],
+            gradient[:, :64],
+            gradient[:, 64:],
+            moment_out[:, :64],
+        ],
+        axis=0,
+    )
+    groups = sent_ref.shape[0]
+    share = packed.shape[0] // groups
+    sent_ref[:, 0:share, :] = in_halves(packed).reshape(groups, share, 128)
+    feats = jnp.transpose(pool_ref[...])[:samples]
+    own = own_ref[...].astype(F32)
+    own = jnp.concatenate([own[:, :64], own[:, 64:], jnp.zeros((samples - 2, 64), F32)], axis=0)
+    both = jnp.concatenate([feats, own], axis=1).astype(BF16)
+    sent_ref[:, share:, :] = jnp.broadcast_to(both[None], (groups, samples, 128))
+
+
+def conv_moments(sizes, sums, weight, cot_group, own, groups):
+    samples = sizes[-1]
+    rows = 256 // groups + samples
+    vmem = pl.BlockSpec(memory_space=pltpu.VMEM)
+    return pl.pallas_call(
+        functools.partial(moments_body, sizes),
+        in_specs=[vmem] * 6,
+        out_specs=vmem,
+        out_shape=jax.ShapeDtypeStruct((groups, rows, 128), BF16),
+        scratch_shapes=[pltpu.VMEM((ROWS_IN, 128), F32), pltpu.VMEM((128, 128), F32)],
+        compiler_params=pltpu.CompilerParams(vmem_limit_bytes=16 * 1024 * 1024),
+    )(*sums, weight, cot_group, own)
 
 
 def in_halves(x):
@@ -157,39 +287,6 @@
 def from_halves(x):
     wide = x.astype(F32)
     return wide[..., :64] + wide[..., 64:]
-
-
-def conv_moments(volume, before, after, bands, weight, cot_group, own, filters, groups):
-    samples, channels, planes, height, length = volume.shape
-    per_plane = channels * 9
-    rows = (planes + 2) * per_plane
-    top = planes * filters
-    sizes = (channels, planes, height, length, filters, samples)
-    whole = lambda shape: pl.BlockSpec(shape, lambda b: (0,) * len(shape))
-    return pl.pallas_call(
-        functools.partial(conv_kernel_body, sizes),
-        grid=(samples,),
-        in_specs=[
-            pl.BlockSpec((1, channels, planes, height, length), lambda b: (b, 0, 0, 0, 0)),
-            pl.BlockSpec((1, channels, 1, height, length), lambda b: (b, 0, 0, 0, 0)),
-            pl.BlockSpec((1, channels, 1, height, length), lambda b: (b, 0, 0, 0, 0)),
-            whole(bands.shape),
-            whole(weight.shape),
-            whole(cot_group.shape),
-            whole(own.shape),
-        ],
-        out_specs=whole((groups, 256 // groups + samples, 128)),
-        out_shape=jax.ShapeDtypeStruct((groups, 256 // groups + samples, 128), BF16),
-        scratch_shapes=[
-            pltpu.VMEM((filters * PC, 128), F32),
-            pltpu.VMEM(((height + 2) * rows, length), F32),
-            pltpu.VMEM((top + rows, height * length), BF16),
-            pltpu.VMEM((filters * PC, samples), F32),
-            pltpu.VMEM((top + rows + 8, 256), F32),
-            pltpu.VMEM((top, top), F32),
-        ],
-        compiler_params=pltpu.CompilerParams(vmem_limit_bytes=48 * 1024 * 1024),
-    )(volume, before, after, bands, weight, cot_group, own)
 
 
 def middle_body(got_ref, sent_ref):
@@ -431,8 +528,8 @@
 def column_order(channels):
     row = lax.broadcasted_iota(jnp.int32, (128, 128), 0)
     column = lax.broadcasted_iota(jnp.int32, (128, 128), 1)
-    channel, rest = column // 27, column % 27
-    source = (rest // 9) * (9 * channels) + channel * 9 + rest % 9
+    channel, i, j, k = column // 27, column // 9 % 3, column // 3 % 3, column % 3
+    source = ((j * 3 + i) * channels + channel) * 3 + k
     return jnp.where(jnp.logical_and(row == source, column < 27 * channels), 1.0, 0.0)
 
 
@@ -446,27 +543,28 @@
 
     up = [(i, i + 1) for i in range(spaces - 1)]
     down = [(j, i) for i, j in up]
-    cot_group = gather_from(cotangent[0], SPACE, spaces)
     before = lax.ppermute(volume[:, :, planes - 1:], SPACE, up)
     after = lax.ppermute(volume[:, :, :1], SPACE, down)
-
-    mixed = conv_kernel.reshape(filters, channels, 3, 9).transpose(0, 2, 1, 3)
-    mixed = mixed.reshape(filters, patch_rows)
-    spare = (planes + 2) * channels * 9 - patch_rows
+    cot_group = gather_from(cotangent[0], SPACE, spaces)
+
+    mixed = conv_kernel.reshape(filters, channels, 3, 3, 3).transpose(0, 3, 2, 1, 4)
+    mixed = mixed.reshape(filters, 3, channels * 9)
+    inner = channels * 3
+    spare = (planes - 1) * inner
     bands = jnp.concatenate(
         [
-            jnp.pad(mixed, ((0, 0), (p * channels * 9, spare - p * channels * 9)))
+            jnp.pad(mixed, ((0, 0), (0, 0), (p * inner, spare - p * inner)))
             for p in range(planes)
         ],
         axis=0,
-    )
+    ).reshape(planes * filters, -1)
     place = lax.axis_index(SPACE)
     weight = lax.dynamic_slice_in_dim(dense_weight, place * slab, slab, 0)
     weight = weight.reshape(filters, PC, -1).transpose(1, 0, 2).reshape(slab, -1)
 
-    sent = conv_moments(
-        volume, before, after, bands, weight, cot_group, cotangent, filters, column
-    )
+    sums = conv_sums(volume, before, after, bands, filters)
+    sizes = (channels, planes, planes * height * length // PC, filters, samples)
+    sent = conv_moments(sizes, sums, weight, cot_group, cotangent, column)
     peers = spaces * groups // column
     got = exchange(middle(exchange(sent, COLUMN), peers), PLANE)
     reduced = exchange(spread(got, column), COLUMN)

time: 80.4 us -> 79.9 us (level)
  blocking collectives: 19.4 us -> 0 us
  starting transfers between devices: 20.7 us -> 31.9 us
  waiting for transfers between devices: 16.8 us -> 25.1 us
    all_to_all x1 -> x0, blocking collectives: 19.4 us -> none  [exchange(): return lax.all_to_all(x, axes, split_axis=0, concat_axis=0, tiled=True)]
    all_to_all x3 -> x4, starting transfers between devices: 15.4 us -> 26.5 us  [exchange(): return lax.all_to_all(x, axes, split_axis=0, concat_axis=0, tiled=True)]
    all_to_all x3 -> x4, waiting for transfers between devices: 16.8 us -> 25.1 us  [exchange(): return lax.all_to_all(x, axes, split_axis=0, concat_axis=0, tiled=True)]
    pallas_call x1 -> x2, Pallas kernels: 10.4 us -> 9.65 us  [the longest x1 8.19 us: conv_sums(): pl.pallas_call(functools.partial(conv_kernel_body, sizes), grid=(samples...]
  transfers between devices with their start and end apart: 5 -> 6, of which waited for: 3 -> 4; matrix products, arithmetic and copies ran while one was open for 1% -> 1% of each run, Pallas kernels for 6% -> 6%
where the time goes in v6:
time: 79.9 us; the launch traced here: 79.4 us
  starting transfers between devices  31.9 us (40%)
  waiting for transfers between devices  25.1 us (31%)
  Pallas kernels  19.4 us (24%)
  local copies, waits for them, and re-layouts  2.01 us (3%)
  between operations  0.83 us (1%)
    all_to_all x4, starting transfers between devices, exchange(): return lax.all_to_all(x, axes, split_axis=0, concat_axis=0, tiled=True)  26.5 us
    all_to_all x4, waiting for transfers between devices, exchange(): return lax.all_to_all(x, axes, split_axis=0, concat_axis=0, tiled=True)  25.1 us
    pallas_call x1, Pallas kernels, conv_sums(): pl.pallas_call(functools.partial(conv_kernel_body, sizes), grid=(samples...  8.19 us
    pallas_call x1, Pallas kernels, dense_delta(): pl.pallas_call(functools.partial(dense_kernel_body, groups, spaces), in_s...  4.46 us
    ppermute x1, starting transfers between devices, on_device(): before = lax.ppermute(volume[:, :, planes - 1:], SPACE, up)  4.03 us
    pallas_call x1, Pallas kernels, final_steps(): pl.pallas_call(functools.partial(final_kernel_body, filters, patch_rows,...  3.58 us
  transfers between devices with their start and end apart: 6, of which 4 were waited for; matrix products, arithmetic and copies ran while one was open for 1% of the time, Pallas kernels for 6%

profile of v6, /device:TPU:1, one launch (start us, length us, event | category | flops | bytes accessed | tf_op | source)
XLA Modules:
  0.0 79.4 jit_solution(2175901835877647732)
XLA Ops:
  0.6 0.0 copy-start
  0.6 0.0 copy-start.1
  0.7 1.1 %fusion.25 = (bf16[8,4,1,16,128]{4,3,2,1,0:T(8,128)(2,1)S(1)}, bf16[8,4,1,16,128]{4,3,2,1,0:T(8,128)(2,1)S(1)}) fusion(bf16[8,4,4,16,128]{4,3,2,1,0:T(8,128)(2,1)} %vol_ref.1), kind=kLoop, calls=%fused_computation.54 | loop fusion | bytes 524288 | tf_op jit(solution)/shard_map/slice | solution.py:547
  1.7 4.0 %collective-permute-start = (bf16[8,4,1,16,128]{4,3,2,1,0:T(8,128)(2,1)S(1)}, bf16[8,4,1,16,128]{4,3,2,1,0:T(8,128)(2,1)S(1)}, u32[]{:S(2)}, u32[]{:S(2)}) collective-permute-start(bf16[8,4,1,16,128]{4,3,2,1,0:T(8,128)(2,1)S(1)} %get-tuple-element.17), channel_id=1, source_target_pairs={{0,1},{1,2},{2,3},{3,4},{4,5},{5,6},{6,7},{8,9},{9,10},{10,11},{11... | collective-permute-start | bytes 393224 | tf_op jit(solution)/shard_map/ppermute | solution.py:546
  5.8 0.0 copy-start.2
  5.8 0.0 copy-start.3
  5.8 1.3 %collective-permute-start.1 = (bf16[8,4,1,16,128]{4,3,2,1,0:T(8,128)(2,1)S(1)}, bf16[8,4,1,16,128]{4,3,2,1,0:T(8,128)(2,1)S(1)}, u32[]{:S(2)}, u32[]{:S(2)}) collective-permute-start(bf16[8,4,1,16,128]{4,3,2,1,0:T(8,128)(2,1)S(1)} %get-tuple-element.16), channel_id=1, source_target_pairs={{1,0},{2,1},{3,2},{4,3},{5,4},{6,5},{7,6},{9,8},{10,9},{11,10},{12... | collective-permute-start | bytes 393224 | tf_op jit(solution)/shard_map/ppermute | solution.py:547
  7.1 0.0 copy-done.2
  7.1 0.6 broadcast_in_dim.13
  7.7 5.9 %all-to-all-start = ((bf16[8,1,128]{2,1,0:T(2,128)(2,1)}), bf16[8,1,128]{2,1,0:T(2,128)(2,1)S(1)}, u32[]{:S(2)}, u32[]{:S(2)}) async-start(bf16[8,1,128]{2,1,0:T(2,128)(2,1)} %broadcast_in_dim.13), calls=%async_computation | async-start | bytes 8192 | tf_op jit(solution)/shard_map/all_to_all | solution.py:30
  13.6 0.0 copy-done.3
  13.6 0.1 copy.15
  13.8 0.1 fusion.22
  13.9 0.0 copy-done
  14.0 0.1 copy.17.bands_ref
  14.1 4.5 %all-to-all-done = bf16[8,1,128]{2,1,0:T(2,128)(2,1)S(1)} async-done(((bf16[8,1,128]{2,1,0:T(2,128)(2,1)}), bf16[8,1,128]{2,1,0:T(2,128)(2,1)S(1)}, u32[]{:S(2)}, u32[]{:S(2)}) %all-to-all-start) | async-done | bytes 2080 | tf_op jit(solution)/shard_map/all_to_all | solution.py:30
  18.5 0.0 collective-permute-done.before_ref
  18.5 0.0 collective-permute-done.1.after_ref
  18.6 0.0 copy-done.1
  18.6 8.2 %shard_map.62 = (f32[64,128]{1,0:T(8,128)S(1)}, f32[16,40,384]{2,1,0:T(8,128)S(1)}, f32[72,512]{1,0:T(8,128)S(1)}) custom-call(bf16[8,4,4,16,128]{4,3,2,1,0:T(8,128)(2,1)S(1)} %copy-done.1, bf16[8,4,1,16,128]{4,3,2,1,0:T(8,128)(2,1)S(1)} %collective-permute-done.before_ref, bf16[8,4,1,16,128]{4,3,2,1,0:T(8,128)(2,1)S(1)} %collective-permute-done.1.after_ref, ...), custom_call_target="tpu_custom_call" | custom-call | tf_op jit(solution)/shard_map/pallas_call | solution.py:149
  26.8 1.5 %shard_map.63 = bf16[16,24,128]{2,1,0:T(8,128)(2,1)} custom-call(f32[64,128]{1,0:T(8,128)S(1)} %get-tuple-element.9.pool_ref, f32[16,40,384]{2,1,0:T(8,128)S(1)} %get-tuple-element.10.sums_ref, f32[72,512]{1,0:T(8,128)S(1)} %get-tuple-element.11.gram_ref, bf16[64,128]{1,0:T(8,128)(2,1)S(1)} %bitcast.16, bf16[8,128]{1,0:T(8,128)(2,1)S(1)} %bitcast.17, ...), custom_call_target="tpu_custom_call" | custom-call | tf_op jit(solution)/shard_map/pallas_call | solution.py:271
  28.2 11.1 %all-to-all-start.1 = ((bf16[16,24,128]{2,1,0:T(8,128)(2,1)}), bf16[16,24,128]{2,1,0:T(8,128)(2,1)S(1)}, u32[]{:S(2)}, u32[]{:S(2)}) async-start(bf16[16,24,128]{2,1,0:T(8,128)(2,1)} %shard_map.63), calls=%async_computation.1 | async-start | bytes 196608 | tf_op jit(solution)/shard_map/all_to_all | solution.py:30
  39.4 8.4 %all-to-all-done.1.got_ref = bf16[16,24,128]{2,1,0:T(8,128)(2,1)S(1)} async-done(((bf16[16,24,128]{2,1,0:T(8,128)(2,1)}), bf16[16,24,128]{2,1,0:T(8,128)(2,1)S(1)}, u32[]{:S(2)}, u32[]{:S(2)}) %all-to-all-start.1) | async-done | bytes 98336 | tf_op jit(solution)/shard_map/all_to_all | solution.py:30
  47.8 0.9 %shard_map.64 = bf16[16,96,128]{2,1,0:T(8,128)(2,1)} custom-call(bf16[16,24,128]{2,1,0:T(8,128)(2,1)S(1)} %all-to-all-done.1.got_ref), custom_call_target="tpu_custom_call" | custom-call | tf_op jit(solution)/shard_map/pallas_call | solution.py:314
  48.7 4.4 %all-to-all-start.2 = ((bf16[16,96,128]{2,1,0:T(8,128)(2,1)}), bf16[16,96,128]{2,1,0:T(8,128)(2,1)S(1)}, u32[]{:S(2)}, u32[]{:S(2)}) async-start(bf16[16,96,128]{2,1,0:T(8,128)(2,1)} %shard_map.64), calls=%async_computation.2 | async-start | bytes 786432 | tf_op jit(solution)/shard_map/all_to_all | solution.py:30
  53.2 8.9 %all-to-all-done.2.got_ref = bf16[16,96,128]{2,1,0:T(8,128)(2,1)S(1)} async-done(((bf16[16,96,128]{2,1,0:T(8,128)(2,1)}), bf16[16,96,128]{2,1,0:T(8,128)(2,1)S(1)}, u32[]{:S(2)}, u32[]{:S(2)}) %all-to-all-start.2) | async-done | bytes 393248 | tf_op jit(solution)/shard_map/all_to_all | solution.py:30
  62.2 0.8 %shard_map.65 = bf16[16,16,128]{2,1,0:T(8,128)(2,1)} custom-call(bf16[16,96,128]{2,1,0:T(8,128)(2,1)S(1)} %all-to-all-done.2.got_ref), custom_call_target="tpu_custom_call" | custom-call | tf_op jit(solution)/shard_map/pallas_call | solution.py:331
  63.0 5.1 %all-to-all-start.3 = ((bf16[16,16,128]{2,1,0:T(8,128)(2,1)}), bf16[16,16,128]{2,1,0:T(8,128)(2,1)S(1)}, u32[]{:S(2)}, u32[]{:S(2)}) async-start(bf16[16,16,128]{2,1,0:T(8,128)(2,1)} %shard_map.65), calls=%async_computation.3 | async-start | bytes 131072 | tf_op jit(solution)/shard_map/all_to_all | solution.py:30
  68.1 4.5 %shard_map.66 = (f32[128,64]{1,0:T(8,128)S(1)}, f32[1,1]{1,0:T(1,128)}) custom-call(s32[1]{0:T(128)} %bitcast.6.place_ref, bf16[16,96,128]{2,1,0:T(8,128)(2,1)S(1)} %all-to-all-done.2.got_ref), custom_call_target="tpu_custom_call" | custom-call | tf_op jit(solution)/shard_map/pallas_call | solution.py:468
  72.5 3.3 %all-to-all-done.3.got_ref = bf16[16,16,128]{2,1,0:T(8,128)(2,1)S(1)} async-done(((bf16[16,16,128]{2,1,0:T(8,128)(2,1)}), bf16[16,16,128]{2,1,0:T(8,128)(2,1)S(1)}, u32[]{:S(2)}, u32[]{:S(2)}) %all-to-all-start.3) | async-done | bytes 65568 | tf_op jit(solution)/shard_map/all_to_all | solution.py:30
  75.9 3.6 %shard_map.67 = (f32[32,108]{1,0:T(8,128)}, f32[4,64]{1,0:T(4,128)}) custom-call(bf16[16,16,128]{2,1,0:T(8,128)(2,1)S(1)} %all-to-all-done.3.got_ref, f32[4,64]{1,0:T(4,128)S(1)} %constant_dynamic-slice_fusion.dense_ref, f32[1,1]{1,0:T(1,128)} %get-tuple-element.13.total_ref, f32[128,128]{1,0:T(8,128)S(1)} %fusion.20.order_ref), custom_call_target="tpu_custom_call" | custom-call | tf_op jit(solution)/shard_map/pallas_call | solution.py:516
  (15 shorter events, 0.2 us)
Async XLA Ops:
  0.6 13.3 %copy-start = (bf16[512,128]{1,0:T(8,128)(2,1)S(1)}, bf16[512,128]{1,0:T(8,128)(2,1)}, u32[]{:S(2)}) copy-start(bf16[512,128]{1,0:T(8,128)(2,1)} %param.6) | copy-start | bytes 393220
  0.6 17.9 %copy-start.1 = (bf16[8,4,4,16,128]{4,3,2,1,0:T(8,128)(2,1)S(1)}, bf16[8,4,4,16,128]{4,3,2,1,0:T(8,128)(2,1)}, u32[]{:S(2)}) copy-start(bf16[8,4,4,16,128]{4,3,2,1,0:T(8,128)(2,1)} %vol_ref.1) | copy-start | bytes 1572868
  1.7 16.8 %collective-permute-start = (bf16[8,4,1,16,128]{4,3,2,1,0:T(8,128)(2,1)S(1)}, bf16[8,4,1,16,128]{4,3,2,1,0:T(8,128)(2,1)S(1)}, u32[]{:S(2)}, u32[]{:S(2)}) collective-permute-start(bf16[8,4,1,16,128]{4,3,2,1,0:T(8,128)(2,1)S(1)} %get-tuple-element.17), channel_id=1, source_target_pairs={{0,1},{1,2},{2,3},{3,4},{4,5},{5,6},{6,7},{8,9},{9,10},{10,11},{11... | collective-permute-start | bytes 393224 | tf_op jit(solution)/shard_map/ppermute | solution.py:546
  5.8 1.3 %copy-start.2 = (bf16[1,128]{1,0:T(2,128)(2,1)S(1)}, bf16[1,128]{1,0:T(2,128)(2,1)}, u32[]{:S(2)}) copy-start(bf16[1,128]{1,0:T(2,128)(2,1)} %own_ref.1) | copy-start | bytes 772
  5.8 7.8 %copy-start.3 = (bf16[32,108]{1,0:T(8,128)(2,1)S(1)}, bf16[32,108]{1,0:T(8,128)(2,1)}, u32[]{:S(2)}) copy-start(bf16[32,108]{1,0:T(8,128)(2,1)} %param.5) | copy-start | bytes 20740
  5.8 12.8 %collective-permute-start.1 = (bf16[8,4,1,16,128]{4,3,2,1,0:T(8,128)(2,1)S(1)}, bf16[8,4,1,16,128]{4,3,2,1,0:T(8,128)(2,1)S(1)}, u32[]{:S(2)}, u32[]{:S(2)}) collective-permute-start(bf16[8,4,1,16,128]{4,3,2,1,0:T(8,128)(2,1)S(1)} %get-tuple-element.16), channel_id=1, source_target_pairs={{1,0},{2,1},{3,2},{4,3},{5,4},{6,5},{7,6},{9,8},{10,9},{11,10},{12... | collective-permute-start | bytes 393224 | tf_op jit(solution)/shard_map/ppermute | solution.py:547
  7.7 10.9 %all-to-all-start = ((bf16[8,1,128]{2,1,0:T(2,128)(2,1)}), bf16[8,1,128]{2,1,0:T(2,128)(2,1)S(1)}, u32[]{:S(2)}, u32[]{:S(2)}) async-start(bf16[8,1,128]{2,1,0:T(2,128)(2,1)} %broadcast_in_dim.13), calls=%async_computation | async-start | bytes 8192 | tf_op jit(solution)/shard_map/all_to_all | solution.py:30
  28.2 19.6 %all-to-all-start.1 = ((bf16[16,24,128]{2,1,0:T(8,128)(2,1)}), bf16[16,24,128]{2,1,0:T(8,128)(2,1)S(1)}, u32[]{:S(2)}, u32[]{:S(2)}) async-start(bf16[16,24,128]{2,1,0:T(8,128)(2,1)} %shard_map.63), calls=%async_computation.1 | async-start | bytes 196608 | tf_op jit(solution)/shard_map/all_to_all | solution.py:30
  48.7 13.4 %all-to-all-start.2 = ((bf16[16,96,128]{2,1,0:T(8,128)(2,1)}), bf16[16,96,128]{2,1,0:T(8,128)(2,1)S(1)}, u32[]{:S(2)}, u32[]{:S(2)}) async-start(bf16[16,96,128]{2,1,0:T(8,128)(2,1)} %shard_map.64), calls=%async_computation.2 | async-start | bytes 786432 | tf_op jit(solution)/shard_map/all_to_all | solution.py:30
  63.0 12.9 %all-to-all-start.3 = ((bf16[16,16,128]{2,1,0:T(8,128)(2,1)}), bf16[16,16,128]{2,1,0:T(8,128)(2,1)S(1)}, u32[]{:S(2)}, u32[]{:S(2)}) async-start(bf16[16,16,128]{2,1,0:T(8,128)(2,1)} %shard_map.65), calls=%async_computation.3 | async-start | bytes 131072 | tf_op jit(solution)/shard_map/all_to_all | solution.py:30

commit v7 on v6

--- a/solution.py
+++ b/solution.py
@@ -289,35 +289,36 @@
     return wide[..., :64] + wide[..., 64:]
 
 
-def middle_body(got_ref, sent_ref):
-    groups = got_ref.shape[0]
-    pairs = groups // 2
-    rows = pairs * 8
-    share = got_ref.shape[1] - 8
-    chunk = jnp.sum(from_halves(got_ref[:, 0:share, :]), axis=0)
-    wide = got_ref[:, share:, :].astype(F32)
+def middle_body(core_ref, got_ref, sent_ref):
+    depth, cores, rows, _ = got_ref.shape
+    share = rows - 8
+    chunk = jnp.sum(from_halves(got_ref[:, 0, 0:share, :]), axis=0)
+    for core in range(1, cores):
+        chunk += jnp.sum(from_halves(got_ref[:, core, 0:share, :]), axis=0)
+    wide = got_ref[:, core_ref[0], share:, :].astype(F32)
+    pairs = depth // 2
     feats = wide[:, :, :64]
-    feats = jnp.concatenate([feats[:pairs], feats[pairs:]], axis=2).reshape(rows, 128)
+    feats = jnp.concatenate([feats[:pairs], feats[pairs:]], axis=2).reshape(pairs * 8, 128)
     cots = jnp.concatenate([wide[:, 0, 64:], wide[:, 1, 64:]], axis=1)
     feats = feats.astype(BF16)
     cots = cots.astype(BF16)
     chunk = in_halves(chunk)
     for peer in range(sent_ref.shape[0]):
-        sent_ref[peer, 0:rows, :] = feats
-        sent_ref[peer, rows:rows + groups, :] = cots
-        sent_ref[peer, rows + groups:, :] = chunk
-
-
-def middle(got, peers):
-    groups, rows, lanes = got.shape
+        sent_ref[peer, 0:share, :] = chunk
+        sent_ref[peer, share:share + pairs * 8, :] = feats
+        sent_ref[peer, share + pairs * 8:, :] = cots
+
+
+def middle(core, got, peers):
+    depth, _, rows, lanes = got.shape
     vmem = pl.BlockSpec(memory_space=pltpu.VMEM)
     return pl.pallas_call(
         middle_body,
-        in_specs=[vmem],
+        in_specs=[pl.BlockSpec(memory_space=pltpu.SMEM), vmem],
         out_specs=vmem,
-        out_shape=jax.ShapeDtypeStruct((peers, groups * 5 + rows - 8, lanes), BF16),
+        out_shape=jax.ShapeDtypeStruct((peers, rows - 8 + depth * 5, lanes), BF16),
         compiler_params=pltpu.CompilerParams(vmem_limit_bytes=8 * 1024 * 1024),
-    )(got)
+    )(core, got)
 
 
 def spread_body(got_ref, sent_ref):
@@ -326,12 +327,12 @@
 
 
 def spread(got, groups):
-    peers, rows, lanes = got.shape
+    peers, _, lanes = got.shape
     share = 256 // groups
     return pl.pallas_call(
         spread_body,
         grid=(1,),
-        in_specs=[pl.BlockSpec((peers, share, lanes), lambda i: (0, rows // share - 1, 0))],
+        in_specs=[pl.BlockSpec((peers, share, lanes), lambda i: (0, 0, 0))],
         out_specs=pl.BlockSpec((groups, share, lanes), lambda i: (0, 0, 0)),
         out_shape=jax.ShapeDtypeStruct((groups, share, lanes), BF16),
         compiler_params=pltpu.CompilerParams(vmem_limit_bytes=8 * 1024 * 1024),
@@ -409,18 +410,27 @@
     return start - factor / bound, bound
 
 
-def dense_kernel_body(groups, spaces, place_ref, got_ref, delta_ref, total_ref, whole, cots):
-    parts = got_ref.shape[0] // spaces
+def dense_kernel_body(
+    depth, spaces, place_ref, own_ref, other_ref, delta_ref, whole, cots,
+):
+    parts = own_ref.shape[0] // spaces
     width = 64
-    block = groups * 8
-    count = parts * block
+    block = depth * 8
     half = block // 2
+    share = own_ref.shape[1] - other_ref.shape[1]
+    count = parts * 2 * block
+    lower = place_ref[1] == 0
+
+    def both_cores(index):
+        own = own_ref[index].astype(F32)[share:]
+        other = other_ref[index].astype(F32)
+        return jnp.where(lower, own, other), jnp.where(lower, other, own)
 
     def slab_of(index):
         pieces = []
         for part in range(parts):
-            both = got_ref[part * spaces + index].astype(F32)[:half]
-            pieces += [both[:, :width], both[:, width:]]
+            for rows in both_cores(part * spaces + index):
+                pieces += [rows[:half, :width], rows[:half, width:]]
         return jnp.concatenate(pieces, axis=0)
 
     for slab in range(0, spaces, 2):
@@ -428,9 +438,9 @@
         whole[:, slab * width:(slab + 2) * width] = pair.astype(BF16)
     for part in range(parts):
         for slab in range(spaces):
-            cots[pl.ds(part * block + slab, groups, stride=spaces), :] = got_ref[
-                part * spaces + slab, half:half + groups, :
-            ].astype(F32)
+            for core, rows in enumerate(both_cores(part * spaces + slab)):
+                first = (part * 2 + core) * block + slab
+                cots[pl.ds(first, depth, stride=spaces), :] = rows[half:]
     cot_wide = cots[...]
     cot = cot_wide.astype(BF16)
     feats = whole[...]
@@ -446,7 +456,7 @@
     left = jnp.where(eye, 1.0 - damping / bound, 0.0) - gram / bound
     right, bound_out = residual(dense_out, dense_out.shape[0])
     held = two_sided(left, cot_wide * (scale / bound / bound_out), right)
-    total_ref[...] = scalar_sum(held * split_dot(gram, cot_wide))
+    total = scalar_sum(held * split_dot(gram, cot_wide))
     mine = slab_of(place_ref[0])
     source = lax.broadcasted_iota(jnp.int32, (width, width), 0)
     target = lax.broadcasted_iota(jnp.int32, (width, width), 1)
@@ -454,7 +464,9 @@
     pick = jnp.where(source == spot, 1.0, 0.0).astype(BF16)
     mine = jnp.dot(mine.astype(BF16), pick, preferred_element_type=F32).astype(BF16)
     high, low = parts_of(held)
-    delta_ref[...] = lax.dot_general(
+    outputs = cot_wide.shape[1]
+    delta_ref[outputs:, :] = jnp.broadcast_to(total, (8, width))
+    delta_ref[0:outputs, :] = lax.dot_general(
         jnp.concatenate([high, low], axis=0),
         jnp.concatenate([mine, mine], axis=0),
         LEADING,
@@ -462,27 +474,24 @@
     )
 
 
-def dense_delta(place, got, groups, spaces, outputs):
-    count = groups * 8 * (got.shape[0] // spaces)
+def dense_delta(place, own, other, depth, spaces, outputs):
+    count = depth * 16 * (own.shape[0] // spaces)
     vmem = pl.BlockSpec(memory_space=pltpu.VMEM)
     return pl.pallas_call(
-        functools.partial(dense_kernel_body, groups, spaces),
-        in_specs=[pl.BlockSpec(memory_space=pltpu.SMEM), vmem],
-        out_specs=[vmem, vmem],
-        out_shape=[
-            jax.ShapeDtypeStruct((outputs, 64), F32),
-            jax.ShapeDtypeStruct((1, 1), F32),
-        ],
+        functools.partial(dense_kernel_body, depth, spaces),
+        in_specs=[pl.BlockSpec(memory_space=pltpu.SMEM), vmem, vmem],
+        out_specs=vmem,
+        out_shape=jax.ShapeDtypeStruct((outputs + 8, 64), F32),
         scratch_shapes=[
             pltpu.VMEM((count, spaces * 64), BF16),
             pltpu.VMEM((count, outputs), F32),
         ],
         compiler_params=pltpu.CompilerParams(vmem_limit_bytes=48 * 1024 * 1024),
-    )(place, got)
+    )(place, own, other)
 
 
 def final_kernel_body(
-    filters, patch_rows, cells, got_ref, dense_ref, total_ref, order_ref,
+    filters, patch_rows, cells, place_ref, got_ref, delta_ref, order_ref,
     step_conv_ref, step_dense_ref,
 ):
     scale = 1.0 / cells
@@ -504,25 +513,28 @@
     right, bound_in = residual(conv_in, patch_rows)
     left, bound_out = residual(conv_out, filters)
     held = two_sided(left[0:filters], conv_grad / bound_in / bound_out, right)
-    total = scalar_sum(held * conv_grad) + total_ref[...]
+    total = scalar_sum(held * conv_grad) + delta_ref[delta_ref.shape[0] - 8:, 0:1][0:1]
     scaling = jnp.minimum(1.0, jnp.sqrt(KL_BOUND / (LEARN_RATE * LEARN_RATE * total)))
     moved = split_dot(held, order_ref[...])
     step_conv_ref[...] = scaling * moved[:, 0:patch_rows]
-    step_dense_ref[...] = scaling * dense_ref[...]
-
-
-def final_steps(moments, dense_block, dense_total, order, filters, patch_rows, cells):
+    first = place_ref[2] // 2 * 8
+    window = delta_ref[pl.ds(pl.multiple_of(first, 8), 8), :]
+    mine = jnp.where(place_ref[2] % 2 == 0, window[0:4], window[4:8])
+    step_dense_ref[...] = scaling * mine
+
+
+def final_steps(place, moments, delta, order, filters, patch_rows, cells):
     vmem = pl.BlockSpec(memory_space=pltpu.VMEM)
     return pl.pallas_call(
         functools.partial(final_kernel_body, filters, patch_rows, cells),
-        in_specs=[vmem] * 4,
+        in_specs=[pl.BlockSpec(memory_space=pltpu.SMEM)] + [vmem] * 3,
         out_specs=[vmem] * 2,
         out_shape=[
             jax.ShapeDtypeStruct((filters, patch_rows), F32),
-            jax.ShapeDtypeStruct(dense_block.shape, F32),
+            jax.ShapeDtypeStruct((4, delta.shape[1]), F32),
         ],
         compiler_params=pltpu.CompilerParams(vmem_limit_bytes=32 * 1024 * 1024),
-    )(moments, dense_block, dense_total, order)
+    )(place, moments, delta, order)
 
 
 def column_order(channels):
@@ -566,16 +578,16 @@
     sizes = (channels, planes, planes * height * length // PC, filters, samples)
     sent = conv_moments(sizes, sums, weight, cot_group, cotangent, column)
     peers = spaces * groups // column
-    got = exchange(middle(exchange(sent, COLUMN), peers), PLANE)
+    core = lax.axis_index("core")
+    got = exchange(sent, COLUMN).reshape(column // 2, 2, -1, 128)
+    got = exchange(middle(core.reshape(1), got, peers), PLANE)
     reduced = exchange(spread(got, column), COLUMN)
-    delta, dense_total = dense_delta(
-        place.reshape(1), got, column, spaces, cotangent.shape[1]
-    )
-    share = cotangent.shape[1] // groups
-    dense_block = lax.dynamic_slice_in_dim(delta, lax.axis_index(DP) * share, share, 0)
+    other = lax.ppermute(got[:, 256 // column:], "core", [(0, 1), (1, 0)])
+    places = jnp.stack([place, core, lax.axis_index(DP)])
+    delta = dense_delta(places, got, other, column // 2, spaces, cotangent.shape[1])
     cells = samples * groups * planes * spaces * height * length
     step_conv, step_dense = final_steps(
-        reduced, dense_block, dense_total, column_order(channels), filters, patch_rows, cells
+        places, reduced, delta, column_order(channels), filters, patch_rows, cells
     )
     return step_conv, step_dense.T
 

time: 79.9 us -> 78 us (0.976)
  waiting for transfers between devices: 25.1 us -> 22.5 us
    all_to_all x4, waiting for transfers between devices: 25.1 us -> 21.5 us  [exchange(): return lax.all_to_all(x, axes, split_axis=0, concat_axis=0, tiled=True)]
    ppermute x0 -> x1, waiting for transfers between devices: none -> 1.05 us  [on_device(): other = lax.ppermute(got[:, 256 // column:], 'core', [(0, 1), (1, 0)])]
  transfers between devices with their start and end apart: 6 -> 7, of which waited for: 4 -> 5; matrix products, arithmetic and copies ran while one was open for 1% -> 2% of each run, Pallas kernels for 6% -> 6%
where the time goes in v7:
time: 78 us; the launch traced here: 77.5 us
  starting transfers between devices  32 us (41%)
  waiting for transfers between devices  22.5 us (29%)
  Pallas kernels  19.2 us (25%)
  local copies, waits for them, and re-layouts  2.68 us (3%)
  between operations  0.85 us (1%)
    all_to_all x4, starting transfers between devices, exchange(): return lax.all_to_all(x, axes, split_axis=0, concat_axis=0, tiled=True)  26.4 us
    all_to_all x4, waiting for transfers between devices, exchange(): return lax.all_to_all(x, axes, split_axis=0, concat_axis=0, tiled=True)  21.5 us
    pallas_call x1, Pallas kernels, conv_sums(): pl.pallas_call(functools.partial(conv_kernel_body, sizes), grid=(samples...  8.19 us
    pallas_call x1, Pallas kernels, dense_delta(): pl.pallas_call(functools.partial(dense_kernel_body, depth, spaces), in_sp...  4.48 us
    ppermute x1, starting transfers between devices, on_device(): before = lax.ppermute(volume[:, :, planes - 1:], SPACE, up)  4.03 us
    pallas_call x1, Pallas kernels, final_steps(): pl.pallas_call(functools.partial(final_kernel_body, filters, patch_rows,...  3.39 us
  transfers between devices with their start and end apart: 7, of which 5 were waited for; matrix products, arithmetic and copies ran while one was open for 2% of the time, Pallas kernels for 6%

profile of v7, /device:TPU:1, one launch (start us, length us, event | category | flops | bytes accessed | tf_op | source)
XLA Modules:
  0.0 77.5 jit_solution(9773662294760653068)
XLA Ops:
  0.6 0.0 copy-start
  0.6 0.0 copy-start.1
  0.7 1.1 %fusion.25 = (bf16[8,4,1,16,128]{4,3,2,1,0:T(8,128)(2,1)S(1)}, bf16[8,4,1,16,128]{4,3,2,1,0:T(8,128)(2,1)S(1)}) fusion(bf16[8,4,4,16,128]{4,3,2,1,0:T(8,128)(2,1)} %vol_ref.1), kind=kLoop, calls=%fused_computation.54 | loop fusion | bytes 524288 | tf_op jit(solution)/shard_map/slice | solution.py:559
  1.7 4.0 %collective-permute-start = (bf16[8,4,1,16,128]{4,3,2,1,0:T(8,128)(2,1)S(1)}, bf16[8,4,1,16,128]{4,3,2,1,0:T(8,128)(2,1)S(1)}, u32[]{:S(2)}, u32[]{:S(2)}) collective-permute-start(bf16[8,4,1,16,128]{4,3,2,1,0:T(8,128)(2,1)S(1)} %get-tuple-element.13), channel_id=1, source_target_pairs={{0,1},{1,2},{2,3},{3,4},{4,5},{5,6},{6,7},{8,9},{9,10},{10,11},{11... | collective-permute-start | bytes 393224 | tf_op jit(solution)/shard_map/ppermute | solution.py:558
  5.8 0.0 copy-start.2
  5.8 1.3 %collective-permute-start.1 = (bf16[8,4,1,16,128]{4,3,2,1,0:T(8,128)(2,1)S(1)}, bf16[8,4,1,16,128]{4,3,2,1,0:T(8,128)(2,1)S(1)}, u32[]{:S(2)}, u32[]{:S(2)}) collective-permute-start(bf16[8,4,1,16,128]{4,3,2,1,0:T(8,128)(2,1)S(1)} %get-tuple-element.12), channel_id=1, source_target_pairs={{1,0},{2,1},{3,2},{4,3},{5,4},{6,5},{7,6},{9,8},{10,9},{11,10},{12... | collective-permute-start | bytes 393224 | tf_op jit(solution)/shard_map/ppermute | solution.py:559
  7.1 0.0 copy-done.2
  7.1 0.6 broadcast_in_dim.13
  7.7 5.9 %all-to-all-start = ((bf16[8,1,128]{2,1,0:T(2,128)(2,1)}), bf16[8,1,128]{2,1,0:T(2,128)(2,1)S(1)}, u32[]{:S(2)}, u32[]{:S(2)}) async-start(bf16[8,1,128]{2,1,0:T(2,128)(2,1)} %broadcast_in_dim.13), calls=%async_computation | async-start | bytes 8192 | tf_op jit(solution)/shard_map/all_to_all | solution.py:30
  13.6 0.0 copy-start.3
  13.6 0.7 copy-done.3
  14.3 0.1 copy.15
  14.5 0.1 fusion.22
  14.6 0.0 copy-done
  14.7 0.1 copy.17.bands_ref
  14.8 3.7 %all-to-all-done = bf16[8,1,128]{2,1,0:T(2,128)(2,1)S(1)} async-done(((bf16[8,1,128]{2,1,0:T(2,128)(2,1)}), bf16[8,1,128]{2,1,0:T(2,128)(2,1)S(1)}, u32[]{:S(2)}, u32[]{:S(2)}) %all-to-all-start) | async-done | bytes 2080 | tf_op jit(solution)/shard_map/all_to_all | solution.py:30
  18.5 0.0 collective-permute-done.before_ref
  18.5 0.0 collective-permute-done.1.after_ref
  18.5 0.0 copy-done.1
  18.6 8.2 %shard_map.62 = (f32[64,128]{1,0:T(8,128)S(1)}, f32[16,40,384]{2,1,0:T(8,128)S(1)}, f32[72,512]{1,0:T(8,128)S(1)}) custom-call(bf16[8,4,4,16,128]{4,3,2,1,0:T(8,128)(2,1)S(1)} %copy-done.1, bf16[8,4,1,16,128]{4,3,2,1,0:T(8,128)(2,1)S(1)} %collective-permute-done.before_ref, bf16[8,4,1,16,128]{4,3,2,1,0:T(8,128)(2,1)S(1)} %collective-permute-done.1.after_ref, ...), custom_call_target="tpu_custom_call" | custom-call | tf_op jit(solution)/shard_map/pallas_call | solution.py:149
  26.8 1.5 %shard_map.63 = bf16[16,24,128]{2,1,0:T(8,128)(2,1)} custom-call(f32[64,128]{1,0:T(8,128)S(1)} %get-tuple-element.7.pool_ref, f32[16,40,384]{2,1,0:T(8,128)S(1)} %get-tuple-element.8.sums_ref, f32[72,512]{1,0:T(8,128)S(1)} %get-tuple-element.9.gram_ref, bf16[64,128]{1,0:T(8,128)(2,1)S(1)} %bitcast.20, bf16[8,128]{1,0:T(8,128)(2,1)S(1)} %bitcast.21, ...), custom_call_target="tpu_custom_call" | custom-call | tf_op jit(solution)/shard_map/pallas_call | solution.py:271
  28.2 11.1 %all-to-all-start.1 = ((bf16[16,24,128]{2,1,0:T(8,128)(2,1)}), bf16[16,24,128]{2,1,0:T(8,128)(2,1)S(1)}, u32[]{:S(2)}, u32[]{:S(2)}) async-start(bf16[16,24,128]{2,1,0:T(8,128)(2,1)} %shard_map.63), calls=%async_computation.1 | async-start | bytes 196608 | tf_op jit(solution)/shard_map/all_to_all | solution.py:30
  39.4 8.4 %all-to-all-done.1 = bf16[16,24,128]{2,1,0:T(8,128)(2,1)S(1)} async-done(((bf16[16,24,128]{2,1,0:T(8,128)(2,1)}), bf16[16,24,128]{2,1,0:T(8,128)(2,1)S(1)}, u32[]{:S(2)}, u32[]{:S(2)}) %all-to-all-start.1) | async-done | bytes 98336 | tf_op jit(solution)/shard_map/all_to_all | solution.py:30
  47.8 0.9 %shard_map.64 = bf16[16,56,128]{2,1,0:T(8,128)(2,1)} custom-call(s32[1]{0:T(128)} %bitcast.1.core_ref, bf16[8,2,24,128]{3,2,1,0:T(8,128)(2,1)S(1)} %bitcast.19), custom_call_target="tpu_custom_call" | custom-call | tf_op jit(solution)/shard_map/pallas_call | solution.py:315
  48.7 4.4 %all-to-all-start.2 = ((bf16[16,56,128]{2,1,0:T(8,128)(2,1)}), bf16[16,56,128]{2,1,0:T(8,128)(2,1)S(1)}, u32[]{:S(2)}, u32[]{:S(2)}) async-start(bf16[16,56,128]{2,1,0:T(8,128)(2,1)} %shard_map.64), calls=%async_computation.2 | async-start | bytes 458752 | tf_op jit(solution)/shard_map/all_to_all | solution.py:30
  53.1 7.5 %all-to-all-done.2.got_ref.own_ref = bf16[16,56,128]{2,1,0:T(8,128)(2,1)S(1)} async-done(((bf16[16,56,128]{2,1,0:T(8,128)(2,1)}), bf16[16,56,128]{2,1,0:T(8,128)(2,1)S(1)}, u32[]{:S(2)}, u32[]{:S(2)}) %all-to-all-start.2) | async-done | bytes 229408 | tf_op jit(solution)/shard_map/all_to_all | solution.py:30
  60.6 0.8 %shard_map.65 = bf16[16,16,128]{2,1,0:T(8,128)(2,1)} custom-call(bf16[16,56,128]{2,1,0:T(8,128)(2,1)S(1)} %all-to-all-done.2.got_ref.own_ref), custom_call_target="tpu_custom_call" | custom-call | tf_op jit(solution)/shard_map/pallas_call | solution.py:332
  61.4 4.9 %all-to-all-start.3 = ((bf16[16,16,128]{2,1,0:T(8,128)(2,1)}), bf16[16,16,128]{2,1,0:T(8,128)(2,1)S(1)}, u32[]{:S(2)}, u32[]{:S(2)}) async-start(bf16[16,16,128]{2,1,0:T(8,128)(2,1)} %shard_map.65), calls=%async_computation.3 | async-start | bytes 131072 | tf_op jit(solution)/shard_map/all_to_all | solution.py:30
  66.3 0.3 collective-permute-start.2
  66.7 0.1 pad_add_fusion.place_ref
  66.8 1.0 %collective-permute-done.2.other_ref = bf16[16,40,128]{2,1,0:T(8,128)(2,1)S(1)} collective-permute-done((bf16[16,40,128]{2,1,0:T(8,128)(2,1)S(1)}, bf16[16,40,128]{2,1,0:T(8,128)(2,1)S(1)}, u32[]{:S(2)}, u32[]{:S(2)}) %collective-permute-start.2) | collective-permute-done | bytes 163872 | tf_op jit(solution)/shard_map/ppermute | solution.py:585
  67.8 4.5 %shard_map.66.delta_ref = f32[136,64]{1,0:T(8,128)S(1)} custom-call(s32[3]{0:T(128)S(1)} %pad_add_fusion.place_ref, bf16[16,56,128]{2,1,0:T(8,128)(2,1)S(1)} %all-to-all-done.2.got_ref.own_ref, bf16[16,40,128]{2,1,0:T(8,128)(2,1)S(1)} %collective-permute-done.2.other_ref), custom_call_target="tpu_custom_call" | custom-call | tf_op jit(solution)/shard_map/pallas_call | solution.py:480
  72.3 1.8 %all-to-all-done.3.got_ref = bf16[16,16,128]{2,1,0:T(8,128)(2,1)S(1)} async-done(((bf16[16,16,128]{2,1,0:T(8,128)(2,1)}), bf16[16,16,128]{2,1,0:T(8,128)(2,1)S(1)}, u32[]{:S(2)}, u32[]{:S(2)}) %all-to-all-start.3) | async-done | bytes 65568 | tf_op jit(solution)/shard_map/all_to_all | solution.py:30
  74.1 3.4 %shard_map.67 = (f32[32,108]{1,0:T(8,128)}, f32[4,64]{1,0:T(4,128)}) custom-call(s32[3]{0:T(128)S(1)} %pad_add_fusion.place_ref, bf16[16,16,128]{2,1,0:T(8,128)(2,1)S(1)} %all-to-all-done.3.got_ref, f32[136,64]{1,0:T(8,128)S(1)} %shard_map.66.delta_ref, f32[128,128]{1,0:T(8,128)S(1)} %fusion.20.order_ref), custom_call_target="tpu_custom_call" | custom-call | tf_op jit(solution)/shard_map/pallas_call | solution.py:528
  (15 shorter events, 0.2 us)
Async XLA Ops:
  0.6 14.0 %copy-start = (bf16[512,128]{1,0:T(8,128)(2,1)S(1)}, bf16[512,128]{1,0:T(8,128)(2,1)}, u32[]{:S(2)}) copy-start(bf16[512,128]{1,0:T(8,128)(2,1)} %param.6) | copy-start | bytes 393220
  0.6 17.9 %copy-start.1 = (bf16[8,4,4,16,128]{4,3,2,1,0:T(8,128)(2,1)S(1)}, bf16[8,4,4,16,128]{4,3,2,1,0:T(8,128)(2,1)}, u32[]{:S(2)}) copy-start(bf16[8,4,4,16,128]{4,3,2,1,0:T(8,128)(2,1)} %vol_ref.1) | copy-start | bytes 1572868
  1.7 16.8 %collective-permute-start = (bf16[8,4,1,16,128]{4,3,2,1,0:T(8,128)(2,1)S(1)}, bf16[8,4,1,16,128]{4,3,2,1,0:T(8,128)(2,1)S(1)}, u32[]{:S(2)}, u32[]{:S(2)}) collective-permute-start(bf16[8,4,1,16,128]{4,3,2,1,0:T(8,128)(2,1)S(1)} %get-tuple-element.13), channel_id=1, source_target_pairs={{0,1},{1,2},{2,3},{3,4},{4,5},{5,6},{6,7},{8,9},{9,10},{10,11},{11... | collective-permute-start | bytes 393224 | tf_op jit(solution)/shard_map/ppermute | solution.py:558
  5.8 1.3 %copy-start.2 = (bf16[1,128]{1,0:T(2,128)(2,1)S(1)}, bf16[1,128]{1,0:T(2,128)(2,1)}, u32[]{:S(2)}) copy-start(bf16[1,128]{1,0:T(2,128)(2,1)} %own_ref.1) | copy-start | bytes 772
  5.8 12.8 %collective-permute-start.1 = (bf16[8,4,1,16,128]{4,3,2,1,0:T(8,128)(2,1)S(1)}, bf16[8,4,1,16,128]{4,3,2,1,0:T(8,128)(2,1)S(1)}, u32[]{:S(2)}, u32[]{:S(2)}) collective-permute-start(bf16[8,4,1,16,128]{4,3,2,1,0:T(8,128)(2,1)S(1)} %get-tuple-element.12), channel_id=1, source_target_pairs={{1,0},{2,1},{3,2},{4,3},{5,4},{6,5},{7,6},{9,8},{10,9},{11,10},{12... | collective-permute-start | bytes 393224 | tf_op jit(solution)/shard_map/ppermute | solution.py:559
  7.7 10.9 %all-to-all-start = ((bf16[8,1,128]{2,1,0:T(2,128)(2,1)}), bf16[8,1,128]{2,1,0:T(2,128)(2,1)S(1)}, u32[]{:S(2)}, u32[]{:S(2)}) async-start(bf16[8,1,128]{2,1,0:T(2,128)(2,1)} %broadcast_in_dim.13), calls=%async_computation | async-start | bytes 8192 | tf_op jit(solution)/shard_map/all_to_all | solution.py:30
  13.6 0.7 copy-start.3
  28.2 19.6 %all-to-all-start.1 = ((bf16[16,24,128]{2,1,0:T(8,128)(2,1)}), bf16[16,24,128]{2,1,0:T(8,128)(2,1)S(1)}, u32[]{:S(2)}, u32[]{:S(2)}) async-start(bf16[16,24,128]{2,1,0:T(8,128)(2,1)} %shard_map.63), calls=%async_computation.1 | async-start | bytes 196608 | tf_op jit(solution)/shard_map/all_to_all | solution.py:30
  48.7 11.9 %all-to-all-start.2 = ((bf16[16,56,128]{2,1,0:T(8,128)(2,1)}), bf16[16,56,128]{2,1,0:T(8,128)(2,1)S(1)}, u32[]{:S(2)}, u32[]{:S(2)}) async-start(bf16[16,56,128]{2,1,0:T(8,128)(2,1)} %shard_map.64), calls=%async_computation.2 | async-start | bytes 458752 | tf_op jit(solution)/shard_map/all_to_all | solution.py:30
  61.4 12.7 %all-to-all-start.3 = ((bf16[16,16,128]{2,1,0:T(8,128)(2,1)}), bf16[16,16,128]{2,1,0:T(8,128)(2,1)S(1)}, u32[]{:S(2)}, u32[]{:S(2)}) async-start(bf16[16,16,128]{2,1,0:T(8,128)(2,1)} %shard_map.65), calls=%async_computation.3 | async-start | bytes 131072 | tf_op jit(solution)/shard_map/all_to_all | solution.py:30
  66.3 1.5 %collective-permute-start.2 = (bf16[16,40,128]{2,1,0:T(8,128)(2,1)S(1)}, bf16[16,40,128]{2,1,0:T(8,128)(2,1)S(1)}, u32[]{:S(2)}, u32[]{:S(2)}) collective-permute-start(bf16[16,40,128]{2,1,0:T(8,128)(2,1)S(1)} %slice.12), channel_id=1, source_target_pairs={{0,8},{8,0},{1,9},{9,1},{2,10},{10,2},{3,11},{11,3},{4,12},{12,4},... | collective-permute-start | bytes 491528 | tf_op jit(solution)/shard_map/ppermute | solution.py:585

commit v8 on v7

--- a/solution.py
+++ b/solution.py
@@ -39,8 +39,8 @@
 
 
 def conv_kernel_body(
-    sizes, vol_ref, before_ref, after_ref, bands_ref,
-    pool_ref, sums_ref, gram_ref, shift_a, shift_b, stack_a, stack_b, wide_a, wide_b,
+    sizes, vol_ref, before_ref, after_ref, kernel_ref, pool_ref, sums_ref, gram_ref,
+    shift_a, shift_b, stack_a, stack_b, wide_a, wide_b, edges, bands_ref, taken, done,
 ):
     channels, planes, height, length, filters, samples = sizes
     rim = planes + 2
@@ -113,34 +113,59 @@
                 to = slice(0, filters) if first == 0 else slice(filters, filters + 8)
                 sums_ref[slot + part, to, :256] = patch
                 sums_ref[slot + part, to, 256:] = mask
+        spot = pl.ds(pl.multiple_of(sample * length, length), length)
         for side, y in ((0, height - 1), (1, 0)):
-            edge = stacked[base + group:base + 2 * group, y * length:(y + 1) * length]
-            gram_ref[:, 256 + side * 128:256 + side * 128 + group] += lax.dot_general(
-                edge, edge, CONTRACT, preferred_element_type=F32
-            )
+            edges[side, :, spot] = stacked[
+                base + group:base + 2 * group, y * length:(y + 1) * length
+            ]
         pooled = jnp.concatenate(pooled, axis=0) * (1.0 / (planes * half))
         spot = lax.broadcasted_iota(jnp.int32, pool_ref.shape, 1)
         pool_ref[...] = jnp.where(spot == sample, pooled, pool_ref[...])
 
     @pl.when(step == 0)
     def _():
-        shift_a[...] = jnp.zeros_like(shift_a)
-        shift_b[...] = jnp.zeros_like(shift_b)
+        fetch = pltpu.make_async_copy(kernel_ref, taken, done)
+        fetch.start()
+        blank = jnp.zeros((group, length), F32)
+        for shifted in (shift_a, shift_b):
+            shifted[0:group, :] = blank
+            shifted[(height + 1) * group:, :] = blank
         ones = jnp.ones((16, height * length), BF16)
         stack_a[top:base, :] = ones
         stack_b[top:base, :] = ones
         gram_ref[...] = jnp.zeros_like(gram_ref)
         pool_ref[...] = jnp.zeros_like(pool_ref)
         build(0, shift_a, stack_a)
+        at = lax.broadcasted_iota(jnp.int32, (1, 256), 1)
+        j, rest = at // group, at % group
+        inner = channels * 3
+        i, channel, k = rest // inner, rest % inner // 3, rest % 3
+        used = jnp.logical_and(rest < 3 * inner, at < rows)
+        source = jnp.where(used, channel * 27 + i * 9 + j * 3 + k, -1)
+        row = lax.broadcasted_iota(jnp.int32, (kernel_ref.shape[1], 256), 0)
+        pick = jnp.where(row == source, 1.0, 0.0).astype(BF16)
+        fetch.wait()
+        band = jnp.dot(taken[...], pick, preferred_element_type=F32)
+        bands_ref[...] = jnp.concatenate(
+            [band] + [pltpu.roll(band, plane * inner, 1) for plane in range(1, planes)], axis=0
+        )[:, :rows].astype(BF16)
 
     build(2 * step + 1, shift_b, stack_b)
     consume(2 * step, stack_a, wide_a)
     build(jnp.minimum(2 * step + 2, samples - 1), shift_a, stack_a)
     consume(2 * step + 1, stack_b, wide_b)
 
-
-def conv_sums(volume, before, after, bands, filters):
+    @pl.when(step == pl.num_programs(0) - 1)
+    def _():
+        for side in range(2):
+            gram_ref[:, 256 + side * 128:256 + side * 128 + group] = lax.dot_general(
+                edges[side], edges[side], CONTRACT, preferred_element_type=F32
+            )
+
+
+def conv_sums(volume, before, after, conv_kernel):
     samples, channels, planes, height, length = volume.shape
+    filters = conv_kernel.shape[0]
     group = (planes + 2) * channels * 3
     top = planes * filters
     stack = top + 16 + 3 * group
@@ -149,7 +174,7 @@
     return pl.pallas_call(
         functools.partial(conv_kernel_body, sizes),
         grid=(samples // 2,),
-        in_specs=[vmem] * 4,
+        in_specs=[vmem] * 3 + [pl.BlockSpec(memory_space=pltpu.HBM)],
         out_specs=[vmem] * 3,
         out_shape=[
             jax.ShapeDtypeStruct((filters * PC, 128), F32),
@@ -163,9 +188,13 @@
             pltpu.VMEM((stack, height * length), BF16),
             pltpu.VMEM((PC, top + 8, 256), F32),
             pltpu.VMEM((PC, top + 8, 256), F32),
+            pltpu.VMEM((2, group, samples * length), BF16),
+            pltpu.VMEM((top, 3 * group), BF16),
+            pltpu.VMEM(conv_kernel.shape, BF16),
+            pltpu.SemaphoreType.DMA(()),
         ],
         compiler_params=pltpu.CompilerParams(vmem_limit_bytes=24 * 1024 * 1024),
-    )(volume, before, after, bands)
+    )(volume, before, after, conv_kernel)
 
 
 def moments_body(
@@ -411,7 +440,7 @@
 
 
 def dense_kernel_body(
-    depth, spaces, place_ref, own_ref, other_ref, delta_ref, whole, cots,
+    depth, spaces, place_ref, own_ref, other_ref, delta_ref, whole, cots, every,
 ):
     parts = own_ref.shape[0] // spaces
     width = 64
@@ -464,14 +493,17 @@
     pick = jnp.where(source == spot, 1.0, 0.0).astype(BF16)
     mine = jnp.dot(mine.astype(BF16), pick, preferred_element_type=F32).astype(BF16)
     high, low = parts_of(held)
-    outputs = cot_wide.shape[1]
-    delta_ref[outputs:, :] = jnp.broadcast_to(total, (8, width))
-    delta_ref[0:outputs, :] = lax.dot_general(
+    every[...] = lax.dot_general(
         jnp.concatenate([high, low], axis=0),
         jnp.concatenate([mine, mine], axis=0),
         LEADING,
         preferred_element_type=F32,
     )
+    share = delta_ref.shape[0] - 8
+    first = place_ref[2] * share // 8 * 8
+    window = every[pl.ds(pl.multiple_of(first, 8), 8), :]
+    delta_ref[0:share, :] = jnp.where(place_ref[2] % 2 == 0, window[:share], window[share:])
+    delta_ref[share:, :] = jnp.broadcast_to(total, (8, width))
 
 
 def dense_delta(place, own, other, depth, spaces, outputs):
@@ -481,17 +513,18 @@
         functools.partial(dense_kernel_body, depth, spaces),
         in_specs=[pl.BlockSpec(memory_space=pltpu.SMEM), vmem, vmem],
         out_specs=vmem,
-        out_shape=jax.ShapeDtypeStruct((outputs + 8, 64), F32),
+        out_shape=jax.ShapeDtypeStruct((4 + 8, 64), F32),
         scratch_shapes=[
             pltpu.VMEM((count, spaces * 64), BF16),
             pltpu.VMEM((count, outputs), F32),
+            pltpu.VMEM((outputs, 64), F32),
         ],
         compiler_params=pltpu.CompilerParams(vmem_limit_bytes=48 * 1024 * 1024),
     )(place, own, other)
 
 
 def final_kernel_body(
-    filters, patch_rows, cells, place_ref, got_ref, delta_ref, order_ref,
+    filters, patch_rows, cells, got_ref, delta_ref, order_ref,
     step_conv_ref, step_dense_ref,
 ):
     scale = 1.0 / cells
@@ -513,28 +546,25 @@
     right, bound_in = residual(conv_in, patch_rows)
     left, bound_out = residual(conv_out, filters)
     held = two_sided(left[0:filters], conv_grad / bound_in / bound_out, right)
-    total = scalar_sum(held * conv_grad) + delta_ref[delta_ref.shape[0] - 8:, 0:1][0:1]
+    total = scalar_sum(held * conv_grad) + delta_ref[4:5, 0:1]
     scaling = jnp.minimum(1.0, jnp.sqrt(KL_BOUND / (LEARN_RATE * LEARN_RATE * total)))
     moved = split_dot(held, order_ref[...])
     step_conv_ref[...] = scaling * moved[:, 0:patch_rows]
-    first = place_ref[2] // 2 * 8
-    window = delta_ref[pl.ds(pl.multiple_of(first, 8), 8), :]
-    mine = jnp.where(place_ref[2] % 2 == 0, window[0:4], window[4:8])
-    step_dense_ref[...] = scaling * mine
-
-
-def final_steps(place, moments, delta, order, filters, patch_rows, cells):
+    step_dense_ref[...] = scaling * delta_ref[0:4, :]
+
+
+def final_steps(moments, delta, order, filters, patch_rows, cells):
     vmem = pl.BlockSpec(memory_space=pltpu.VMEM)
     return pl.pallas_call(
         functools.partial(final_kernel_body, filters, patch_rows, cells),
-        in_specs=[pl.BlockSpec(memory_space=pltpu.SMEM)] + [vmem] * 3,
+        in_specs=[vmem] * 3,
         out_specs=[vmem] * 2,
         out_shape=[
             jax.ShapeDtypeStruct((filters, patch_rows), F32),
             jax.ShapeDtypeStruct((4, delta.shape[1]), F32),
         ],
         compiler_params=pltpu.CompilerParams(vmem_limit_bytes=32 * 1024 * 1024),
-    )(place, moments, delta, order)
+    )(moments, delta, order)
 
 
 def column_order(channels):
@@ -559,22 +589,11 @@
     after = lax.ppermute(volume[:, :, :1], SPACE, down)
     cot_group = gather_from(cotangent[0], SPACE, spaces)
 
-    mixed = conv_kernel.reshape(filters, channels, 3, 3, 3).transpose(0, 3, 2, 1, 4)
-    mixed = mixed.reshape(filters, 3, channels * 9)
-    inner = channels * 3
-    spare = (planes - 1) * inner
-    bands = jnp.concatenate(
-        [
-            jnp.pad(mixed, ((0, 0), (0, 0), (p * inner, spare - p * inner)))
-            for p in range(planes)
-        ],
-        axis=0,
-    ).reshape(planes * filters, -1)
     place = lax.axis_index(SPACE)
     weight = lax.dynamic_slice_in_dim(dense_weight, place * slab, slab, 0)
     weight = weight.reshape(filters, PC, -1).transpose(1, 0, 2).reshape(slab, -1)
 
-    sums = conv_sums(volume, before, after, bands, filters)
+    sums = conv_sums(volume, before, after, conv_kernel)
     sizes = (channels, planes, planes * height * length // PC, filters, samples)
     sent = conv_moments(sizes, sums, weight, cot_group, cotangent, column)
     peers = spaces * groups // column
@@ -587,7 +606,7 @@
     delta = dense_delta(places, got, other, column // 2, spaces, cotangent.shape[1])
     cells = samples * groups * planes * spaces * height * length
     step_conv, step_dense = final_steps(
-        places, reduced, delta, column_order(channels), filters, patch_rows, cells
+        reduced, delta, column_order(channels), filters, patch_rows, cells
     )
     return step_conv, step_dense.T
 

time: 78 us -> 77.8 us (level)
  waiting for transfers between devices: 22.5 us -> 23.6 us
  local copies, waits for them, and re-layouts: 2.68 us -> 1.72 us
    all_to_all x4, waiting for transfers between devices: 21.5 us -> 22.6 us  [exchange(): return lax.all_to_all(x, axes, split_axis=0, concat_axis=0, tiled=True)]
    unnamed x10 -> x9, local copies, waits for them, and re-layouts: 0.82 us -> 0.03 us
  transfers between devices with their start and end apart: 7 -> 7, of which waited for: 5 -> 5; matrix products, arithmetic and copies ran while one was open for 2% -> 1% of each run, Pallas kernels for 6% -> 6%
where the time goes in v8:
time: 77.8 us; the launch traced here: 77.3 us
  starting transfers between devices  32 us (41%)
  waiting for transfers between devices  23.6 us (30%)
  Pallas kernels  18.9 us (24%)
  local copies, waits for them, and re-layouts  1.72 us (2%)
  between operations  0.82 us (1%)
    all_to_all x4, starting transfers between devices, exchange(): return lax.all_to_all(x, axes, split_axis=0, concat_axis=0, tiled=True)  26.4 us
    all_to_all x4, waiting for transfers between devices, exchange(): return lax.all_to_all(x, axes, split_axis=0, concat_axis=0, tiled=True)  22.6 us
    pallas_call x1, Pallas kernels, conv_sums(): pl.pallas_call(functools.partial(conv_kernel_body, sizes), grid=(samples...  8.47 us
    pallas_call x1, Pallas kernels, dense_delta(): pl.pallas_call(functools.partial(dense_kernel_body, depth, spaces), in_sp...  4.48 us
    ppermute x1, starting transfers between devices, on_device(): before = lax.ppermute(volume[:, :, planes - 1:], SPACE, up)  4.03 us
    pallas_call x1, Pallas kernels, final_steps(): pl.pallas_call(functools.partial(final_kernel_body, filters, patch_rows,...  2.85 us
  transfers between devices with their start and end apart: 7, of which 5 were waited for; matrix products, arithmetic and copies ran while one was open for 1% of the time, Pallas kernels for 6%

profile of v8, /device:TPU:1, one launch (start us, length us, event | category | flops | bytes accessed | tf_op | source)
XLA Modules:
  0.0 77.3 jit_solution(8982409272662783079)
XLA Ops:
  0.6 0.0 copy-start
  0.6 0.0 copy-start.1
  0.7 1.1 %fusion.16 = (bf16[8,4,1,16,128]{4,3,2,1,0:T(8,128)(2,1)S(1)}, bf16[8,4,1,16,128]{4,3,2,1,0:T(8,128)(2,1)S(1)}) fusion(bf16[8,4,4,16,128]{4,3,2,1,0:T(8,128)(2,1)} %vol_ref.1), kind=kLoop, calls=%fused_computation.39 | loop fusion | bytes 524288 | tf_op jit(solution)/shard_map/slice | solution.py:589
  1.7 4.0 %collective-permute-start = (bf16[8,4,1,16,128]{4,3,2,1,0:T(8,128)(2,1)S(1)}, bf16[8,4,1,16,128]{4,3,2,1,0:T(8,128)(2,1)S(1)}, u32[]{:S(2)}, u32[]{:S(2)}) collective-permute-start(bf16[8,4,1,16,128]{4,3,2,1,0:T(8,128)(2,1)S(1)} %get-tuple-element.13), channel_id=1, source_target_pairs={{0,1},{1,2},{2,3},{3,4},{4,5},{5,6},{6,7},{8,9},{9,10},{10,11},{11... | collective-permute-start | bytes 393224 | tf_op jit(solution)/shard_map/ppermute | solution.py:588
  5.8 0.0 copy-start.3
  5.8 1.3 %collective-permute-start.1 = (bf16[8,4,1,16,128]{4,3,2,1,0:T(8,128)(2,1)S(1)}, bf16[8,4,1,16,128]{4,3,2,1,0:T(8,128)(2,1)S(1)}, u32[]{:S(2)}, u32[]{:S(2)}) collective-permute-start(bf16[8,4,1,16,128]{4,3,2,1,0:T(8,128)(2,1)S(1)} %get-tuple-element.12), channel_id=1, source_target_pairs={{1,0},{2,1},{3,2},{4,3},{5,4},{6,5},{7,6},{9,8},{10,9},{11,10},{12... | collective-permute-start | bytes 393224 | tf_op jit(solution)/shard_map/ppermute | solution.py:589
  7.1 0.0 copy-done.3
  7.1 0.6 broadcast_in_dim.13
  7.7 5.9 %all-to-all-start = ((bf16[8,1,128]{2,1,0:T(2,128)(2,1)}), bf16[8,1,128]{2,1,0:T(2,128)(2,1)S(1)}, u32[]{:S(2)}, u32[]{:S(2)}) async-start(bf16[8,1,128]{2,1,0:T(2,128)(2,1)} %broadcast_in_dim.13), calls=%async_computation | async-start | bytes 8192 | tf_op jit(solution)/shard_map/all_to_all | solution.py:30
  13.6 0.0 copy-done
  13.6 0.0 copy-start.2
  13.7 4.9 %all-to-all-done = bf16[8,1,128]{2,1,0:T(2,128)(2,1)S(1)} async-done(((bf16[8,1,128]{2,1,0:T(2,128)(2,1)}), bf16[8,1,128]{2,1,0:T(2,128)(2,1)S(1)}, u32[]{:S(2)}, u32[]{:S(2)}) %all-to-all-start) | async-done | bytes 2080 | tf_op jit(solution)/shard_map/all_to_all | solution.py:30
  18.5 0.0 collective-permute-done.before_ref
  18.5 0.0 collective-permute-done.1.after_ref
  18.5 0.0 copy-done.1
  18.6 0.0 copy-done.2
  18.6 8.5 %shard_map.62 = (f32[64,128]{1,0:T(8,128)S(1)}, f32[16,40,384]{2,1,0:T(8,128)S(1)}, f32[72,512]{1,0:T(8,128)S(1)}) custom-call(bf16[8,4,4,16,128]{4,3,2,1,0:T(8,128)(2,1)S(1)} %copy-done.1, bf16[8,4,1,16,128]{4,3,2,1,0:T(8,128)(2,1)S(1)} %collective-permute-done.before_ref, bf16[8,4,1,16,128]{4,3,2,1,0:T(8,128)(2,1)S(1)} %collective-permute-done.1.after_ref, ...), custom_call_target="tpu_custom_call" | custom-call | tf_op jit(solution)/shard_map/pallas_call | solution.py:174
  27.0 1.5 %shard_map.63 = bf16[16,24,128]{2,1,0:T(8,128)(2,1)} custom-call(f32[64,128]{1,0:T(8,128)S(1)} %get-tuple-element.7.pool_ref, f32[16,40,384]{2,1,0:T(8,128)S(1)} %get-tuple-element.8.sums_ref, f32[72,512]{1,0:T(8,128)S(1)} %get-tuple-element.9.gram_ref, bf16[64,128]{1,0:T(8,128)(2,1)S(1)} %bitcast.14, bf16[8,128]{1,0:T(8,128)(2,1)S(1)} %bitcast.15, ...), custom_call_target="tpu_custom_call" | custom-call | tf_op jit(solution)/shard_map/pallas_call | solution.py:300
  28.5 11.1 %all-to-all-start.1 = ((bf16[16,24,128]{2,1,0:T(8,128)(2,1)}), bf16[16,24,128]{2,1,0:T(8,128)(2,1)S(1)}, u32[]{:S(2)}, u32[]{:S(2)}) async-start(bf16[16,24,128]{2,1,0:T(8,128)(2,1)} %shard_map.63), calls=%async_computation.1 | async-start | bytes 196608 | tf_op jit(solution)/shard_map/all_to_all | solution.py:30
  39.7 8.4 %all-to-all-done.1 = bf16[16,24,128]{2,1,0:T(8,128)(2,1)S(1)} async-done(((bf16[16,24,128]{2,1,0:T(8,128)(2,1)}), bf16[16,24,128]{2,1,0:T(8,128)(2,1)S(1)}, u32[]{:S(2)}, u32[]{:S(2)}) %all-to-all-start.1) | async-done | bytes 98336 | tf_op jit(solution)/shard_map/all_to_all | solution.py:30
  48.1 0.9 %shard_map.64 = bf16[16,56,128]{2,1,0:T(8,128)(2,1)} custom-call(s32[1]{0:T(128)} %bitcast.core_ref, bf16[8,2,24,128]{3,2,1,0:T(8,128)(2,1)S(1)} %bitcast.13), custom_call_target="tpu_custom_call" | custom-call | tf_op jit(solution)/shard_map/pallas_call | solution.py:344
  49.0 4.4 %all-to-all-start.2 = ((bf16[16,56,128]{2,1,0:T(8,128)(2,1)}), bf16[16,56,128]{2,1,0:T(8,128)(2,1)S(1)}, u32[]{:S(2)}, u32[]{:S(2)}) async-start(bf16[16,56,128]{2,1,0:T(8,128)(2,1)} %shard_map.64), calls=%async_computation.2 | async-start | bytes 458752 | tf_op jit(solution)/shard_map/all_to_all | solution.py:30
  53.5 7.5 %all-to-all-done.2.got_ref.own_ref = bf16[16,56,128]{2,1,0:T(8,128)(2,1)S(1)} async-done(((bf16[16,56,128]{2,1,0:T(8,128)(2,1)}), bf16[16,56,128]{2,1,0:T(8,128)(2,1)S(1)}, u32[]{:S(2)}, u32[]{:S(2)}) %all-to-all-start.2) | async-done | bytes 229408 | tf_op jit(solution)/shard_map/all_to_all | solution.py:30
  60.9 0.8 %shard_map.65 = bf16[16,16,128]{2,1,0:T(8,128)(2,1)} custom-call(bf16[16,56,128]{2,1,0:T(8,128)(2,1)S(1)} %all-to-all-done.2.got_ref.own_ref), custom_call_target="tpu_custom_call" | custom-call | tf_op jit(solution)/shard_map/pallas_call | solution.py:361
  61.7 4.9 %all-to-all-start.3 = ((bf16[16,16,128]{2,1,0:T(8,128)(2,1)}), bf16[16,16,128]{2,1,0:T(8,128)(2,1)S(1)}, u32[]{:S(2)}, u32[]{:S(2)}) async-start(bf16[16,16,128]{2,1,0:T(8,128)(2,1)} %shard_map.65), calls=%async_computation.3 | async-start | bytes 131072 | tf_op jit(solution)/shard_map/all_to_all | solution.py:30
  66.6 0.3 collective-permute-start.2
  67.0 0.1 pad_add_fusion.place_ref
  67.1 1.0 %collective-permute-done.2.other_ref = bf16[16,40,128]{2,1,0:T(8,128)(2,1)S(1)} collective-permute-done((bf16[16,40,128]{2,1,0:T(8,128)(2,1)S(1)}, bf16[16,40,128]{2,1,0:T(8,128)(2,1)S(1)}, u32[]{:S(2)}, u32[]{:S(2)}) %collective-permute-start.2) | collective-permute-done | bytes 163872 | tf_op jit(solution)/shard_map/ppermute | solution.py:604
  68.1 4.5 %shard_map.66.delta_ref = f32[12,64]{1,0:T(8,128)S(1)} custom-call(s32[3]{0:T(128)S(1)} %pad_add_fusion.place_ref, bf16[16,56,128]{2,1,0:T(8,128)(2,1)S(1)} %all-to-all-done.2.got_ref.own_ref, bf16[16,40,128]{2,1,0:T(8,128)(2,1)S(1)} %collective-permute-done.2.other_ref), custom_call_target="tpu_custom_call" | custom-call | tf_op jit(solution)/shard_map/pallas_call | solution.py:512
  72.6 1.8 %all-to-all-done.3.got_ref = bf16[16,16,128]{2,1,0:T(8,128)(2,1)S(1)} async-done(((bf16[16,16,128]{2,1,0:T(8,128)(2,1)}), bf16[16,16,128]{2,1,0:T(8,128)(2,1)S(1)}, u32[]{:S(2)}, u32[]{:S(2)}) %all-to-all-start.3) | async-done | bytes 65568 | tf_op jit(solution)/shard_map/all_to_all | solution.py:30
  74.4 2.8 %shard_map.67 = (f32[32,108]{1,0:T(8,128)}, f32[4,64]{1,0:T(4,128)}) custom-call(bf16[16,16,128]{2,1,0:T(8,128)(2,1)S(1)} %all-to-all-done.3.got_ref, f32[12,64]{1,0:T(8,128)S(1)} %shard_map.66.delta_ref, f32[128,128]{1,0:T(8,128)S(1)} %fusion.14.order_ref), custom_call_target="tpu_custom_call" | custom-call | tf_op jit(solution)/shard_map/pallas_call | solution.py:558
  (12 shorter events, 0.1 us)
Async XLA Ops:
  0.6 13.0 %copy-start = (bf16[512,128]{1,0:T(8,128)(2,1)S(1)}, bf16[512,128]{1,0:T(8,128)(2,1)}, u32[]{:S(2)}) copy-start(bf16[512,128]{1,0:T(8,128)(2,1)} %param.6) | copy-start | bytes 393220
  0.6 17.9 %copy-start.1 = (bf16[8,4,4,16,128]{4,3,2,1,0:T(8,128)(2,1)S(1)}, bf16[8,4,4,16,128]{4,3,2,1,0:T(8,128)(2,1)}, u32[]{:S(2)}) copy-start(bf16[8,4,4,16,128]{4,3,2,1,0:T(8,128)(2,1)} %vol_ref.1) | copy-start | bytes 1572868
  1.7 16.8 %collective-permute-start = (bf16[8,4,1,16,128]{4,3,2,1,0:T(8,128)(2,1)S(1)}, bf16[8,4,1,16,128]{4,3,2,1,0:T(8,128)(2,1)S(1)}, u32[]{:S(2)}, u32[]{:S(2)}) collective-permute-start(bf16[8,4,1,16,128]{4,3,2,1,0:T(8,128)(2,1)S(1)} %get-tuple-element.13), channel_id=1, source_target_pairs={{0,1},{1,2},{2,3},{3,4},{4,5},{5,6},{6,7},{8,9},{9,10},{10,11},{11... | collective-permute-start | bytes 393224 | tf_op jit(solution)/shard_map/ppermute | solution.py:588
  5.8 1.3 %copy-start.3 = (bf16[1,128]{1,0:T(2,128)(2,1)S(1)}, bf16[1,128]{1,0:T(2,128)(2,1)}, u32[]{:S(2)}) copy-start(bf16[1,128]{1,0:T(2,128)(2,1)} %own_ref.1) | copy-start | bytes 772
  5.8 12.8 %collective-permute-start.1 = (bf16[8,4,1,16,128]{4,3,2,1,0:T(8,128)(2,1)S(1)}, bf16[8,4,1,16,128]{4,3,2,1,0:T(8,128)(2,1)S(1)}, u32[]{:S(2)}, u32[]{:S(2)}) collective-permute-start(bf16[8,4,1,16,128]{4,3,2,1,0:T(8,128)(2,1)S(1)} %get-tuple-element.12), channel_id=1, source_target_pairs={{1,0},{2,1},{3,2},{4,3},{5,4},{6,5},{7,6},{9,8},{10,9},{11,10},{12... | collective-permute-start | bytes 393224 | tf_op jit(solution)/shard_map/ppermute | solution.py:589
  7.7 10.9 %all-to-all-start = ((bf16[8,1,128]{2,1,0:T(2,128)(2,1)}), bf16[8,1,128]{2,1,0:T(2,128)(2,1)S(1)}, u32[]{:S(2)}, u32[]{:S(2)}) async-start(bf16[8,1,128]{2,1,0:T(2,128)(2,1)} %broadcast_in_dim.13), calls=%async_computation | async-start | bytes 8192 | tf_op jit(solution)/shard_map/all_to_all | solution.py:30
  13.6 4.9 %copy-start.2 = (bf16[32,108]{1,0:T(8,128)(2,1)S(1)}, bf16[32,108]{1,0:T(8,128)(2,1)}, u32[]{:S(2)}) copy-start(bf16[32,108]{1,0:T(8,128)(2,1)} %kernel_ref.1) | copy-start | bytes 20740
  28.5 19.6 %all-to-all-start.1 = ((bf16[16,24,128]{2,1,0:T(8,128)(2,1)}), bf16[16,24,128]{2,1,0:T(8,128)(2,1)S(1)}, u32[]{:S(2)}, u32[]{:S(2)}) async-start(bf16[16,24,128]{2,1,0:T(8,128)(2,1)} %shard_map.63), calls=%async_computation.1 | async-start | bytes 196608 | tf_op jit(solution)/shard_map/all_to_all | solution.py:30
  49.0 11.9 %all-to-all-start.2 = ((bf16[16,56,128]{2,1,0:T(8,128)(2,1)}), bf16[16,56,128]{2,1,0:T(8,128)(2,1)S(1)}, u32[]{:S(2)}, u32[]{:S(2)}) async-start(bf16[16,56,128]{2,1,0:T(8,128)(2,1)} %shard_map.64), calls=%async_computation.2 | async-start | bytes 458752 | tf_op jit(solution)/shard_map/all_to_all | solution.py:30
  61.7 12.7 %all-to-all-start.3 = ((bf16[16,16,128]{2,1,0:T(8,128)(2,1)}), bf16[16,16,128]{2,1,0:T(8,128)(2,1)S(1)}, u32[]{:S(2)}, u32[]{:S(2)}) async-start(bf16[16,16,128]{2,1,0:T(8,128)(2,1)} %shard_map.65), calls=%async_computation.3 | async-start | bytes 131072 | tf_op jit(solution)/shard_map/all_to_all | solution.py:30
  66.6 1.5 %collective-permute-start.2 = (bf16[16,40,128]{2,1,0:T(8,128)(2,1)S(1)}, bf16[16,40,128]{2,1,0:T(8,128)(2,1)S(1)}, u32[]{:S(2)}, u32[]{:S(2)}) collective-permute-start(bf16[16,40,128]{2,1,0:T(8,128)(2,1)S(1)} %slice.12), channel_id=1, source_target_pairs={{0,8},{8,0},{1,9},{9,1},{2,10},{10,2},{3,11},{11,3},{4,12},{12,4},... | collective-permute-start | bytes 491528 | tf_op jit(solution)/shard_map/ppermute | solution.py:604

commit v9 on v8

--- a/solution.py
+++ b/solution.py
@@ -194,7 +194,7 @@
             pltpu.SemaphoreType.DMA(()),
         ],
         compiler_params=pltpu.CompilerParams(vmem_limit_bytes=24 * 1024 * 1024),
-    )(volume, before, after, conv_kernel)
+    )(volume, before, after, pltpu.with_memory_space_constraint(conv_kernel, pltpu.HBM))
 
 
 def moments_body(
@@ -324,7 +324,10 @@
     chunk = jnp.sum(from_halves(got_ref[:, 0, 0:share, :]), axis=0)
     for core in range(1, cores):
         chunk += jnp.sum(from_halves(got_ref[:, core, 0:share, :]), axis=0)
-    wide = got_ref[:, core_ref[0], share:, :].astype(F32)
+    upper = core_ref[...] > 0.5
+    wide = jnp.where(
+        upper[None], got_ref[:, 1, share:, :].astype(F32), got_ref[:, 0, share:, :].astype(F32)
+    )
     pairs = depth // 2
     feats = wide[:, :, :64]
     feats = jnp.concatenate([feats[:pairs], feats[pairs:]], axis=2).reshape(pairs * 8, 128)
@@ -343,7 +346,7 @@
     vmem = pl.BlockSpec(memory_space=pltpu.VMEM)
     return pl.pallas_call(
         middle_body,
-        in_specs=[pl.BlockSpec(memory_space=pltpu.SMEM), vmem],
+        in_specs=[vmem, vmem],
         out_specs=vmem,
         out_shape=jax.ShapeDtypeStruct((peers, rows - 8 + depth * 5, lanes), BF16),
         compiler_params=pltpu.CompilerParams(vmem_limit_bytes=8 * 1024 * 1024),
@@ -599,7 +602,7 @@
     peers = spaces * groups // column
     core = lax.axis_index("core")
     got = exchange(sent, COLUMN).reshape(column // 2, 2, -1, 128)
-    got = exchange(middle(core.reshape(1), got, peers), PLANE)
+    got = exchange(middle(jnp.broadcast_to(core.astype(F32), (8, 128)), got, peers), PLANE)
     reduced = exchange(spread(got, column), COLUMN)
     other = lax.ppermute(got[:, 256 // column:], "core", [(0, 1), (1, 0)])
     places = jnp.stack([place, core, lax.axis_index(DP)])

time: 77.8 us -> 78.3 us (level)
  no operation moved by 1% of the time
where the time goes in v9:
time: 78.3 us; the launch traced here: 77.8 us
  starting transfers between devices  32 us (41%)
  waiting for transfers between devices  23.7 us (30%)
  Pallas kernels  19.4 us (25%)
  local copies, waits for them, and re-layouts  1.71 us (2%)
  between operations  0.8 us (1%)
    all_to_all x4, starting transfers between devices, exchange(): return lax.all_to_all(x, axes, split_axis=0, concat_axis=0, tiled=True)  26.4 us
    all_to_all x4, waiting for transfers between devices, exchange(): return lax.all_to_all(x, axes, split_axis=0, concat_axis=0, tiled=True)  22.6 us
    pallas_call x1, Pallas kernels, conv_sums(): pl.pallas_call(functools.partial(conv_kernel_body, sizes), grid=(samples...  8.94 us
    pallas_call x1, Pallas kernels, dense_delta(): pl.pallas_call(functools.partial(dense_kernel_body, depth, spaces), in_sp...  4.49 us
    ppermute x1, starting transfers between devices, on_device(): before = lax.ppermute(volume[:, :, planes - 1:], SPACE, up)  4.03 us
    pallas_call x1, Pallas kernels, final_steps(): pl.pallas_call(functools.partial(final_kernel_body, filters, patch_rows,...  2.84 us
  transfers between devices with their start and end apart: 7, of which 5 were waited for; matrix products, arithmetic and copies ran while one was open for 1% of the time, Pallas kernels for 6%

profile of v9, /device:TPU:1, one launch (start us, length us, event | category | flops | bytes accessed | tf_op | source)
XLA Modules:
  0.0 77.8 jit_solution(17988998758367173813)
XLA Ops:
  0.6 0.0 copy-start
  0.6 0.0 copy-start.1
  0.7 1.1 %fusion.16 = (bf16[8,4,1,16,128]{4,3,2,1,0:T(8,128)(2,1)S(1)}, bf16[8,4,1,16,128]{4,3,2,1,0:T(8,128)(2,1)S(1)}) fusion(bf16[8,4,4,16,128]{4,3,2,1,0:T(8,128)(2,1)} %vol_ref.1), kind=kLoop, calls=%fused_computation.39 | loop fusion | bytes 524288 | tf_op jit(solution)/shard_map/slice | solution.py:592
  1.7 4.0 %collective-permute-start = (bf16[8,4,1,16,128]{4,3,2,1,0:T(8,128)(2,1)S(1)}, bf16[8,4,1,16,128]{4,3,2,1,0:T(8,128)(2,1)S(1)}, u32[]{:S(2)}, u32[]{:S(2)}) collective-permute-start(bf16[8,4,1,16,128]{4,3,2,1,0:T(8,128)(2,1)S(1)} %get-tuple-element.13), channel_id=1, source_target_pairs={{0,1},{1,2},{2,3},{3,4},{4,5},{5,6},{6,7},{8,9},{9,10},{10,11},{11... | collective-permute-start | bytes 393224 | tf_op jit(solution)/shard_map/ppermute | solution.py:591
  5.8 0.0 copy-start.2
  5.8 1.3 %collective-permute-start.1 = (bf16[8,4,1,16,128]{4,3,2,1,0:T(8,128)(2,1)S(1)}, bf16[8,4,1,16,128]{4,3,2,1,0:T(8,128)(2,1)S(1)}, u32[]{:S(2)}, u32[]{:S(2)}) collective-permute-start(bf16[8,4,1,16,128]{4,3,2,1,0:T(8,128)(2,1)S(1)} %get-tuple-element.12), channel_id=1, source_target_pairs={{1,0},{2,1},{3,2},{4,3},{5,4},{6,5},{7,6},{9,8},{10,9},{11,10},{12... | collective-permute-start | bytes 393224 | tf_op jit(solution)/shard_map/ppermute | solution.py:592
  7.1 0.0 copy-done.2
  7.1 0.6 broadcast_in_dim.17
  7.7 5.9 %all-to-all-start = ((bf16[8,1,128]{2,1,0:T(2,128)(2,1)}), bf16[8,1,128]{2,1,0:T(2,128)(2,1)S(1)}, u32[]{:S(2)}, u32[]{:S(2)}) async-start(bf16[8,1,128]{2,1,0:T(2,128)(2,1)} %broadcast_in_dim.17), calls=%async_computation | async-start | bytes 8192 | tf_op jit(solution)/shard_map/all_to_all | solution.py:30
  13.6 0.0 copy-done
  13.7 4.9 %all-to-all-done = bf16[8,1,128]{2,1,0:T(2,128)(2,1)S(1)} async-done(((bf16[8,1,128]{2,1,0:T(2,128)(2,1)}), bf16[8,1,128]{2,1,0:T(2,128)(2,1)S(1)}, u32[]{:S(2)}, u32[]{:S(2)}) %all-to-all-start) | async-done | bytes 2080 | tf_op jit(solution)/shard_map/all_to_all | solution.py:30
  18.5 0.0 collective-permute-done.before_ref
  18.5 0.0 collective-permute-done.1.after_ref
  18.5 0.0 copy-done.1
  18.6 8.9 %shard_map.62 = (f32[64,128]{1,0:T(8,128)S(1)}, f32[16,40,384]{2,1,0:T(8,128)S(1)}, f32[72,512]{1,0:T(8,128)S(1)}) custom-call(bf16[8,4,4,16,128]{4,3,2,1,0:T(8,128)(2,1)S(1)} %copy-done.1, bf16[8,4,1,16,128]{4,3,2,1,0:T(8,128)(2,1)S(1)} %collective-permute-done.before_ref, bf16[8,4,1,16,128]{4,3,2,1,0:T(8,128)(2,1)S(1)} %collective-permute-done.1.after_ref, ...), custom_call_target="tpu_custom_call" | custom-call | tf_op jit(solution)/shard_map/pallas_call | solution.py:174
  27.5 1.5 %shard_map.63 = bf16[16,24,128]{2,1,0:T(8,128)(2,1)} custom-call(f32[64,128]{1,0:T(8,128)S(1)} %get-tuple-element.7.pool_ref, f32[16,40,384]{2,1,0:T(8,128)S(1)} %get-tuple-element.8.sums_ref, f32[72,512]{1,0:T(8,128)S(1)} %get-tuple-element.9.gram_ref, bf16[64,128]{1,0:T(8,128)(2,1)S(1)} %bitcast.14, bf16[8,128]{1,0:T(8,128)(2,1)S(1)} %bitcast.15, ...), custom_call_target="tpu_custom_call" | custom-call | tf_op jit(solution)/shard_map/pallas_call | solution.py:300
  29.0 11.1 %all-to-all-start.1 = ((bf16[16,24,128]{2,1,0:T(8,128)(2,1)}), bf16[16,24,128]{2,1,0:T(8,128)(2,1)S(1)}, u32[]{:S(2)}, u32[]{:S(2)}) async-start(bf16[16,24,128]{2,1,0:T(8,128)(2,1)} %shard_map.63), calls=%async_computation.1 | async-start | bytes 196608 | tf_op jit(solution)/shard_map/all_to_all | solution.py:30
  40.1 8.4 %all-to-all-done.1 = bf16[16,24,128]{2,1,0:T(8,128)(2,1)S(1)} async-done(((bf16[16,24,128]{2,1,0:T(8,128)(2,1)}), bf16[16,24,128]{2,1,0:T(8,128)(2,1)S(1)}, u32[]{:S(2)}, u32[]{:S(2)}) %all-to-all-start.1) | async-done | bytes 98336 | tf_op jit(solution)/shard_map/all_to_all | solution.py:30
  48.6 0.9 %shard_map.64 = bf16[16,56,128]{2,1,0:T(8,128)(2,1)} custom-call(f32[8,128]{1,0:T(8,128)S(1)} %broadcast_in_dim.16.core_ref, bf16[8,2,24,128]{3,2,1,0:T(8,128)(2,1)S(1)} %bitcast.13), custom_call_target="tpu_custom_call" | custom-call | tf_op jit(solution)/shard_map/pallas_call | solution.py:347
  49.4 4.4 %all-to-all-start.2 = ((bf16[16,56,128]{2,1,0:T(8,128)(2,1)}), bf16[16,56,128]{2,1,0:T(8,128)(2,1)S(1)}, u32[]{:S(2)}, u32[]{:S(2)}) async-start(bf16[16,56,128]{2,1,0:T(8,128)(2,1)} %shard_map.64), calls=%async_computation.2 | async-start | bytes 458752 | tf_op jit(solution)/shard_map/all_to_all | solution.py:30
  53.9 7.5 %all-to-all-done.2.got_ref.own_ref = bf16[16,56,128]{2,1,0:T(8,128)(2,1)S(1)} async-done(((bf16[16,56,128]{2,1,0:T(8,128)(2,1)}), bf16[16,56,128]{2,1,0:T(8,128)(2,1)S(1)}, u32[]{:S(2)}, u32[]{:S(2)}) %all-to-all-start.2) | async-done | bytes 229408 | tf_op jit(solution)/shard_map/all_to_all | solution.py:30
  61.4 0.8 %shard_map.65 = bf16[16,16,128]{2,1,0:T(8,128)(2,1)} custom-call(bf16[16,56,128]{2,1,0:T(8,128)(2,1)S(1)} %all-to-all-done.2.got_ref.own_ref), custom_call_target="tpu_custom_call" | custom-call | tf_op jit(solution)/shard_map/pallas_call | solution.py:364
  62.2 4.9 %all-to-all-start.3 = ((bf16[16,16,128]{2,1,0:T(8,128)(2,1)}), bf16[16,16,128]{2,1,0:T(8,128)(2,1)S(1)}, u32[]{:S(2)}, u32[]{:S(2)}) async-start(bf16[16,16,128]{2,1,0:T(8,128)(2,1)} %shard_map.65), calls=%async_computation.3 | async-start | bytes 131072 | tf_op jit(solution)/shard_map/all_to_all | solution.py:30
  67.1 0.3 collective-permute-start.2
  67.5 0.1 pad_add_fusion.place_ref
  67.5 1.0 %collective-permute-done.2.other_ref = bf16[16,40,128]{2,1,0:T(8,128)(2,1)S(1)} collective-permute-done((bf16[16,40,128]{2,1,0:T(8,128)(2,1)S(1)}, bf16[16,40,128]{2,1,0:T(8,128)(2,1)S(1)}, u32[]{:S(2)}, u32[]{:S(2)}) %collective-permute-start.2) | collective-permute-done | bytes 163872 | tf_op jit(solution)/shard_map/ppermute | solution.py:607
  68.6 4.5 %shard_map.66.delta_ref = f32[12,64]{1,0:T(8,128)S(1)} custom-call(s32[3]{0:T(128)S(1)} %pad_add_fusion.place_ref, bf16[16,56,128]{2,1,0:T(8,128)(2,1)S(1)} %all-to-all-done.2.got_ref.own_ref, bf16[16,40,128]{2,1,0:T(8,128)(2,1)S(1)} %collective-permute-done.2.other_ref), custom_call_target="tpu_custom_call" | custom-call | tf_op jit(solution)/shard_map/pallas_call | solution.py:515
  73.1 1.8 %all-to-all-done.3.got_ref = bf16[16,16,128]{2,1,0:T(8,128)(2,1)S(1)} async-done(((bf16[16,16,128]{2,1,0:T(8,128)(2,1)}), bf16[16,16,128]{2,1,0:T(8,128)(2,1)S(1)}, u32[]{:S(2)}, u32[]{:S(2)}) %all-to-all-start.3) | async-done | bytes 65568 | tf_op jit(solution)/shard_map/all_to_all | solution.py:30
  74.9 2.8 %shard_map.67 = (f32[32,108]{1,0:T(8,128)}, f32[4,64]{1,0:T(4,128)}) custom-call(bf16[16,16,128]{2,1,0:T(8,128)(2,1)S(1)} %all-to-all-done.3.got_ref, f32[12,64]{1,0:T(8,128)S(1)} %shard_map.66.delta_ref, f32[128,128]{1,0:T(8,128)S(1)} %fusion.14.order_ref), custom_call_target="tpu_custom_call" | custom-call | tf_op jit(solution)/shard_map/pallas_call | solution.py:561
  (13 shorter events, 0.1 us)
Async XLA Ops:
  0.6 13.0 %copy-start = (bf16[512,128]{1,0:T(8,128)(2,1)S(1)}, bf16[512,128]{1,0:T(8,128)(2,1)}, u32[]{:S(2)}) copy-start(bf16[512,128]{1,0:T(8,128)(2,1)} %param.6) | copy-start | bytes 393220
  0.6 17.9 %copy-start.1 = (bf16[8,4,4,16,128]{4,3,2,1,0:T(8,128)(2,1)S(1)}, bf16[8,4,4,16,128]{4,3,2,1,0:T(8,128)(2,1)}, u32[]{:S(2)}) copy-start(bf16[8,4,4,16,128]{4,3,2,1,0:T(8,128)(2,1)} %vol_ref.1) | copy-start | bytes 1572868
  1.7 16.8 %collective-permute-start = (bf16[8,4,1,16,128]{4,3,2,1,0:T(8,128)(2,1)S(1)}, bf16[8,4,1,16,128]{4,3,2,1,0:T(8,128)(2,1)S(1)}, u32[]{:S(2)}, u32[]{:S(2)}) collective-permute-start(bf16[8,4,1,16,128]{4,3,2,1,0:T(8,128)(2,1)S(1)} %get-tuple-element.13), channel_id=1, source_target_pairs={{0,1},{1,2},{2,3},{3,4},{4,5},{5,6},{6,7},{8,9},{9,10},{10,11},{11... | collective-permute-start | bytes 393224 | tf_op jit(solution)/shard_map/ppermute | solution.py:591
  5.8 1.3 %copy-start.2 = (bf16[1,128]{1,0:T(2,128)(2,1)S(1)}, bf16[1,128]{1,0:T(2,128)(2,1)}, u32[]{:S(2)}) copy-start(bf16[1,128]{1,0:T(2,128)(2,1)} %own_ref.1) | copy-start | bytes 772
  5.8 12.8 %collective-permute-start.1 = (bf16[8,4,1,16,128]{4,3,2,1,0:T(8,128)(2,1)S(1)}, bf16[8,4,1,16,128]{4,3,2,1,0:T(8,128)(2,1)S(1)}, u32[]{:S(2)}, u32[]{:S(2)}) collective-permute-start(bf16[8,4,1,16,128]{4,3,2,1,0:T(8,128)(2,1)S(1)} %get-tuple-element.12), channel_id=1, source_target_pairs={{1,0},{2,1},{3,2},{4,3},{5,4},{6,5},{7,6},{9,8},{10,9},{11,10},{12... | collective-permute-start | bytes 393224 | tf_op jit(solution)/shard_map/ppermute | solution.py:592
  7.7 10.9 %all-to-all-start = ((bf16[8,1,128]{2,1,0:T(2,128)(2,1)}), bf16[8,1,128]{2,1,0:T(2,128)(2,1)S(1)}, u32[]{:S(2)}, u32[]{:S(2)}) async-start(bf16[8,1,128]{2,1,0:T(2,128)(2,1)} %broadcast_in_dim.17), calls=%async_computation | async-start | bytes 8192 | tf_op jit(solution)/shard_map/all_to_all | solution.py:30
  29.0 19.6 %all-to-all-start.1 = ((bf16[16,24,128]{2,1,0:T(8,128)(2,1)}), bf16[16,24,128]{2,1,0:T(8,128)(2,1)S(1)}, u32[]{:S(2)}, u32[]{:S(2)}) async-start(bf16[16,24,128]{2,1,0:T(8,128)(2,1)} %shard_map.63), calls=%async_computation.1 | async-start | bytes 196608 | tf_op jit(solution)/shard_map/all_to_all | solution.py:30
  49.4 11.9 %all-to-all-start.2 = ((bf16[16,56,128]{2,1,0:T(8,128)(2,1)}), bf16[16,56,128]{2,1,0:T(8,128)(2,1)S(1)}, u32[]{:S(2)}, u32[]{:S(2)}) async-start(bf16[16,56,128]{2,1,0:T(8,128)(2,1)} %shard_map.64), calls=%async_computation.2 | async-start | bytes 458752 | tf_op jit(solution)/shard_map/all_to_all | solution.py:30
  62.2 12.7 %all-to-all-start.3 = ((bf16[16,16,128]{2,1,0:T(8,128)(2,1)}), bf16[16,16,128]{2,1,0:T(8,128)(2,1)S(1)}, u32[]{:S(2)}, u32[]{:S(2)}) async-start(bf16[16,16,128]{2,1,0:T(8,128)(2,1)} %shard_map.65), calls=%async_computation.3 | async-start | bytes 131072 | tf_op jit(solution)/shard_map/all_to_all | solution.py:30
  67.1 1.5 %collective-permute-start.2 = (bf16[16,40,128]{2,1,0:T(8,128)(2,1)S(1)}, bf16[16,40,128]{2,1,0:T(8,128)(2,1)S(1)}, u32[]{:S(2)}, u32[]{:S(2)}) collective-permute-start(bf16[16,40,128]{2,1,0:T(8,128)(2,1)S(1)} %slice.12), channel_id=1, source_target_pairs={{0,8},{8,0},{1,9},{9,1},{2,10},{10,2},{3,11},{11,3},{4,12},{12,4},... | collective-permute-start | bytes 491528 | tf_op jit(solution)/shard_map/ppermute | solution.py:607

commit v10 on v9

--- a/solution.py
+++ b/solution.py
@@ -39,8 +39,8 @@
 
 
 def conv_kernel_body(
-    sizes, vol_ref, before_ref, after_ref, kernel_ref, pool_ref, sums_ref, gram_ref,
-    shift_a, shift_b, stack_a, stack_b, wide_a, wide_b, edges, bands_ref, taken, done,
+    sizes, vol_ref, before_ref, after_ref, bands_ref, pool_ref, sums_ref, gram_ref,
+    shift_a, shift_b, stack_a, stack_b, wide_a, wide_b, edges,
 ):
     channels, planes, height, length, filters, samples = sizes
     rim = planes + 2
@@ -124,8 +124,6 @@
 
     @pl.when(step == 0)
     def _():
-        fetch = pltpu.make_async_copy(kernel_ref, taken, done)
-        fetch.start()
         blank = jnp.zeros((group, length), F32)
         for shifted in (shift_a, shift_b):
             shifted[0:group, :] = blank
@@ -136,19 +134,6 @@
         gram_ref[...] = jnp.zeros_like(gram_ref)
         pool_ref[...] = jnp.zeros_like(pool_ref)
         build(0, shift_a, stack_a)
-        at = lax.broadcasted_iota(jnp.int32, (1, 256), 1)
-        j, rest = at // group, at % group
-        inner = channels * 3
-        i, channel, k = rest // inner, rest % inner // 3, rest % 3
-        used = jnp.logical_and(rest < 3 * inner, at < rows)
-        source = jnp.where(used, channel * 27 + i * 9 + j * 3 + k, -1)
-        row = lax.broadcasted_iota(jnp.int32, (kernel_ref.shape[1], 256), 0)
-        pick = jnp.where(row == source, 1.0, 0.0).astype(BF16)
-        fetch.wait()
-        band = jnp.dot(taken[...], pick, preferred_element_type=F32)
-        bands_ref[...] = jnp.concatenate(
-            [band] + [pltpu.roll(band, plane * inner, 1) for plane in range(1, planes)], axis=0
-        )[:, :rows].astype(BF16)
 
     build(2 * step + 1, shift_b, stack_b)
     consume(2 * step, stack_a, wide_a)
@@ -163,9 +148,8 @@
             )
 
 
-def conv_sums(volume, before, after, conv_kernel):
+def conv_sums(volume, before, after, bands, filters):
     samples, channels, planes, height, length = volume.shape
-    filters = conv_kernel.shape[0]
     group = (planes + 2) * channels * 3
     top = planes * filters
     stack = top + 16 + 3 * group
@@ -174,7 +158,7 @@
     return pl.pallas_call(
         functools.partial(conv_kernel_body, sizes),
         grid=(samples // 2,),
-        in_specs=[vmem] * 3 + [pl.BlockSpec(memory_space=pltpu.HBM)],
+        in_specs=[vmem] * 4,
         out_specs=[vmem] * 3,
         out_shape=[
             jax.ShapeDtypeStruct((filters * PC, 128), F32),
@@ -189,12 +173,9 @@
             pltpu.VMEM((PC, top + 8, 256), F32),
             pltpu.VMEM((PC, top + 8, 256), F32),
             pltpu.VMEM((2, group, samples * length), BF16),
-            pltpu.VMEM((top, 3 * group), BF16),
-            pltpu.VMEM(conv_kernel.shape, BF16),
-            pltpu.SemaphoreType.DMA(()),
         ],
         compiler_params=pltpu.CompilerParams(vmem_limit_bytes=24 * 1024 * 1024),
-    )(volume, before, after, pltpu.with_memory_space_constraint(conv_kernel, pltpu.HBM))
+    )(volume, before, after, bands)
 
 
 def moments_body(
@@ -590,13 +571,24 @@
     down = [(j, i) for i, j in up]
     before = lax.ppermute(volume[:, :, planes - 1:], SPACE, up)
     after = lax.ppermute(volume[:, :, :1], SPACE, down)
+    mixed = conv_kernel.reshape(filters, channels, 3, 3, 3).transpose(0, 3, 2, 1, 4)
+    mixed = mixed.reshape(filters, 3, channels * 9)
+    inner = channels * 3
+    spare = (planes - 1) * inner
+    bands = jnp.concatenate(
+        [
+            jnp.pad(mixed, ((0, 0), (0, 0), (p * inner, spare - p * inner)))
+            for p in range(planes)
+        ],
+        axis=0,
+    ).reshape(planes * filters, -1)
     cot_group = gather_from(cotangent[0], SPACE, spaces)
 
     place = lax.axis_index(SPACE)
     weight = lax.dynamic_slice_in_dim(dense_weight, place * slab, slab, 0)
     weight = weight.reshape(filters, PC, -1).transpose(1, 0, 2).reshape(slab, -1)
 
-    sums = conv_sums(volume, before, after, conv_kernel)
+    sums = conv_sums(volume, before, after, bands, filters)
     sizes = (channels, planes, planes * height * length // PC, filters, samples)
     sent = conv_moments(sizes, sums, weight, cot_group, cotangent, column)
     peers = spaces * groups // column

time: 78.3 us -> 77.5 us (0.990)
  transfers between devices with their start and end apart: 7 -> 7, of which waited for: 5 -> 5; matrix products, arithmetic and copies ran while one was open for 1% -> 2% of each run, Pallas kernels for 6% -> 6%
where the time goes in v10:
time: 77.5 us; the launch traced here: 77.1 us
  starting transfers between devices  32 us (41%)
  waiting for transfers between devices  23.2 us (30%)
  Pallas kernels  18.7 us (24%)
  local copies, waits for them, and re-layouts  2.02 us (3%)
  between operations  0.85 us (1%)
    all_to_all x4, starting transfers between devices, exchange(): return lax.all_to_all(x, axes, split_axis=0, concat_axis=0, tiled=True)  26.4 us
    all_to_all x4, waiting for transfers between devices, exchange(): return lax.all_to_all(x, axes, split_axis=0, concat_axis=0, tiled=True)  22.2 us
    pallas_call x1, Pallas kernels, conv_sums(): pl.pallas_call(functools.partial(conv_kernel_body, sizes), grid=(samples...  8.24 us
    pallas_call x1, Pallas kernels, dense_delta(): pl.pallas_call(functools.partial(dense_kernel_body, depth, spaces), in_sp...  4.49 us
    ppermute x1, starting transfers between devices, on_device(): before = lax.ppermute(volume[:, :, planes - 1:], SPACE, up)  4.03 us
    pallas_call x1, Pallas kernels, final_steps(): pl.pallas_call(functools.partial(final_kernel_body, filters, patch_rows,...  2.85 us
  transfers between devices with their start and end apart: 7, of which 5 were waited for; matrix products, arithmetic and copies ran while one was open for 2% of the time, Pallas kernels for 6%

profile of v10, /device:TPU:1, one launch (start us, length us, event | category | flops | bytes accessed | tf_op | source)
XLA Modules:
  0.0 77.1 jit_solution(17777207288992715734)
XLA Ops:
  0.6 0.0 copy-start
  0.6 0.0 copy-start.1
  0.7 1.1 %fusion.25 = (bf16[8,4,1,16,128]{4,3,2,1,0:T(8,128)(2,1)S(1)}, bf16[8,4,1,16,128]{4,3,2,1,0:T(8,128)(2,1)S(1)}) fusion(bf16[8,4,4,16,128]{4,3,2,1,0:T(8,128)(2,1)} %vol_ref.1), kind=kLoop, calls=%fused_computation.54 | loop fusion | bytes 524288 | tf_op jit(solution)/shard_map/slice | solution.py:573
  1.7 4.0 %collective-permute-start = (bf16[8,4,1,16,128]{4,3,2,1,0:T(8,128)(2,1)S(1)}, bf16[8,4,1,16,128]{4,3,2,1,0:T(8,128)(2,1)S(1)}, u32[]{:S(2)}, u32[]{:S(2)}) collective-permute-start(bf16[8,4,1,16,128]{4,3,2,1,0:T(8,128)(2,1)S(1)} %get-tuple-element.13), channel_id=1, source_target_pairs={{0,1},{1,2},{2,3},{3,4},{4,5},{5,6},{6,7},{8,9},{9,10},{10,11},{11... | collective-permute-start | bytes 393224 | tf_op jit(solution)/shard_map/ppermute | solution.py:572
  5.8 0.0 copy-start.2
  5.8 1.3 %collective-permute-start.1 = (bf16[8,4,1,16,128]{4,3,2,1,0:T(8,128)(2,1)S(1)}, bf16[8,4,1,16,128]{4,3,2,1,0:T(8,128)(2,1)S(1)}, u32[]{:S(2)}, u32[]{:S(2)}) collective-permute-start(bf16[8,4,1,16,128]{4,3,2,1,0:T(8,128)(2,1)S(1)} %get-tuple-element.12), channel_id=1, source_target_pairs={{1,0},{2,1},{3,2},{4,3},{5,4},{6,5},{7,6},{9,8},{10,9},{11,10},{12... | collective-permute-start | bytes 393224 | tf_op jit(solution)/shard_map/ppermute | solution.py:573
  7.1 0.0 copy-done.2
  7.1 0.0 copy-start.3
  7.1 0.6 broadcast_in_dim.17
  7.7 5.9 %all-to-all-start = ((bf16[8,1,128]{2,1,0:T(2,128)(2,1)}), bf16[8,1,128]{2,1,0:T(2,128)(2,1)S(1)}, u32[]{:S(2)}, u32[]{:S(2)}) async-start(bf16[8,1,128]{2,1,0:T(2,128)(2,1)} %broadcast_in_dim.17), calls=%async_computation | async-start | bytes 8192 | tf_op jit(solution)/shard_map/all_to_all | solution.py:30
  13.6 0.0 copy-done.3
  13.6 0.1 copy.15
  13.8 0.1 fusion.22
  13.9 0.0 copy-done
  14.0 0.1 copy.17.bands_ref
  14.1 4.4 %all-to-all-done = bf16[8,1,128]{2,1,0:T(2,128)(2,1)S(1)} async-done(((bf16[8,1,128]{2,1,0:T(2,128)(2,1)}), bf16[8,1,128]{2,1,0:T(2,128)(2,1)S(1)}, u32[]{:S(2)}, u32[]{:S(2)}) %all-to-all-start) | async-done | bytes 2080 | tf_op jit(solution)/shard_map/all_to_all | solution.py:30
  18.5 0.0 collective-permute-done.before_ref
  18.5 0.0 collective-permute-done.1.after_ref
  18.6 0.0 copy-done.1
  18.6 8.2 %shard_map.62 = (f32[64,128]{1,0:T(8,128)S(1)}, f32[16,40,384]{2,1,0:T(8,128)S(1)}, f32[72,512]{1,0:T(8,128)S(1)}) custom-call(bf16[8,4,4,16,128]{4,3,2,1,0:T(8,128)(2,1)S(1)} %copy-done.1, bf16[8,4,1,16,128]{4,3,2,1,0:T(8,128)(2,1)S(1)} %collective-permute-done.before_ref, bf16[8,4,1,16,128]{4,3,2,1,0:T(8,128)(2,1)S(1)} %collective-permute-done.1.after_ref, ...), custom_call_target="tpu_custom_call" | custom-call | tf_op jit(solution)/shard_map/pallas_call | solution.py:158
  26.8 1.5 %shard_map.63 = bf16[16,24,128]{2,1,0:T(8,128)(2,1)} custom-call(f32[64,128]{1,0:T(8,128)S(1)} %get-tuple-element.7.pool_ref, f32[16,40,384]{2,1,0:T(8,128)S(1)} %get-tuple-element.8.sums_ref, f32[72,512]{1,0:T(8,128)S(1)} %get-tuple-element.9.gram_ref, bf16[64,128]{1,0:T(8,128)(2,1)S(1)} %bitcast.20, bf16[8,128]{1,0:T(8,128)(2,1)S(1)} %bitcast.21, ...), custom_call_target="tpu_custom_call" | custom-call | tf_op jit(solution)/shard_map/pallas_call | solution.py:281
  28.3 11.1 %all-to-all-start.1 = ((bf16[16,24,128]{2,1,0:T(8,128)(2,1)}), bf16[16,24,128]{2,1,0:T(8,128)(2,1)S(1)}, u32[]{:S(2)}, u32[]{:S(2)}) async-start(bf16[16,24,128]{2,1,0:T(8,128)(2,1)} %shard_map.63), calls=%async_computation.1 | async-start | bytes 196608 | tf_op jit(solution)/shard_map/all_to_all | solution.py:30
  39.4 8.4 %all-to-all-done.1 = bf16[16,24,128]{2,1,0:T(8,128)(2,1)S(1)} async-done(((bf16[16,24,128]{2,1,0:T(8,128)(2,1)}), bf16[16,24,128]{2,1,0:T(8,128)(2,1)S(1)}, u32[]{:S(2)}, u32[]{:S(2)}) %all-to-all-start.1) | async-done | bytes 98336 | tf_op jit(solution)/shard_map/all_to_all | solution.py:30
  47.9 0.9 %shard_map.64 = bf16[16,56,128]{2,1,0:T(8,128)(2,1)} custom-call(f32[8,128]{1,0:T(8,128)S(1)} %broadcast_in_dim.16.core_ref, bf16[8,2,24,128]{3,2,1,0:T(8,128)(2,1)S(1)} %bitcast.19), custom_call_target="tpu_custom_call" | custom-call | tf_op jit(solution)/shard_map/pallas_call | solution.py:328
  48.7 4.4 %all-to-all-start.2 = ((bf16[16,56,128]{2,1,0:T(8,128)(2,1)}), bf16[16,56,128]{2,1,0:T(8,128)(2,1)S(1)}, u32[]{:S(2)}, u32[]{:S(2)}) async-start(bf16[16,56,128]{2,1,0:T(8,128)(2,1)} %shard_map.64), calls=%async_computation.2 | async-start | bytes 458752 | tf_op jit(solution)/shard_map/all_to_all | solution.py:30
  53.2 7.5 %all-to-all-done.2.got_ref.own_ref = bf16[16,56,128]{2,1,0:T(8,128)(2,1)S(1)} async-done(((bf16[16,56,128]{2,1,0:T(8,128)(2,1)}), bf16[16,56,128]{2,1,0:T(8,128)(2,1)S(1)}, u32[]{:S(2)}, u32[]{:S(2)}) %all-to-all-start.2) | async-done | bytes 229408 | tf_op jit(solution)/shard_map/all_to_all | solution.py:30
  60.7 0.8 %shard_map.65 = bf16[16,16,128]{2,1,0:T(8,128)(2,1)} custom-call(bf16[16,56,128]{2,1,0:T(8,128)(2,1)S(1)} %all-to-all-done.2.got_ref.own_ref), custom_call_target="tpu_custom_call" | custom-call | tf_op jit(solution)/shard_map/pallas_call | solution.py:345
  61.5 4.9 %all-to-all-start.3 = ((bf16[16,16,128]{2,1,0:T(8,128)(2,1)}), bf16[16,16,128]{2,1,0:T(8,128)(2,1)S(1)}, u32[]{:S(2)}, u32[]{:S(2)}) async-start(bf16[16,16,128]{2,1,0:T(8,128)(2,1)} %shard_map.65), calls=%async_computation.3 | async-start | bytes 131072 | tf_op jit(solution)/shard_map/all_to_all | solution.py:30
  66.4 0.3 collective-permute-start.2
  66.8 0.1 pad_add_fusion.place_ref
  66.8 1.0 %collective-permute-done.2.other_ref = bf16[16,40,128]{2,1,0:T(8,128)(2,1)S(1)} collective-permute-done((bf16[16,40,128]{2,1,0:T(8,128)(2,1)S(1)}, bf16[16,40,128]{2,1,0:T(8,128)(2,1)S(1)}, u32[]{:S(2)}, u32[]{:S(2)}) %collective-permute-start.2) | collective-permute-done | bytes 163872 | tf_op jit(solution)/shard_map/ppermute | solution.py:599
  67.9 4.5 %shard_map.66.delta_ref = f32[12,64]{1,0:T(8,128)S(1)} custom-call(s32[3]{0:T(128)S(1)} %pad_add_fusion.place_ref, bf16[16,56,128]{2,1,0:T(8,128)(2,1)S(1)} %all-to-all-done.2.got_ref.own_ref, bf16[16,40,128]{2,1,0:T(8,128)(2,1)S(1)} %collective-permute-done.2.other_ref), custom_call_target="tpu_custom_call" | custom-call | tf_op jit(solution)/shard_map/pallas_call | solution.py:496
  72.4 1.8 %all-to-all-done.3.got_ref = bf16[16,16,128]{2,1,0:T(8,128)(2,1)S(1)} async-done(((bf16[16,16,128]{2,1,0:T(8,128)(2,1)}), bf16[16,16,128]{2,1,0:T(8,128)(2,1)S(1)}, u32[]{:S(2)}, u32[]{:S(2)}) %all-to-all-start.3) | async-done | bytes 65568 | tf_op jit(solution)/shard_map/all_to_all | solution.py:30
  74.2 2.9 %shard_map.67 = (f32[32,108]{1,0:T(8,128)}, f32[4,64]{1,0:T(4,128)}) custom-call(bf16[16,16,128]{2,1,0:T(8,128)(2,1)S(1)} %all-to-all-done.3.got_ref, f32[12,64]{1,0:T(8,128)S(1)} %shard_map.66.delta_ref, f32[128,128]{1,0:T(8,128)S(1)} %fusion.20.order_ref), custom_call_target="tpu_custom_call" | custom-call | tf_op jit(solution)/shard_map/pallas_call | solution.py:542
  (16 shorter events, 0.2 us)
Async XLA Ops:
  0.6 13.3 %copy-start = (bf16[512,128]{1,0:T(8,128)(2,1)S(1)}, bf16[512,128]{1,0:T(8,128)(2,1)}, u32[]{:S(2)}) copy-start(bf16[512,128]{1,0:T(8,128)(2,1)} %param.6) | copy-start | bytes 393220
  0.6 17.9 %copy-start.1 = (bf16[8,4,4,16,128]{4,3,2,1,0:T(8,128)(2,1)S(1)}, bf16[8,4,4,16,128]{4,3,2,1,0:T(8,128)(2,1)}, u32[]{:S(2)}) copy-start(bf16[8,4,4,16,128]{4,3,2,1,0:T(8,128)(2,1)} %vol_ref.1) | copy-start | bytes 1572868
  1.7 16.8 %collective-permute-start = (bf16[8,4,1,16,128]{4,3,2,1,0:T(8,128)(2,1)S(1)}, bf16[8,4,1,16,128]{4,3,2,1,0:T(8,128)(2,1)S(1)}, u32[]{:S(2)}, u32[]{:S(2)}) collective-permute-start(bf16[8,4,1,16,128]{4,3,2,1,0:T(8,128)(2,1)S(1)} %get-tuple-element.13), channel_id=1, source_target_pairs={{0,1},{1,2},{2,3},{3,4},{4,5},{5,6},{6,7},{8,9},{9,10},{10,11},{11... | collective-permute-start | bytes 393224 | tf_op jit(solution)/shard_map/ppermute | solution.py:572
  5.8 1.3 %copy-start.2 = (bf16[1,128]{1,0:T(2,128)(2,1)S(1)}, bf16[1,128]{1,0:T(2,128)(2,1)}, u32[]{:S(2)}) copy-start(bf16[1,128]{1,0:T(2,128)(2,1)} %own_ref.1) | copy-start | bytes 772
  5.8 12.8 %collective-permute-start.1 = (bf16[8,4,1,16,128]{4,3,2,1,0:T(8,128)(2,1)S(1)}, bf16[8,4,1,16,128]{4,3,2,1,0:T(8,128)(2,1)S(1)}, u32[]{:S(2)}, u32[]{:S(2)}) collective-permute-start(bf16[8,4,1,16,128]{4,3,2,1,0:T(8,128)(2,1)S(1)} %get-tuple-element.12), channel_id=1, source_target_pairs={{1,0},{2,1},{3,2},{4,3},{5,4},{6,5},{7,6},{9,8},{10,9},{11,10},{12... | collective-permute-start | bytes 393224 | tf_op jit(solution)/shard_map/ppermute | solution.py:573
  7.1 6.5 %copy-start.3 = (bf16[32,108]{1,0:T(8,128)(2,1)S(1)}, bf16[32,108]{1,0:T(8,128)(2,1)}, u32[]{:S(2)}) copy-start(bf16[32,108]{1,0:T(8,128)(2,1)} %param.5) | copy-start | bytes 20740
  7.7 10.9 %all-to-all-start = ((bf16[8,1,128]{2,1,0:T(2,128)(2,1)}), bf16[8,1,128]{2,1,0:T(2,128)(2,1)S(1)}, u32[]{:S(2)}, u32[]{:S(2)}) async-start(bf16[8,1,128]{2,1,0:T(2,128)(2,1)} %broadcast_in_dim.17), calls=%async_computation | async-start | bytes 8192 | tf_op jit(solution)/shard_map/all_to_all | solution.py:30
  28.3 19.6 %all-to-all-start.1 = ((bf16[16,24,128]{2,1,0:T(8,128)(2,1)}), bf16[16,24,128]{2,1,0:T(8,128)(2,1)S(1)}, u32[]{:S(2)}, u32[]{:S(2)}) async-start(bf16[16,24,128]{2,1,0:T(8,128)(2,1)} %shard_map.63), calls=%async_computation.1 | async-start | bytes 196608 | tf_op jit(solution)/shard_map/all_to_all | solution.py:30
  48.7 11.9 %all-to-all-start.2 = ((bf16[16,56,128]{2,1,0:T(8,128)(2,1)}), bf16[16,56,128]{2,1,0:T(8,128)(2,1)S(1)}, u32[]{:S(2)}, u32[]{:S(2)}) async-start(bf16[16,56,128]{2,1,0:T(8,128)(2,1)} %shard_map.64), calls=%async_computation.2 | async-start | bytes 458752 | tf_op jit(solution)/shard_map/all_to_all | solution.py:30
  61.5 12.7 %all-to-all-start.3 = ((bf16[16,16,128]{2,1,0:T(8,128)(2,1)}), bf16[16,16,128]{2,1,0:T(8,128)(2,1)S(1)}, u32[]{:S(2)}, u32[]{:S(2)}) async-start(bf16[16,16,128]{2,1,0:T(8,128)(2,1)} %shard_map.65), calls=%async_computation.3 | async-start | bytes 131072 | tf_op jit(solution)/shard_map/all_to_all | solution.py:30
  66.4 1.5 %collective-permute-start.2 = (bf16[16,40,128]{2,1,0:T(8,128)(2,1)S(1)}, bf16[16,40,128]{2,1,0:T(8,128)(2,1)S(1)}, u32[]{:S(2)}, u32[]{:S(2)}) collective-permute-start(bf16[16,40,128]{2,1,0:T(8,128)(2,1)S(1)} %slice.12), channel_id=1, source_target_pairs={{0,8},{8,0},{1,9},{9,1},{2,10},{10,2},{3,11},{11,3},{4,12},{12,4},... | collective-permute-start | bytes 491528 | tf_op jit(solution)/shard_map/ppermute | solution.py:599

commit v11 on v10

--- a/solution.py
+++ b/solution.py
@@ -532,7 +532,12 @@
     held = two_sided(left[0:filters], conv_grad / bound_in / bound_out, right)
     total = scalar_sum(held * conv_grad) + delta_ref[4:5, 0:1]
     scaling = jnp.minimum(1.0, jnp.sqrt(KL_BOUND / (LEARN_RATE * LEARN_RATE * total)))
-    moved = split_dot(held, order_ref[...])
+    order = order_ref[...].astype(BF16)
+    moved = jnp.dot(
+        jnp.concatenate(parts_of(held), axis=1),
+        jnp.concatenate([order, order], axis=0),
+        preferred_element_type=F32,
+    )
     step_conv_ref[...] = scaling * moved[:, 0:patch_rows]
     step_dense_ref[...] = scaling * delta_ref[0:4, :]
 

time: 77.5 us -> 77.5 us (level)
  no operation moved by 1% of the time
where the time goes in v11:
time: 77.5 us; the launch traced here: 77.1 us
  starting transfers between devices  32 us (41%)
  waiting for transfers between devices  23.2 us (30%)
  Pallas kernels  18.7 us (24%)
  local copies, waits for them, and re-layouts  2.02 us (3%)
  between operations  0.85 us (1%)
    all_to_all x4, starting transfers between devices, exchange(): return lax.all_to_all(x, axes, split_axis=0, concat_axis=0, tiled=True)  26.4 us
    all_to_all x4, waiting for transfers between devices, exchange(): return lax.all_to_all(x, axes, split_axis=0, concat_axis=0, tiled=True)  22.2 us
    pallas_call x1, Pallas kernels, conv_sums(): pl.pallas_call(functools.partial(conv_kernel_body, sizes), grid=(samples...  8.24 us
    pallas_call x1, Pallas kernels, dense_delta(): pl.pallas_call(functools.partial(dense_kernel_body, depth, spaces), in_sp...  4.49 us
    ppermute x1, starting transfers between devices, on_device(): before = lax.ppermute(volume[:, :, planes - 1:], SPACE, up)  4.03 us
    pallas_call x1, Pallas kernels, final_steps(): pl.pallas_call(functools.partial(final_kernel_body, filters, patch_rows,...  2.85 us
  transfers between devices with their start and end apart: 7, of which 5 were waited for; matrix products, arithmetic and copies ran while one was open for 2% of the time, Pallas kernels for 6%

profile of v11, /device:TPU:1, one launch (start us, length us, event | category | flops | bytes accessed | tf_op | source)
XLA Modules:
  0.0 77.1 jit_solution(17252503461421404362)
XLA Ops:
  0.6 0.0 copy-start
  0.6 0.0 copy-start.1
  0.7 1.1 %fusion.25 = (bf16[8,4,1,16,128]{4,3,2,1,0:T(8,128)(2,1)S(1)}, bf16[8,4,1,16,128]{4,3,2,1,0:T(8,128)(2,1)S(1)}) fusion(bf16[8,4,4,16,128]{4,3,2,1,0:T(8,128)(2,1)} %vol_ref.1), kind=kLoop, calls=%fused_computation.54 | loop fusion | bytes 524288 | tf_op jit(solution)/shard_map/slice | solution.py:578
  1.7 4.0 %collective-permute-start = (bf16[8,4,1,16,128]{4,3,2,1,0:T(8,128)(2,1)S(1)}, bf16[8,4,1,16,128]{4,3,2,1,0:T(8,128)(2,1)S(1)}, u32[]{:S(2)}, u32[]{:S(2)}) collective-permute-start(bf16[8,4,1,16,128]{4,3,2,1,0:T(8,128)(2,1)S(1)} %get-tuple-element.13), channel_id=1, source_target_pairs={{0,1},{1,2},{2,3},{3,4},{4,5},{5,6},{6,7},{8,9},{9,10},{10,11},{11... | collective-permute-start | bytes 393224 | tf_op jit(solution)/shard_map/ppermute | solution.py:577
  5.8 0.0 copy-start.2
  5.8 1.3 %collective-permute-start.1 = (bf16[8,4,1,16,128]{4,3,2,1,0:T(8,128)(2,1)S(1)}, bf16[8,4,1,16,128]{4,3,2,1,0:T(8,128)(2,1)S(1)}, u32[]{:S(2)}, u32[]{:S(2)}) collective-permute-start(bf16[8,4,1,16,128]{4,3,2,1,0:T(8,128)(2,1)S(1)} %get-tuple-element.12), channel_id=1, source_target_pairs={{1,0},{2,1},{3,2},{4,3},{5,4},{6,5},{7,6},{9,8},{10,9},{11,10},{12... | collective-permute-start | bytes 393224 | tf_op jit(solution)/shard_map/ppermute | solution.py:578
  7.1 0.0 copy-done.2
  7.1 0.0 copy-start.3
  7.1 0.6 broadcast_in_dim.17
  7.7 5.9 %all-to-all-start = ((bf16[8,1,128]{2,1,0:T(2,128)(2,1)}), bf16[8,1,128]{2,1,0:T(2,128)(2,1)S(1)}, u32[]{:S(2)}, u32[]{:S(2)}) async-start(bf16[8,1,128]{2,1,0:T(2,128)(2,1)} %broadcast_in_dim.17), calls=%async_computation | async-start | bytes 8192 | tf_op jit(solution)/shard_map/all_to_all | solution.py:30
  13.6 0.0 copy-done.3
  13.6 0.1 copy.15
  13.8 0.1 fusion.22
  13.9 0.0 copy-done
  14.0 0.1 copy.17.bands_ref
  14.1 4.4 %all-to-all-done = bf16[8,1,128]{2,1,0:T(2,128)(2,1)S(1)} async-done(((bf16[8,1,128]{2,1,0:T(2,128)(2,1)}), bf16[8,1,128]{2,1,0:T(2,128)(2,1)S(1)}, u32[]{:S(2)}, u32[]{:S(2)}) %all-to-all-start) | async-done | bytes 2080 | tf_op jit(solution)/shard_map/all_to_all | solution.py:30
  18.5 0.0 collective-permute-done.before_ref
  18.5 0.0 collective-permute-done.1.after_ref
  18.6 0.0 copy-done.1
  18.6 8.2 %shard_map.62 = (f32[64,128]{1,0:T(8,128)S(1)}, f32[16,40,384]{2,1,0:T(8,128)S(1)}, f32[72,512]{1,0:T(8,128)S(1)}) custom-call(bf16[8,4,4,16,128]{4,3,2,1,0:T(8,128)(2,1)S(1)} %copy-done.1, bf16[8,4,1,16,128]{4,3,2,1,0:T(8,128)(2,1)S(1)} %collective-permute-done.before_ref, bf16[8,4,1,16,128]{4,3,2,1,0:T(8,128)(2,1)S(1)} %collective-permute-done.1.after_ref, ...), custom_call_target="tpu_custom_call" | custom-call | tf_op jit(solution)/shard_map/pallas_call | solution.py:158
  26.8 1.5 %shard_map.63 = bf16[16,24,128]{2,1,0:T(8,128)(2,1)} custom-call(f32[64,128]{1,0:T(8,128)S(1)} %get-tuple-element.7.pool_ref, f32[16,40,384]{2,1,0:T(8,128)S(1)} %get-tuple-element.8.sums_ref, f32[72,512]{1,0:T(8,128)S(1)} %get-tuple-element.9.gram_ref, bf16[64,128]{1,0:T(8,128)(2,1)S(1)} %bitcast.20, bf16[8,128]{1,0:T(8,128)(2,1)S(1)} %bitcast.21, ...), custom_call_target="tpu_custom_call" | custom-call | tf_op jit(solution)/shard_map/pallas_call | solution.py:281
  28.3 11.1 %all-to-all-start.1 = ((bf16[16,24,128]{2,1,0:T(8,128)(2,1)}), bf16[16,24,128]{2,1,0:T(8,128)(2,1)S(1)}, u32[]{:S(2)}, u32[]{:S(2)}) async-start(bf16[16,24,128]{2,1,0:T(8,128)(2,1)} %shard_map.63), calls=%async_computation.1 | async-start | bytes 196608 | tf_op jit(solution)/shard_map/all_to_all | solution.py:30
  39.4 8.4 %all-to-all-done.1 = bf16[16,24,128]{2,1,0:T(8,128)(2,1)S(1)} async-done(((bf16[16,24,128]{2,1,0:T(8,128)(2,1)}), bf16[16,24,128]{2,1,0:T(8,128)(2,1)S(1)}, u32[]{:S(2)}, u32[]{:S(2)}) %all-to-all-start.1) | async-done | bytes 98336 | tf_op jit(solution)/shard_map/all_to_all | solution.py:30
  47.9 0.9 %shard_map.64 = bf16[16,56,128]{2,1,0:T(8,128)(2,1)} custom-call(f32[8,128]{1,0:T(8,128)S(1)} %broadcast_in_dim.16.core_ref, bf16[8,2,24,128]{3,2,1,0:T(8,128)(2,1)S(1)} %bitcast.19), custom_call_target="tpu_custom_call" | custom-call | tf_op jit(solution)/shard_map/pallas_call | solution.py:328
  48.7 4.4 %all-to-all-start.2 = ((bf16[16,56,128]{2,1,0:T(8,128)(2,1)}), bf16[16,56,128]{2,1,0:T(8,128)(2,1)S(1)}, u32[]{:S(2)}, u32[]{:S(2)}) async-start(bf16[16,56,128]{2,1,0:T(8,128)(2,1)} %shard_map.64), calls=%async_computation.2 | async-start | bytes 458752 | tf_op jit(solution)/shard_map/all_to_all | solution.py:30
  53.2 7.5 %all-to-all-done.2.got_ref.own_ref = bf16[16,56,128]{2,1,0:T(8,128)(2,1)S(1)} async-done(((bf16[16,56,128]{2,1,0:T(8,128)(2,1)}), bf16[16,56,128]{2,1,0:T(8,128)(2,1)S(1)}, u32[]{:S(2)}, u32[]{:S(2)}) %all-to-all-start.2) | async-done | bytes 229408 | tf_op jit(solution)/shard_map/all_to_all | solution.py:30
  60.7 0.8 %shard_map.65 = bf16[16,16,128]{2,1,0:T(8,128)(2,1)} custom-call(bf16[16,56,128]{2,1,0:T(8,128)(2,1)S(1)} %all-to-all-done.2.got_ref.own_ref), custom_call_target="tpu_custom_call" | custom-call | tf_op jit(solution)/shard_map/pallas_call | solution.py:345
  61.5 4.9 %all-to-all-start.3 = ((bf16[16,16,128]{2,1,0:T(8,128)(2,1)}), bf16[16,16,128]{2,1,0:T(8,128)(2,1)S(1)}, u32[]{:S(2)}, u32[]{:S(2)}) async-start(bf16[16,16,128]{2,1,0:T(8,128)(2,1)} %shard_map.65), calls=%async_computation.3 | async-start | bytes 131072 | tf_op jit(solution)/shard_map/all_to_all | solution.py:30
  66.4 0.3 collective-permute-start.2
  66.8 0.1 pad_add_fusion.place_ref
  66.8 1.0 %collective-permute-done.2.other_ref = bf16[16,40,128]{2,1,0:T(8,128)(2,1)S(1)} collective-permute-done((bf16[16,40,128]{2,1,0:T(8,128)(2,1)S(1)}, bf16[16,40,128]{2,1,0:T(8,128)(2,1)S(1)}, u32[]{:S(2)}, u32[]{:S(2)}) %collective-permute-start.2) | collective-permute-done | bytes 163872 | tf_op jit(solution)/shard_map/ppermute | solution.py:604
  67.9 4.5 %shard_map.66.delta_ref = f32[12,64]{1,0:T(8,128)S(1)} custom-call(s32[3]{0:T(128)S(1)} %pad_add_fusion.place_ref, bf16[16,56,128]{2,1,0:T(8,128)(2,1)S(1)} %all-to-all-done.2.got_ref.own_ref, bf16[16,40,128]{2,1,0:T(8,128)(2,1)S(1)} %collective-permute-done.2.other_ref), custom_call_target="tpu_custom_call" | custom-call | tf_op jit(solution)/shard_map/pallas_call | solution.py:496
  72.4 1.8 %all-to-all-done.3.got_ref = bf16[16,16,128]{2,1,0:T(8,128)(2,1)S(1)} async-done(((bf16[16,16,128]{2,1,0:T(8,128)(2,1)}), bf16[16,16,128]{2,1,0:T(8,128)(2,1)S(1)}, u32[]{:S(2)}, u32[]{:S(2)}) %all-to-all-start.3) | async-done | bytes 65568 | tf_op jit(solution)/shard_map/all_to_all | solution.py:30
  74.2 2.9 %shard_map.67 = (f32[32,108]{1,0:T(8,128)}, f32[4,64]{1,0:T(4,128)}) custom-call(bf16[16,16,128]{2,1,0:T(8,128)(2,1)S(1)} %all-to-all-done.3.got_ref, f32[12,64]{1,0:T(8,128)S(1)} %shard_map.66.delta_ref, f32[128,128]{1,0:T(8,128)S(1)} %fusion.20.order_ref), custom_call_target="tpu_custom_call" | custom-call | tf_op jit(solution)/shard_map/pallas_call | solution.py:547
  (16 shorter events, 0.2 us)
Async XLA Ops:
  0.6 13.3 %copy-start = (bf16[512,128]{1,0:T(8,128)(2,1)S(1)}, bf16[512,128]{1,0:T(8,128)(2,1)}, u32[]{:S(2)}) copy-start(bf16[512,128]{1,0:T(8,128)(2,1)} %param.6) | copy-start | bytes 393220
  0.6 17.9 %copy-start.1 = (bf16[8,4,4,16,128]{4,3,2,1,0:T(8,128)(2,1)S(1)}, bf16[8,4,4,16,128]{4,3,2,1,0:T(8,128)(2,1)}, u32[]{:S(2)}) copy-start(bf16[8,4,4,16,128]{4,3,2,1,0:T(8,128)(2,1)} %vol_ref.1) | copy-start | bytes 1572868
  1.7 16.8 %collective-permute-start = (bf16[8,4,1,16,128]{4,3,2,1,0:T(8,128)(2,1)S(1)}, bf16[8,4,1,16,128]{4,3,2,1,0:T(8,128)(2,1)S(1)}, u32[]{:S(2)}, u32[]{:S(2)}) collective-permute-start(bf16[8,4,1,16,128]{4,3,2,1,0:T(8,128)(2,1)S(1)} %get-tuple-element.13), channel_id=1, source_target_pairs={{0,1},{1,2},{2,3},{3,4},{4,5},{5,6},{6,7},{8,9},{9,10},{10,11},{11... | collective-permute-start | bytes 393224 | tf_op jit(solution)/shard_map/ppermute | solution.py:577
  5.8 1.3 %copy-start.2 = (bf16[1,128]{1,0:T(2,128)(2,1)S(1)}, bf16[1,128]{1,0:T(2,128)(2,1)}, u32[]{:S(2)}) copy-start(bf16[1,128]{1,0:T(2,128)(2,1)} %own_ref.1) | copy-start | bytes 772
  5.8 12.8 %collective-permute-start.1 = (bf16[8,4,1,16,128]{4,3,2,1,0:T(8,128)(2,1)S(1)}, bf16[8,4,1,16,128]{4,3,2,1,0:T(8,128)(2,1)S(1)}, u32[]{:S(2)}, u32[]{:S(2)}) collective-permute-start(bf16[8,4,1,16,128]{4,3,2,1,0:T(8,128)(2,1)S(1)} %get-tuple-element.12), channel_id=1, source_target_pairs={{1,0},{2,1},{3,2},{4,3},{5,4},{6,5},{7,6},{9,8},{10,9},{11,10},{12... | collective-permute-start | bytes 393224 | tf_op jit(solution)/shard_map/ppermute | solution.py:578
  7.1 6.5 %copy-start.3 = (bf16[32,108]{1,0:T(8,128)(2,1)S(1)}, bf16[32,108]{1,0:T(8,128)(2,1)}, u32[]{:S(2)}) copy-start(bf16[32,108]{1,0:T(8,128)(2,1)} %param.5) | copy-start | bytes 20740
  7.7 10.9 %all-to-all-start = ((bf16[8,1,128]{2,1,0:T(2,128)(2,1)}), bf16[8,1,128]{2,1,0:T(2,128)(2,1)S(1)}, u32[]{:S(2)}, u32[]{:S(2)}) async-start(bf16[8,1,128]{2,1,0:T(2,128)(2,1)} %broadcast_in_dim.17), calls=%async_computation | async-start | bytes 8192 | tf_op jit(solution)/shard_map/all_to_all | solution.py:30
  28.3 19.6 %all-to-all-start.1 = ((bf16[16,24,128]{2,1,0:T(8,128)(2,1)}), bf16[16,24,128]{2,1,0:T(8,128)(2,1)S(1)}, u32[]{:S(2)}, u32[]{:S(2)}) async-start(bf16[16,24,128]{2,1,0:T(8,128)(2,1)} %shard_map.63), calls=%async_computation.1 | async-start | bytes 196608 | tf_op jit(solution)/shard_map/all_to_all | solution.py:30
  48.7 11.9 %all-to-all-start.2 = ((bf16[16,56,128]{2,1,0:T(8,128)(2,1)}), bf16[16,56,128]{2,1,0:T(8,128)(2,1)S(1)}, u32[]{:S(2)}, u32[]{:S(2)}) async-start(bf16[16,56,128]{2,1,0:T(8,128)(2,1)} %shard_map.64), calls=%async_computation.2 | async-start | bytes 458752 | tf_op jit(solution)/shard_map/all_to_all | solution.py:30
  61.5 12.7 %all-to-all-start.3 = ((bf16[16,16,128]{2,1,0:T(8,128)(2,1)}), bf16[16,16,128]{2,1,0:T(8,128)(2,1)S(1)}, u32[]{:S(2)}, u32[]{:S(2)}) async-start(bf16[16,16,128]{2,1,0:T(8,128)(2,1)} %shard_map.65), calls=%async_computation.3 | async-start | bytes 131072 | tf_op jit(solution)/shard_map/all_to_all | solution.py:30
  66.4 1.5 %collective-permute-start.2 = (bf16[16,40,128]{2,1,0:T(8,128)(2,1)S(1)}, bf16[16,40,128]{2,1,0:T(8,128)(2,1)S(1)}, u32[]{:S(2)}, u32[]{:S(2)}) collective-permute-start(bf16[16,40,128]{2,1,0:T(8,128)(2,1)S(1)} %slice.12), channel_id=1, source_target_pairs={{0,8},{8,0},{1,9},{9,1},{2,10},{10,2},{3,11},{11,3},{4,12},{12,4},... | collective-permute-start | bytes 491528 | tf_op jit(solution)/shard_map/ppermute | solution.py:604
